TPU v7x, 128 devices: a whole 4x4x4 slice. The times are simulated.
128 devices in a mesh: pair: 4 (over z), bulk: 32 (over x, y, core).
Axes of the slice: x: 4, y: 4, z: 4, core: 2. Of those that a mesh axis runs over, the one named last changes fastest.
Arguments:
- wavefield_now: float32 [512, 96, 128], P(('pair', 'bulk')), may hold values from -6 to 6
- wavefield_vel: float32 [512, 96, 128], P(('pair', 'bulk')), may hold values from -6 to 6
- speed_sq: float32 [128, 24, 32], P(('pair', 'bulk')), may hold values from 0.5 to 2
- source_field: float32 [512, 96, 128], P(('pair', 'bulk')), may hold values from -300 to 300
- wavelet: float32 [6], replicated, may hold values from -4 to 4
- slot_elem: int32 [16384], P(('pair', 'bulk')), may hold values from 0 to 767
- slot_station: int32 [16384], replicated, may hold values from 0 to 8192, as said below
- slot_weight: float32 [125, 16384], P(None, ('pair', 'bulk')), may hold values from -0.5 to 0.5
- pair_blocks: int32 [128, 2], P(('pair', 'bulk')), may hold values from 0 to 255
Outputs:
- wavefield_end: float32 [512, 96, 128], P(('pair', 'bulk'))
- cross: bfloat16 [128, 2, 256, 1024], P(('pair', 'bulk'))
Inputs may be any that keep to these rules, and one draw needn't show every extreme that they name: `slot_station`: every station number 0 .. 8191 appears in exactly one slot; empty slots hold 8192. Within each device block of 128 slots the live slots come first; some device block is full in every draw. `slot_elem`: index of the slot's element within the slot block's elements. `pair_blocks`: block k holds stations k * 32 to k * 32 + 31.
All inputs are finite; a program needn't handle non-finite values.
Results may differ from a plain program's by a relative error of at most 0.0057.
Values may be sent and summed in bfloat16 or wider, within the bound.
No kernel may reach another device: no remote copies, remote signals or barrier semaphores. Data moves between devices by JAX's collectives and lax.ppermute only.
A program may use at most 128 MiB of HBM per device.

v0:
```python
import functools
import math

import jax
import jax.numpy as jnp
import numpy as np
from jax import lax
from jax.experimental import pallas as pl
from jax.experimental.pallas import tpu as pltpu
from jax.sharding import PartitionSpec as P

NT = 6
F = 256
SB = 32
STEP_DT = 0.04
NY = 96
NZ = 128
EY = 24
EZ = 32
CAP = 128
AXES = ("pair", "bulk")
HIGHEST = lax.Precision.HIGHEST
W1 = np.array([0.1, 49.0 / 90.0, 32.0 / 45.0, 49.0 / 90.0, 0.1])


def stiffness_1d():
    points = np.array([-1.0, -math.sqrt(3.0 / 7.0), 0.0, math.sqrt(3.0 / 7.0), 1.0])
    factor = np.array(
        [np.prod([points[i] - points[j] for j in range(5) if j != i]) for i in range(5)]
    )
    d = np.zeros((5, 5))
    for i in range(5):
        for j in range(5):
            if i != j:
                d[i, j] = factor[i] / (factor[j] * (points[i] - points[j]))
        d[i, i] = -np.sum(d[i])
    return d.T @ np.diag(W1) @ d


A = stiffness_1d()
MX = np.array([0.2, W1[1], W1[2], W1[3], 0.2])
AB = A / MX[:, None]
KAPPA = float(sum(AB[4, k] * AB[k, 4] for k in range(4)))


def f32(x):
    return np.asarray(x, np.float32)


def tables():
    my = np.array([MX[y % 4] for y in range(NY)])
    mz = np.array([0.1 if z == 0 else MX[z % 4] for z in range(NZ)])
    mat_z = np.zeros((NZ, 2 * NZ))
    for z in range(NZ):
        e, c = divmod(z, 4)
        for m in range(5):
            if 4 * e + m < NZ:
                mat_z[4 * e + m, z] += A[c, m]
            if c == 0 and e > 0:
                mat_z[4 * (e - 1) + m, NZ + z] += A[4, m]
    mat_y = np.zeros((2 * NY, NY))
    for y in range(NY):
        e, b = divmod(y, 4)
        for m in range(5):
            mat_y[y, (4 * e + m) % NY] += A[b, m]
            if b == 0:
                mat_y[NY + y, (4 * (e - 1) + m) % NY] += A[4, m]
    left = np.zeros((3 * NY, EY))
    for y in range(NY):
        e, b = divmod(y, 4)
        left[y, e] += W1[b]
        left[NY + y, e] += 1.0
        if b == 0:
            left[y, (e - 1) % EY] += W1[4]
            left[2 * NY + y, (e - 1) % EY] += 1.0
    left = left / np.tile(my, 3)[:, None]
    right = np.zeros((EZ, 3 * NZ))
    for z in range(NZ):
        e, c = divmod(z, 4)
        right[e, z] += 1.0
        right[e, 2 * NZ + z] += W1[c]
        if c == 0 and e > 0:
            right[e - 1, NZ + z] += 1.0
            right[e - 1, 2 * NZ + z] += W1[4]
    right = right / np.tile(mz, 3)[None, :] * (STEP_DT * STEP_DT)
    left_pad = np.zeros((3 * NY, 128))
    left_pad[:, :EY] = left
    right_pad = np.zeros((128, 3 * NZ))
    right_pad[:EZ] = right
    return f32(mat_z), f32(mat_y), f32(left_pad[:, :EY]), f32(right_pad)


def dft_table():
    angle = np.pi * (np.arange(F) + 0.5) / F
    phase = angle[:, None] * np.arange(NT)[None, :]
    table = np.zeros((2 * F, 128))
    table[:F, :NT] = np.cos(phase)
    table[F:, :NT] = -np.sin(phase)
    return f32(table)


def dot(a, b):
    return jnp.dot(a, b, precision=HIGHEST, preferred_element_type=jnp.float32)


VMEM = pl.BlockSpec(memory_space=pltpu.VMEM)
SMEM = pl.BlockSpec(memory_space=pltpu.SMEM)


def call(kernel, outs, args, name, smem=0, flops=4_000_000, nbytes=1_000_000):
    return pl.pallas_call(
        kernel,
        out_shape=[jax.ShapeDtypeStruct(s, d) for s, d in outs],
        in_specs=[SMEM] * smem + [VMEM] * (len(args) - smem),
        out_specs=[VMEM] * len(outs),
        compiler_params=pltpu.CompilerParams(vmem_limit_bytes=24 * 1024 * 1024),
        cost_estimate=pl.CostEstimate(flops=flops, bytes_accessed=nbytes, transcendentals=0),
        name=name,
    )(*args)


PLANE = (NY, NZ)
FOUR = (4, NY, NZ)
FIVE = (5, NY, NZ)
FP = jnp.float32


def expand_speed(speed, left, right):
    rows = dot(left, speed)
    by_z = dot(rows[:NY], right)
    by_y = dot(rows[NY:], right[:, 2 * NZ :])
    return by_z[:, :NZ], by_z[:, NZ : 2 * NZ], by_y[:NY], by_y[NY:], by_z[:, 2 * NZ :]


def lateral(plane_z, plane_y, coefs):
    return (
        coefs[0] * plane_z[:, :NZ]
        + coefs[1] * plane_z[:, NZ:]
        + coefs[2] * plane_y[:NY]
        + coefs[3] * plane_y[NY:]
    )


def to_right(sx, u):
    total = float(AB[4, 0]) * u[0]
    for m in range(1, 4):
        total = total + float(AB[4, m]) * u[m]
    return sx * total


def start_kernel(par, now, speed, left, right, coef_ref, first_ref, msg_ref):
    coefs = expand_speed(speed[...], left[...], right[...])
    for i in range(5):
        coef_ref[i] = coefs[i]
    g = to_right(coefs[4], [now[k] for k in range(4)])
    first_ref[...] = g
    msg_ref[:NY] = jnp.where(par[0] == 1, now[0], g)
    msg_ref[NY:] = speed[...]


def base_first_kernel(wave, now, vel, src, coef, mat_z, mat_y, out):
    base_body(0, wave, now, None, vel, src, coef, None, mat_z, mat_y, out)


def base_body(step, wave, now, prev, vel, src, coef, coef0, mat_z, mat_y, out):
    scale = wave[step] * (STEP_DT * STEP_DT)
    sx = coef[4]
    for k in range(4):
        u = now[k]
        pz = dot(u, mat_z[...])
        py = dot(mat_y[...], u)
        if k == 0:
            if coef0 is None:
                force = 0.5 * lateral(pz, py, [coef[i] for i in range(4)])
            else:
                force = lateral(pz, py, [coef0[i] for i in range(4)]) + coef0[4] * u
        else:
            force = lateral(pz, py, [coef[i] for i in range(4)])
        mix = float(AB[k, 0]) * now[0]
        for m in range(1, 4):
            mix = mix + float(AB[k, m]) * now[m]
        force = force + sx * mix
        if prev is None:
            out[k] = u + STEP_DT * vel[k] + (scale * src[k] - force)
        else:
            out[k] = 2.0 * u - prev[k] + (scale * src[k] - force)


def base_kernel(step, wave, now, prev, src, coef, coef0, mat_z, mat_y, out):
    base_body(step, wave, now, prev, None, src, coef, coef0, mat_z, mat_y, out)


def half_left(plane, coefs, mat_z, mat_y):
    pz = dot(plane, mat_z)
    py = dot(mat_y, plane)
    return 0.5 * lateral(pz, py, coefs) + float(AB[4, 4]) * (coefs[4] * plane)


def inner_first_kernel(
    par, base, now, first, recv, speed, coef, left, right, mat_z, mat_y, tent_ref, msg_ref, cleft_ref
):
    odd = par[0] == 1
    coefs = expand_speed(jnp.where(odd, recv[NY:], 0.0), left[...], right[...])
    for i in range(5):
        cleft_ref[i] = coefs[i]
    share = half_left(now[0], coefs, mat_z[...], mat_y[...])
    inner_finish(odd, base, now, first[...], recv[:NY], coef[4], share, tent_ref, msg_ref)
    msg_ref[2 * NY :] = speed[...]


def inner_finish(odd, base, now, g_now, inner, sx, share, tent_ref, msg_ref):
    even_part = jnp.where(odd, 0.0, sx * inner)
    tent = []
    for k in range(4):
        value = base[k] - float(AB[k, 4]) * even_part
        if k == 0:
            value = value - jnp.where(odd, inner, 0.0)
            if share is not None:
                value = value - share
        tent_ref[k] = value
        tent.append(value)
    msg_ref[:NY] = jnp.where(odd, g_now, now[0])
    msg_ref[NY : 2 * NY] = jnp.where(odd, to_right(sx, tent), tent[0])


def inner_kernel(par, base, now, g_now, recv, coef, tent_ref, msg_ref):
    odd = par[0] == 1
    inner_finish(odd, base, now, g_now[...], recv[...], coef[4], None, tent_ref, msg_ref)


def outer_finish(odd, tent, sx, sx_left, recv0, recv1, g_own, u0_own, share, refs):
    u_ref, msg_ref, outer_ref = refs
    odd_part = jnp.where(odd, sx * recv0, 0.0)
    values = []
    for k in range(4):
        value = tent[k] - float(AB[k, 4]) * odd_part
        if k == 0:
            lost = recv0 if share is None else recv0 + share
            value = value - jnp.where(odd, 0.0, lost)
        u_ref[k] = value
        values.append(value)
    msg_ref[...] = jnp.where(odd, values[0], to_right(sx, values))
    mine = g_own if share is None else g_own + share
    outer_ref[...] = recv1 - jnp.where(odd, mine, KAPPA * sx_left * sx_left * u0_own)


def outer_first_kernel(
    par, tent, now, first, recv, inner, coef, cleft, left, right, mat_z, mat_y,
    u_ref, msg_ref, outer_ref, coef0_ref, sxl_ref, last_ref,
):
    odd = par[0] == 1
    theirs = expand_speed(recv[2 * NY :], left[...], right[...])
    coefs = [jnp.where(odd, coef[i], theirs[i]) for i in range(5)]
    recv0 = recv[:NY]
    plane = jnp.where(odd, recv0, now[0])
    share = half_left(plane, coefs, mat_z[...], mat_y[...])
    on_left = [jnp.where(odd, cleft[i], theirs[i]) for i in range(5)]
    for i in range(4):
        coef0_ref[i] = 0.5 * (coef[i] + on_left[i])
    coef0_ref[4] = float(AB[4, 4]) * on_left[4]
    sxl_ref[...] = on_left[4]
    last_ref[...] = jnp.where(odd, recv0, inner[:NY])
    outer_finish(
        odd, tent, coef[4], on_left[4], recv0, recv[NY : 2 * NY], first[...], now[0], share,
        (u_ref, msg_ref, outer_ref),
    )


def outer_kernel(par, tent, now, g_now, recv, inner, coef, sxl, u_ref, msg_ref, outer_ref, last_ref):
    odd = par[0] == 1
    recv0 = recv[:NY]
    last_ref[...] = jnp.where(odd, recv0, inner[...])
    outer_finish(
        odd, tent, coef[4], sxl[...], recv0, recv[NY:], g_now[...], now[0], None,
        (u_ref, msg_ref, outer_ref),
    )


def both_kernel(par, base, inner, outer, coef, u_ref, g_ref, msg_ref, last_ref):
    odd = par[0] == 1
    last = jnp.where(odd, outer[...], inner[...])
    from_left = jnp.where(odd, inner[...], outer[...])
    sx = coef[4]
    pull = sx * last
    values = []
    for k in range(4):
        value = base[k] - float(AB[k, 4]) * pull
        if k == 0:
            value = value - from_left
        u_ref[k] = value
        values.append(value)
    g = to_right(sx, values)
    g_ref[...] = g
    msg_ref[...] = jnp.where(odd, values[0], g)
    last_ref[...] = last


def slots_kernel(elem, weight, pick_ref, spread_ref):
    e = elem[...]
    ey = e // EZ
    ez = e - ey * EZ
    z = lax.broadcasted_iota(jnp.int32, (NZ, CAP), 0)
    for c in range(5):
        hot = (z == 4 * ez + c).astype(FP).astype(jnp.bfloat16)
        for half in range(2):
            pick_ref[half * NZ : (half + 1) * NZ, c * CAP : (c + 1) * CAP] = hot
    y = lax.broadcasted_iota(jnp.int32, (NY, CAP), 0)
    masks = []
    for b in range(5):
        row = 4 * ey + b
        row = jnp.where(row >= NY, row - NY, row)
        masks.append(y == row)
    for a in range(5):
        for c in range(5):
            total = jnp.zeros((NY, CAP), FP)
            for b in range(5):
                at = 25 * a + 5 * b + c
                total = jnp.where(masks[b], weight[at : at + 1, :], total)
            spread_ref[c, a * NY : (a + 1) * NY, :] = total


def sample(u, last, pick, spread):
    acc = jnp.zeros((8, CAP), FP)
    for a in range(5):
        plane = last[...] if a == 4 else u[a]
        high = plane.astype(jnp.bfloat16)
        low = (plane - high.astype(FP)).astype(jnp.bfloat16)
        got = jnp.dot(
            jnp.concatenate([high, low], 1), pick[...], preferred_element_type=jnp.float32
        )
        for c in range(5):
            part = got[:, c * CAP : (c + 1) * CAP] * spread[c, a * NY : (a + 1) * NY, :]
            acc = acc + jnp.sum(part.reshape(NY // 8, 8, CAP), 0)
    return jnp.sum(acc, 0, keepdims=True)


def sample_two_kernel(u0, l0, u1, l1, pick, spread, out):
    out[0:1, :] = sample(u0, l0, pick, spread)
    out[1:2, :] = sample(u1, l1, pick, spread)


def sample_one_kernel(u0, l0, pick, spread, out):
    out[...] = sample(u0, l0, pick, spread)


def stations_kernel(blocks, stations, row_ref, lane_ref):
    lanes = []
    for j in range(2 * SB):
        wanted = blocks[0, j // SB] * SB + j % SB
        hit = jnp.zeros((8, CAP), FP)
        for r in range(16):
            hit = hit + jnp.where(stations[8 * r : 8 * r + 8, :] == wanted, 1.0, 0.0)
        lane_ref[j : j + 1, :] = jnp.sum(hit, 0, keepdims=True)
    lane = lane_ref[...]
    ids = stations[...].astype(FP)
    at = lax.dot_general(
        lane, ids, (((1,), (1,)), ((), ())), precision=HIGHEST, preferred_element_type=jnp.float32
    )
    j = lax.broadcasted_iota(jnp.int32, (2 * SB, 128), 0)
    wanted = jnp.where(j < SB, blocks[0, 0] * SB + j, blocks[0, 1] * SB + (j - SB))
    row_ref[...] = jnp.where(jnp.abs(at - wanted.astype(FP)) < 0.5, 1.0, 0.0)


def cross_kernel(gathered, row, lane, table, spread_a, spread_b, out):
    t_of = lax.broadcasted_iota(jnp.int32, (2 * SB, 128), 1)
    samples = jnp.zeros((2 * SB, 128), FP)
    for t in range(NT):
        slab = gathered[pl.ds(t, 128, stride=8), :]
        found = dot(row[...], slab) * lane[...]
        samples = jnp.where(t_of == t, jnp.sum(found, 1, keepdims=True), samples)
    spectra = lax.dot_general(
        table[...], samples, (((1,), (1,)), ((), ())), precision=HIGHEST,
        preferred_element_type=jnp.float32,
    ).astype(jnp.bfloat16)
    second = jnp.dot(spectra, spread_b[...], preferred_element_type=jnp.float32) * (1.0 / NT)
    b_re = second[:F]
    b_im = second[F:]
    for i in range(8):
        cols = slice(128 * i, 128 * (i + 1))
        first = jnp.dot(spectra, spread_a[:, cols], preferred_element_type=jnp.float32)
        a_re = first[:F]
        a_im = first[F:]
        out[0, 0, :, cols] = (a_re * b_re + a_im * b_im).astype(jnp.bfloat16)
        out[0, 1, :, cols] = (a_im * b_re - a_re * b_im).astype(jnp.bfloat16)


def body(
    now, vel, speed_sq, src, wavelet, slot_elem, slot_station, slot_weight, pair_blocks, devices
):
    inner_route = [(i, i ^ 1) for i in range(devices)]
    outer_route = [(i, (i + 1 if i % 2 else i - 1) % devices) for i in range(devices)]

    def swap_inner(x):
        return lax.ppermute(x, AXES, inner_route)

    def swap_outer(x):
        return lax.ppermute(x, AXES, outer_route)

    mat_z, mat_y, left, right = (jnp.asarray(x) for x in tables())
    table = jnp.asarray(dft_table())
    reps = np.zeros((2 * SB, SB * SB))
    for i in range(SB):
        reps[i, i * SB : (i + 1) * SB] = 1.0
    tiles = np.zeros((2 * SB, 128))
    for i in range(128):
        tiles[SB + i % SB, i] = 1.0
    reps = jnp.asarray(reps, jnp.bfloat16)
    tiles = jnp.asarray(tiles, jnp.bfloat16)

    par = (lax.axis_index("bulk") % 2).astype(jnp.int32).reshape(1)
    speed = jnp.pad(speed_sq[0], ((0, 0), (0, 128 - EZ)))

    coef, g0, msg = call(
        start_kernel, [(FIVE, FP), (PLANE, FP), ((NY + EY, NZ), FP)], (par, now, speed, left, right),
        "start", 1,
    )
    inner0 = swap_inner(msg)
    (base,) = call(
        base_first_kernel, [(FOUR, FP)], (wavelet, now, vel, src, coef, mat_z, mat_y), "base0", 1
    )
    tent, msg, cleft = call(
        inner_first_kernel, [(FOUR, FP), ((2 * NY + EY, NZ), FP), (FIVE, FP)],
        (par, base, now, g0, inner0, speed, coef, left, right, mat_z, mat_y), "inner0", 1,
    )
    outer0 = swap_outer(msg)
    pick, spread = call(
        slots_kernel, [((2 * NZ, 5 * CAP), jnp.bfloat16), ((5, 5 * NY, CAP), FP)],
        (slot_elem.reshape(1, CAP), slot_weight), "slots",
    )
    row, lane = call(
        stations_kernel, [((2 * SB, 128), FP), ((2 * SB, CAP), FP)],
        (pair_blocks, slot_station.reshape(128, CAP)), "stations", 1,
    )
    u_a = now
    u_b, msg, outer, coef0, sxl, last_a = call(
        outer_first_kernel,
        [(FOUR, FP), (PLANE, FP), (PLANE, FP), (FIVE, FP), (PLANE, FP), (PLANE, FP)],
        (par, tent, now, g0, outer0, inner0, coef, cleft, left, right, mat_z, mat_y), "outer0", 1,
    )
    rows = []
    step = 1
    while True:
        inner = swap_inner(msg)
        (base,) = call(
            functools.partial(base_kernel, step), [(FOUR, FP)],
            (wavelet, u_b, u_a, src, coef, coef0, mat_z, mat_y), "base", 1,
        )
        u_c, g_c, msg, last_b = call(
            both_kernel, [(FOUR, FP), (PLANE, FP), (PLANE, FP), (PLANE, FP)],
            (par, base, inner, outer, coef), "both", 1,
        )
        if step == NT - 1:
            break
        inner = swap_inner(msg)
        (base,) = call(
            functools.partial(base_kernel, step + 1), [(FOUR, FP)],
            (wavelet, u_c, u_b, src, coef, coef0, mat_z, mat_y), "base", 1,
        )
        tent, msg = call(
            inner_kernel, [(FOUR, FP), ((2 * NY, NZ), FP)],
            (par, base, u_c, g_c, inner, coef), "inner", 1,
        )
        recv = swap_outer(msg)
        (two,) = call(
            sample_two_kernel, [((2, CAP), FP)], (u_a, last_a, u_b, last_b, pick, spread), "sample2"
        )
        rows.append(two)
        u_a = u_c
        u_b, msg, outer, last_a = call(
            outer_kernel, [(FOUR, FP), (PLANE, FP), (PLANE, FP), (PLANE, FP)],
            (par, tent, u_c, g_c, recv, inner, coef, sxl), "outer", 1,
        )
        step += 2
    (one,) = call(sample_one_kernel, [((1, CAP), FP)], (u_a, last_a, pick, spread), "sample")
    rows.append(one)
    (one,) = call(sample_one_kernel, [((1, CAP), FP)], (u_b, last_b, pick, spread), "sample")
    rows.append(one)
    mine = jnp.pad(jnp.concatenate(rows, 0), ((0, 2), (0, 0)))
    gathered = lax.all_to_all(
        jnp.broadcast_to(mine[None], (devices, 8, CAP)), AXES, 0, 0, tiled=True
    )
    (cross,) = call(
        cross_kernel, [((1, 2, F, SB * SB), jnp.bfloat16)],
        (gathered.reshape(8 * devices, CAP), row, lane, table, reps, tiles), "cross",
    )
    return u_c, cross


def solution(mesh):
    split = P(AXES)
    in_specs = (
        P(AXES, None, None), P(AXES, None, None), P(AXES, None, None), P(AXES, None, None),
        P(), split, P(), P(None, AXES), P(AXES, None),
    )
    out_specs = (P(AXES, None, None), P(AXES, None, None, None))
    devices = math.prod(mesh.shape.values())
    run = functools.partial(body, devices=devices)
    return jax.shard_map(run, mesh=mesh, in_specs=in_specs, out_specs=out_specs, check_vma=False)
```

profile of v0, /device:TPU:1, one launch (start us, length us, event | category | flops | bytes accessed | tf_op | source)
XLA Modules:
  0.0 82.5 jit_solution(13970063472635245792)
XLA Ops:
  1.4 0.9 %copy-done.2 = f32[4,96,128]{2,1,0:T(8,128)S(1)} copy-done((f32[4,96,128]{2,1,0:T(8,128)S(1)}, f32[4,96,128]{2,1,0:T(8,128)}, u32[]{:S(2)}) %copy-start.2) | copy-done | bytes 196632
  2.3 0.9 %copy-done.8 = f32[128,384]{1,0:T(8,128)S(1)} copy-done((f32[128,384]{1,0:T(8,128)S(1)}, f32[128,384]{1,0:T(8,128)}, u32[]{:S(2)}) %copy-start.8) | copy-done | bytes 196632
  3.3 0.9 %copy-done.10 = f32[288,24]{1,0:T(8,128)S(1)} copy-done((f32[288,24]{1,0:T(8,128)S(1)}, f32[288,24]{1,0:T(8,128)}, u32[]{:S(2)}) %copy-start.10) | copy-done | bytes 27672
  4.8 1.5 %collective-permute-start = (f32[120,128]{1,0:T(8,128)S(1)}, f32[120,128]{1,0:T(8,128)S(1)}, u32[]{:S(2)}, u32[]{:S(2)}) collective-permute-start(f32[120,128]{1,0:T(8,128)S(1)} %get-tuple-element.42), channel_id=1, source_target_pairs={{0,1},{1,0},{2,3},{3,2},{4,5},{5,4},{6,7},{7,6},{8,9},{9,8},{10,11... | collective-permute-start | bytes 184328 | tf_op jit(solution)/shard_map/ppermute | solution.py:394
  6.3 0.9 %copy-done = f32[128,256]{1,0:T(8,128)S(1)} copy-done((f32[128,256]{1,0:T(8,128)S(1)}, f32[128,256]{1,0:T(8,128)}, u32[]{:S(2)}) %copy-start) | copy-done | bytes 131096
  7.2 0.9 %copy-done.4 = f32[4,96,128]{2,1,0:T(8,128)S(1)} copy-done((f32[4,96,128]{2,1,0:T(8,128)S(1)}, f32[4,96,128]{2,1,0:T(8,128)}, u32[]{:S(2)}) %copy-start.4) | copy-done | bytes 196632
  9.1 0.9 %copy-done.12 = f32[4,96,128]{2,1,0:T(8,128)S(1)} copy-done((f32[4,96,128]{2,1,0:T(8,128)S(1)}, f32[4,96,128]{2,1,0:T(8,128)}, u32[]{:S(2)}) %copy-start.12) | copy-done | bytes 196632
  10.6 1.4 %base0.1.base = f32[4,96,128]{2,1,0:T(8,128)S(1)} custom-call(f32[6]{0:T(128)S(1)} %copy-done.16, f32[4,96,128]{2,1,0:T(8,128)S(1)} %copy-done.2, f32[4,96,128]{2,1,0:T(8,128)S(1)} %copy-done.12, f32[4,96,128]{2,1,0:T(8,128)S(1)} %copy-done.4, f32[5,96,128]{2,1,0:T(8,128)S(1)} %get-tuple-element.40.coef, f32[128,256]{1,0:T(8,128)S(1)} %copy-done, ...), custom_call_target="tpu_custom_call" | custom-call | flops 4000000 | bytes 1000000 | tf_op jit(solution)/shard_map/base0/pallas_call | solution.py:111
  12.9 1.4 %collective-permute-start.1 = (f32[216,128]{1,0:T(8,128)S(1)}, f32[216,128]{1,0:T(8,128)S(1)}, u32[]{:S(2)}, u32[]{:S(2)}) collective-permute-start(f32[216,128]{1,0:T(8,128)S(1)} %get-tuple-element.44), channel_id=1, source_target_pairs={{0,127},{1,2},{2,1},{3,4},{4,3},{5,6},{6,5},{7,8},{8,7},{9,10},{10... | collective-permute-start | bytes 331784 | tf_op jit(solution)/shard_map/ppermute | solution.py:397
  14.3 2.9 %collective-permute-done.1.recv = f32[216,128]{1,0:T(8,128)S(1)} collective-permute-done((f32[216,128]{1,0:T(8,128)S(1)}, f32[216,128]{1,0:T(8,128)S(1)}, u32[]{:S(2)}, u32[]{:S(2)}) %collective-permute-start.1) | collective-permute-done | bytes 110624 | tf_op jit(solution)/shard_map/ppermute | solution.py:397
  18.1 7.2 %collective-permute-start.2 = (f32[96,128]{1,0:T(8,128)S(1)}, f32[96,128]{1,0:T(8,128)S(1)}, u32[]{:S(2)}, u32[]{:S(2)}) collective-permute-start(f32[96,128]{1,0:T(8,128)S(1)} %get-tuple-element.48), channel_id=1, source_target_pairs={{0,1},{1,0},{2,3},{3,2},{4,5},{5,4},{6,7},{7,6},{8,9},{9,8},{10,11... | collective-permute-start | bytes 147464 | tf_op jit(solution)/shard_map/ppermute | solution.py:394
  25.3 1.4 %base.5 = f32[4,96,128]{2,1,0:T(8,128)S(1)} custom-call(f32[6]{0:T(128)S(1)} %copy-done.17, f32[4,96,128]{2,1,0:T(8,128)S(1)} %get-tuple-element.46.now.prev.u1, f32[4,96,128]{2,1,0:T(8,128)S(1)} %copy-done.2, f32[4,96,128]{2,1,0:T(8,128)S(1)} %copy-done.5, f32[5,96,128]{2,1,0:T(8,128)S(1)} %get-tuple-element.40.coef, ...), custom_call_target="tpu_custom_call" | custom-call | flops 4000000 | bytes 1000000 | tf_op jit(solution)/shard_map/base/pallas_call | solution.py:111
  26.9 1.4 %base.6 = f32[4,96,128]{2,1,0:T(8,128)S(1)} custom-call(f32[6]{0:T(128)S(1)} %copy-done.17, f32[4,96,128]{2,1,0:T(8,128)S(1)} %get-tuple-element.50.now.prev.u0, f32[4,96,128]{2,1,0:T(8,128)S(1)} %get-tuple-element.46.now.prev.u1, f32[4,96,128]{2,1,0:T(8,128)S(1)} %copy-done.5, f32[5,96,128]{2,1,0:T(8,128)S(1)} %get-tuple-element.40.coef, ...), custom_call_target="tpu_custom_call" | custom-call | flops 4000000 | bytes 1000000 | tf_op jit(solution)/shard_map/base/pallas_call | solution.py:111
  28.4 4.0 %collective-permute-done.4.recv = f32[192,128]{1,0:T(8,128)S(1)} collective-permute-done((f32[192,128]{1,0:T(8,128)S(1)}, f32[192,128]{1,0:T(8,128)S(1)}, u32[]{:S(2)}, u32[]{:S(2)}) %collective-permute-start.4) | collective-permute-done | bytes 98336 | tf_op jit(solution)/shard_map/ppermute | solution.py:397
  32.5 6.0 %collective-permute-start.5 = (f32[96,128]{1,0:T(8,128)S(1)}, f32[96,128]{1,0:T(8,128)S(1)}, u32[]{:S(2)}, u32[]{:S(2)}) collective-permute-start(f32[96,128]{1,0:T(8,128)S(1)} %get-tuple-element.57), channel_id=1, source_target_pairs={{0,1},{1,0},{2,3},{3,2},{4,5},{5,4},{6,7},{7,6},{8,9},{9,8},{10,11... | collective-permute-start | bytes 147464 | tf_op jit(solution)/shard_map/ppermute | solution.py:394
  38.5 1.4 %base.7 = f32[4,96,128]{2,1,0:T(8,128)S(1)} custom-call(f32[6]{0:T(128)S(1)} %copy-done.17, f32[4,96,128]{2,1,0:T(8,128)S(1)} %get-tuple-element.56.now.prev.u1, f32[4,96,128]{2,1,0:T(8,128)S(1)} %get-tuple-element.50.now.prev.u0, f32[4,96,128]{2,1,0:T(8,128)S(1)} %copy-done.5, f32[5,96,128]{2,1,0:T(8,128)S(1)} %get-tuple-element.40.coef, ...), custom_call_target="tpu_custom_call" | custom-call | flops 4000000 | bytes 1000000 | tf_op jit(solution)/shard_map/base/pallas_call | solution.py:111
  40.1 1.4 %base.8 = f32[4,96,128]{2,1,0:T(8,128)S(1)} custom-call(f32[6]{0:T(128)S(1)} %copy-done.17, f32[4,96,128]{2,1,0:T(8,128)S(1)} %get-tuple-element.59.now.prev.u0, f32[4,96,128]{2,1,0:T(8,128)S(1)} %get-tuple-element.56.now.prev.u1, f32[4,96,128]{2,1,0:T(8,128)S(1)} %copy-done.5, f32[5,96,128]{2,1,0:T(8,128)S(1)} %get-tuple-element.40.coef, ...), custom_call_target="tpu_custom_call" | custom-call | flops 4000000 | bytes 1000000 | tf_op jit(solution)/shard_map/base/pallas_call | solution.py:111
  41.7 4.0 %collective-permute-done.7.recv = f32[192,128]{1,0:T(8,128)S(1)} collective-permute-done((f32[192,128]{1,0:T(8,128)S(1)}, f32[192,128]{1,0:T(8,128)S(1)}, u32[]{:S(2)}, u32[]{:S(2)}) %collective-permute-start.7) | collective-permute-done | bytes 98336 | tf_op jit(solution)/shard_map/ppermute | solution.py:397
  45.7 6.2 %collective-permute-start.8 = (f32[96,128]{1,0:T(8,128)S(1)}, f32[96,128]{1,0:T(8,128)S(1)}, u32[]{:S(2)}, u32[]{:S(2)}) collective-permute-start(f32[96,128]{1,0:T(8,128)S(1)} %get-tuple-element.65), channel_id=1, source_target_pairs={{0,1},{1,0},{2,3},{3,2},{4,5},{5,4},{6,7},{7,6},{8,9},{9,8},{10,11... | collective-permute-start | bytes 147464 | tf_op jit(solution)/shard_map/ppermute | solution.py:394
  53.9 1.4 %base.9 = f32[4,96,128]{2,1,0:T(8,128)S(1)} custom-call(f32[6]{0:T(128)S(1)} %copy-done.17, f32[4,96,128]{2,1,0:T(8,128)S(1)} %get-tuple-element.64.now.u0, f32[4,96,128]{2,1,0:T(8,128)S(1)} %get-tuple-element.59.now.prev.u0, f32[4,96,128]{2,1,0:T(8,128)S(1)} %copy-done.5, f32[5,96,128]{2,1,0:T(8,128)S(1)} %get-tuple-element.40.coef, ...), custom_call_target="tpu_custom_call" | custom-call | flops 4000000 | bytes 1000000 | tf_op jit(solution)/shard_map/base/pallas_call | solution.py:111
  57.8 8.4 %all-to-all-start = ((f32[128,8,128]{2,1,0:T(8,128)}), f32[128,8,128]{2,1,0:T(8,128)S(1)}, u32[]{:S(2)}, u32[]{:S(2)}) async-start(f32[128,8,128]{2,1,0:T(8,128)} %broadcast_in_dim.2), calls=%async_computation | async-start | bytes 1048576 | tf_op jit(solution)/shard_map/all_to_all | solution.py:479
  66.3 1.2 %stations.1 = (f32[64,128]{1,0:T(8,128)S(1)}, f32[64,128]{1,0:T(8,128)S(1)}) custom-call(s32[1,2]{1,0:T(1,128)S(1)} %copy-done.20, s32[128,128]{1,0:T(8,128)S(1)} %bitcast.6), custom_call_target="tpu_custom_call" | custom-call | flops 4000000 | bytes 1000000 | tf_op jit(solution)/shard_map/stations/pallas_call | solution.py:111
  67.5 12.3 %all-to-all-done = f32[128,8,128]{2,1,0:T(8,128)S(1)} async-done(((f32[128,8,128]{2,1,0:T(8,128)}), f32[128,8,128]{2,1,0:T(8,128)S(1)}, u32[]{:S(2)}, u32[]{:S(2)}) %all-to-all-start) | async-done | bytes 524320 | tf_op jit(solution)/shard_map/all_to_all | solution.py:479
  79.8 2.7 %cross.1 = bf16[1,2,256,1024]{3,2,1,0:T(8,128)(2,1)} custom-call(f32[1024,128]{1,0:T(8,128)S(1)} %bitcast.5, f32[64,128]{1,0:T(8,128)S(1)} %get-tuple-element.76.row, f32[64,128]{1,0:T(8,128)S(1)} %get-tuple-element.77.lane, f32[512,128]{1,0:T(8,128)S(1)} %copy-done.11, bf16[64,1024]{1,0:T(8,128)(2,1)S(1)} %copy-done.13, bf16[64,128]{1,0:T(8,128)(2,1)S(1)} %copy-done.18), custom_call_target="tpu_custom_call" | custom-call | flops 4000000 | bytes 1000000 | tf_op jit(solution)/shard_map/cross/pallas_call | solution.py:111
  (64 shorter events, 9.8 us)
Async XLA Ops:
  0.6 11.4 %copy-start.1 = (f32[128,256]{1,0:T(8,128)S(1)}, f32[128,256]{1,0:T(8,128)}, u32[]{:S(2)}) copy-start(f32[128,256]{1,0:T(8,128)} %constant.34.clone.mat_z) | copy-start | bytes 393220
  1.4 0.9 %copy-start.2 = (f32[4,96,128]{2,1,0:T(8,128)S(1)}, f32[4,96,128]{2,1,0:T(8,128)}, u32[]{:S(2)}) copy-start(f32[4,96,128]{2,1,0:T(8,128)} %u0.1) | copy-start | bytes 589828
  4.2 7.9 %copy-start.9 = (f32[128,384]{1,0:T(8,128)S(1)}, f32[128,384]{1,0:T(8,128)}, u32[]{:S(2)}) copy-start(f32[128,384]{1,0:T(8,128)} %constant.37.clone.right) | copy-start | bytes 589828
  4.8 7.2 %collective-permute-start = (f32[120,128]{1,0:T(8,128)S(1)}, f32[120,128]{1,0:T(8,128)S(1)}, u32[]{:S(2)}, u32[]{:S(2)}) collective-permute-start(f32[120,128]{1,0:T(8,128)S(1)} %get-tuple-element.42), channel_id=1, source_target_pairs={{0,1},{1,0},{2,3},{3,2},{4,5},{5,4},{6,7},{7,6},{8,9},{9,8},{10,11... | collective-permute-start | bytes 184328 | tf_op jit(solution)/shard_map/ppermute | solution.py:394
  12.1 13.2 %copy-start.5 = (f32[4,96,128]{2,1,0:T(8,128)S(1)}, f32[4,96,128]{2,1,0:T(8,128)}, u32[]{:S(2)}) copy-start(f32[4,96,128]{2,1,0:T(8,128)} %src.11) | copy-start | bytes 589828
  12.1 13.2 %copy-start.7 = (f32[192,96]{1,0:T(8,128)S(1)}, f32[192,96]{1,0:T(8,128)}, u32[]{:S(2)}) copy-start(f32[192,96]{1,0:T(8,128)} %constant.35.clone.mat_y) | copy-start | bytes 221188
  12.1 13.2 %copy-start.17 = (f32[6]{0:T(128)S(1)}, f32[6]{0:T(128)}, u32[]{:S(2)}) copy-start(f32[6]{0:T(128)} %wave.11) | copy-start | bytes 76
  12.9 4.3 %collective-permute-start.1 = (f32[216,128]{1,0:T(8,128)S(1)}, f32[216,128]{1,0:T(8,128)S(1)}, u32[]{:S(2)}, u32[]{:S(2)}) collective-permute-start(f32[216,128]{1,0:T(8,128)S(1)} %get-tuple-element.44), channel_id=1, source_target_pairs={{0,127},{1,2},{2,1},{3,4},{4,3},{5,6},{6,5},{7,8},{8,7},{9,10},{10... | collective-permute-start | bytes 331784 | tf_op jit(solution)/shard_map/ppermute | solution.py:397
  18.1 8.6 %collective-permute-start.2 = (f32[96,128]{1,0:T(8,128)S(1)}, f32[96,128]{1,0:T(8,128)S(1)}, u32[]{:S(2)}, u32[]{:S(2)}) collective-permute-start(f32[96,128]{1,0:T(8,128)S(1)} %get-tuple-element.48), channel_id=1, source_target_pairs={{0,1},{1,0},{2,3},{3,2},{4,5},{5,4},{6,7},{7,6},{8,9},{9,8},{10,11... | collective-permute-start | bytes 147464 | tf_op jit(solution)/shard_map/ppermute | solution.py:394
  26.8 1.5 %collective-permute-start.3 = (f32[96,128]{1,0:T(8,128)S(1)}, f32[96,128]{1,0:T(8,128)S(1)}, u32[]{:S(2)}, u32[]{:S(2)}) collective-permute-start(f32[96,128]{1,0:T(8,128)S(1)} %get-tuple-element.52), channel_id=1, source_target_pairs={{0,1},{1,0},{2,3},{3,2},{4,5},{5,4},{6,7},{7,6},{8,9},{9,8},{10,11... | collective-permute-start | bytes 147464 | tf_op jit(solution)/shard_map/ppermute | solution.py:394
  28.3 4.1 %collective-permute-start.4 = (f32[192,128]{1,0:T(8,128)S(1)}, f32[192,128]{1,0:T(8,128)S(1)}, u32[]{:S(2)}, u32[]{:S(2)}) collective-permute-start(f32[192,128]{1,0:T(8,128)S(1)} %get-tuple-element.54), channel_id=1, source_target_pairs={{0,127},{1,2},{2,1},{3,4},{4,3},{5,6},{6,5},{7,8},{8,7},{9,10},{10... | collective-permute-start | bytes 294920 | tf_op jit(solution)/shard_map/ppermute | solution.py:397
  32.5 7.4 %collective-permute-start.5 = (f32[96,128]{1,0:T(8,128)S(1)}, f32[96,128]{1,0:T(8,128)S(1)}, u32[]{:S(2)}, u32[]{:S(2)}) collective-permute-start(f32[96,128]{1,0:T(8,128)S(1)} %get-tuple-element.57), channel_id=1, source_target_pairs={{0,1},{1,0},{2,3},{3,2},{4,5},{5,4},{6,7},{7,6},{8,9},{9,8},{10,11... | collective-permute-start | bytes 147464 | tf_op jit(solution)/shard_map/ppermute | solution.py:394
  40.0 1.5 %collective-permute-start.6 = (f32[96,128]{1,0:T(8,128)S(1)}, f32[96,128]{1,0:T(8,128)S(1)}, u32[]{:S(2)}, u32[]{:S(2)}) collective-permute-start(f32[96,128]{1,0:T(8,128)S(1)} %get-tuple-element.61), channel_id=1, source_target_pairs={{0,1},{1,0},{2,3},{3,2},{4,5},{5,4},{6,7},{7,6},{8,9},{9,8},{10,11... | collective-permute-start | bytes 147464 | tf_op jit(solution)/shard_map/ppermute | solution.py:394
  40.1 11.8 %copy-start.14 = (f32[125,128]{1,0:T(8,128)S(1)}, f32[125,128]{1,0:T(8,128)}, u32[]{:S(2)}) copy-start(f32[125,128]{1,0:T(8,128)} %weight.1) | copy-start | bytes 192004
  40.1 11.8 %copy-start.19 = (s32[128]{0:T(128)S(1)}, s32[128]{0:T(128)}, u32[]{:S(2)}) copy-start(s32[128]{0:T(128)} %param.21) | copy-start | bytes 1540
  41.5 10.9 %copy-start.3 = (f32[4,96,128]{2,1,0:T(8,128)S(1)}, f32[4,96,128]{2,1,0:T(8,128)}, u32[]{:S(2)}) copy-start(f32[4,96,128]{2,1,0:T(8,128)} %u0.1) | copy-start | bytes 589828
  41.6 4.1 %collective-permute-start.7 = (f32[192,128]{1,0:T(8,128)S(1)}, f32[192,128]{1,0:T(8,128)S(1)}, u32[]{:S(2)}, u32[]{:S(2)}) collective-permute-start(f32[192,128]{1,0:T(8,128)S(1)} %get-tuple-element.63), channel_id=1, source_target_pairs={{0,127},{1,2},{2,1},{3,4},{4,3},{5,6},{6,5},{7,8},{8,7},{9,10},{10... | collective-permute-start | bytes 294920 | tf_op jit(solution)/shard_map/ppermute | solution.py:397
  45.7 10.0 %collective-permute-start.8 = (f32[96,128]{1,0:T(8,128)S(1)}, f32[96,128]{1,0:T(8,128)S(1)}, u32[]{:S(2)}, u32[]{:S(2)}) collective-permute-start(f32[96,128]{1,0:T(8,128)S(1)} %get-tuple-element.65), channel_id=1, source_target_pairs={{0,1},{1,0},{2,3},{3,2},{4,5},{5,4},{6,7},{7,6},{8,9},{9,8},{10,11... | collective-permute-start | bytes 147464 | tf_op jit(solution)/shard_map/ppermute | solution.py:394
  56.9 9.3 %copy-start.15 = (s32[16384]{0:T(1024)S(1)}, s32[16384]{0:T(1024)}, u32[]{:S(2)}) copy-start(s32[16384]{0:T(1024)} %param.22) | copy-start | bytes 196612
  56.9 9.3 %copy-start.20 = (s32[1,2]{1,0:T(1,128)S(1)}, s32[1,2]{1,0:T(1,128)}, u32[]{:S(2)}) copy-start(s32[1,2]{1,0:T(1,128)} %blocks.1) | copy-start | bytes 28
  56.9 22.8 %copy-start.11 = (f32[512,128]{1,0:T(8,128)S(1)}, f32[512,128]{1,0:T(8,128)}, u32[]{:S(2)}) copy-start(f32[512,128]{1,0:T(8,128)} %constant.38.clone.table) | copy-start | bytes 786436
  57.0 22.8 %copy-start.13 = (bf16[64,1024]{1,0:T(8,128)(2,1)S(1)}, bf16[64,1024]{1,0:T(8,128)(2,1)}, u32[]{:S(2)}) copy-start(bf16[64,1024]{1,0:T(8,128)(2,1)} %constant.39.clone.spread_a) | copy-start | bytes 393220
  57.0 22.8 %copy-start.18 = (bf16[64,128]{1,0:T(8,128)(2,1)S(1)}, bf16[64,128]{1,0:T(8,128)(2,1)}, u32[]{:S(2)}) copy-start(bf16[64,128]{1,0:T(8,128)(2,1)} %constant.40.clone.spread_b) | copy-start | bytes 49156
  57.8 21.9 %all-to-all-start = ((f32[128,8,128]{2,1,0:T(8,128)}), f32[128,8,128]{2,1,0:T(8,128)S(1)}, u32[]{:S(2)}, u32[]{:S(2)}) async-start(f32[128,8,128]{2,1,0:T(8,128)} %broadcast_in_dim.2), calls=%async_computation | async-start | bytes 1048576 | tf_op jit(solution)/shard_map/all_to_all | solution.py:479
  (7 other events, 6.1 us)
where the time goes:
time: 82.9 us; the launch traced here: 82.5 us
  starting transfers between devices  31.1 us (38%)
  waiting for transfers between devices  23.2 us (28%)
  Pallas kernels  18.5 us (22%)
  local copies, waits for them, and re-layouts  8.72 us (11%)
  between operations  0.99 us (1%)
    ppermute x6, starting transfers between devices, swap_inner(): return lax.ppermute(x, AXES, inner_route)  21.1 us
    pallas_call x23, Pallas kernels, call(): pl.pallas_call(kernel, out_shape=[jax.ShapeDtypeStruct(s, d) for s, d in...  18.5 us
    all_to_all x1, waiting for transfers between devices, body(): lax.all_to_all(jnp.broadcast_to(mine[None], (devices, 8, CAP)), AXES, 0,...  12.3 us
    ppermute x3, waiting for transfers between devices, swap_outer(): return lax.ppermute(x, AXES, outer_route)  10.9 us
    all_to_all x1, starting transfers between devices, body(): lax.all_to_all(jnp.broadcast_to(mine[None], (devices, 8, CAP)), AXES, 0,...  8.43 us
    unnamed x42, local copies, waits for them, and re-layouts  7.14 us
  transfers between devices with their start and end apart: 10, of which 4 were waited for; matrix products, arithmetic and copies ran while one was open for 0% of the time, Pallas kernels for 15%

commit v1 on v0

--- a/solution.py
+++ b/solution.py
@@ -58,13 +58,6 @@
                 mat_z[4 * e + m, z] += A[c, m]
             if c == 0 and e > 0:
                 mat_z[4 * (e - 1) + m, NZ + z] += A[4, m]
-    mat_y = np.zeros((2 * NY, NY))
-    for y in range(NY):
-        e, b = divmod(y, 4)
-        for m in range(5):
-            mat_y[y, (4 * e + m) % NY] += A[b, m]
-            if b == 0:
-                mat_y[NY + y, (4 * (e - 1) + m) % NY] += A[4, m]
     left = np.zeros((3 * NY, EY))
     for y in range(NY):
         e, b = divmod(y, 4)
@@ -83,20 +76,32 @@
             right[e - 1, NZ + z] += 1.0
             right[e - 1, 2 * NZ + z] += W1[4]
     right = right / np.tile(mz, 3)[None, :] * (STEP_DT * STEP_DT)
-    left_pad = np.zeros((3 * NY, 128))
-    left_pad[:, :EY] = left
-    right_pad = np.zeros((128, 3 * NZ))
-    right_pad[:EZ] = right
-    return f32(mat_z), f32(mat_y), f32(left_pad[:, :EY]), f32(right_pad)
+    high = mat_z.astype(jnp.bfloat16).astype(np.float64)
+    low = (mat_z - high).astype(jnp.bfloat16)
+    stack = np.concatenate([mat_z, mat_z], 0).astype(jnp.bfloat16)
+    return np.concatenate([stack, low], 0), f32(left), f32(right)
+
+
+PART_PAIRS = ((0, 0), (1, 0), (0, 1), (1, 1), (2, 0), (0, 2))
+
+
+def parts_of(x, count):
+    parts = []
+    for _ in range(count):
+        part = x.astype(jnp.bfloat16)
+        parts.append(part)
+        x = x - part.astype(x.dtype)
+    return parts
 
 
 def dft_table():
     angle = np.pi * (np.arange(F) + 0.5) / F
     phase = angle[:, None] * np.arange(NT)[None, :]
-    table = np.zeros((2 * F, 128))
-    table[:F, :NT] = np.cos(phase)
-    table[F:, :NT] = -np.sin(phase)
-    return f32(table)
+    parts = parts_of(f32(np.concatenate([np.cos(phase), -np.sin(phase)], 0)), 3)
+    table = np.zeros((2 * F, 128), jnp.bfloat16)
+    for group, (_, part) in enumerate(PART_PAIRS):
+        table[:, 8 * group : 8 * group + NT] = parts[part]
+    return table
 
 
 def dot(a, b):
@@ -105,18 +110,24 @@
 
 VMEM = pl.BlockSpec(memory_space=pltpu.VMEM)
 SMEM = pl.BlockSpec(memory_space=pltpu.SMEM)
-
-
-def call(kernel, outs, args, name, smem=0, flops=4_000_000, nbytes=1_000_000):
+HBM = pl.BlockSpec(memory_space=pltpu.HBM)
+
+
+def call(kernel, outs, args, name, smem=0, specs=None, out_specs=None, scratch=(), flops=4_000_000):
     return pl.pallas_call(
         kernel,
         out_shape=[jax.ShapeDtypeStruct(s, d) for s, d in outs],
-        in_specs=[SMEM] * smem + [VMEM] * (len(args) - smem),
-        out_specs=[VMEM] * len(outs),
+        in_specs=specs or [SMEM] * smem + [VMEM] * (len(args) - smem),
+        out_specs=out_specs or [VMEM] * len(outs),
+        scratch_shapes=list(scratch),
         compiler_params=pltpu.CompilerParams(vmem_limit_bytes=24 * 1024 * 1024),
-        cost_estimate=pl.CostEstimate(flops=flops, bytes_accessed=nbytes, transcendentals=0),
+        cost_estimate=pl.CostEstimate(flops=flops, bytes_accessed=1_000_000, transcendentals=0),
         name=name,
     )(*args)
+
+
+def in_hbm(x):
+    return pltpu.with_memory_space_constraint(x, pltpu.HBM)
 
 
 PLANE = (NY, NZ)
@@ -132,13 +143,44 @@
     return by_z[:, :NZ], by_z[:, NZ : 2 * NZ], by_y[:NY], by_y[NY:], by_z[:, 2 * NZ :]
 
 
-def lateral(plane_z, plane_y, coefs):
-    return (
-        coefs[0] * plane_z[:, :NZ]
-        + coefs[1] * plane_z[:, NZ:]
-        + coefs[2] * plane_y[:NY]
-        + coefs[3] * plane_y[NY:]
-    )
+def along_z(u, mat_z):
+    high, low = parts_of(u, 2)
+    return jnp.dot(
+        jnp.concatenate([high, low], 1), mat_z[: 2 * NZ], preferred_element_type=jnp.float32
+    ) + jnp.dot(high, mat_z[2 * NZ :], preferred_element_type=jnp.float32)
+
+
+def y_patterns():
+    b = lax.broadcasted_iota(jnp.int32, (8, NZ), 0) % 4
+    own, before = {}, {}
+    for d in range(-4, 5):
+        total = jnp.zeros((8, NZ), FP)
+        for row in range(4):
+            if 0 <= row + d <= 4:
+                total = jnp.where(b == row, float(A[row, row + d]), total)
+        own[d] = total
+        if d <= 0:
+            before[d] = jnp.where(b == 0, float(A[4, 4 + d]), 0.0)
+    return own, before
+
+
+def y_coefs(y1, y2, patterns):
+    own, before = patterns
+    return {d: y1 * own[d] + y2 * before[d] if d in before else y1 * own[d] for d in own}
+
+
+def wrap_rows(pad, at, plane):
+    pad[at, 8 : 8 + NY, :] = plane
+    pad[at, 4:8, :] = plane[NY - 4 :]
+    pad[at, 8 + NY : 12 + NY, :] = plane[:4]
+
+
+def along_y(pad, at, row, coefs):
+    total = None
+    for d, c in coefs.items():
+        term = c * pad[at, 8 + row + d : 16 + row + d, :]
+        total = term if total is None else total + term
+    return total
 
 
 def to_right(sx, u):
@@ -148,64 +190,94 @@
     return sx * total
 
 
-def start_kernel(par, now, speed, left, right, coef_ref, first_ref, msg_ref):
+def start_kernel(
+    par, now_in, vel_in, src_in, speed_in, left_in, right_in, mat_in,
+    now, vel, src, speed, left, right, mat, coef_ref, first_ref, msg_ref, sems,
+):
+    pairs = (
+        (speed_in.at[0], speed), (left_in, left), (right_in, right), (now_in, now), (vel_in, vel),
+        (src_in, src), (mat_in, mat),
+    )
+    copies = [pltpu.make_async_copy(a, b, sems.at[i]) for i, (a, b) in enumerate(pairs)]
+    for copy in copies:
+        copy.start()
+    for copy in copies[:3]:
+        copy.wait()
     coefs = expand_speed(speed[...], left[...], right[...])
     for i in range(5):
         coef_ref[i] = coefs[i]
+    msg_ref[NY:] = jnp.zeros((EY, NZ), FP)
+    msg_ref[NY:, :EZ] = speed[...]
+    copies[3].wait()
     g = to_right(coefs[4], [now[k] for k in range(4)])
     first_ref[...] = g
     msg_ref[:NY] = jnp.where(par[0] == 1, now[0], g)
-    msg_ref[NY:] = speed[...]
-
-
-def base_first_kernel(wave, now, vel, src, coef, mat_z, mat_y, out):
-    base_body(0, wave, now, None, vel, src, coef, None, mat_z, mat_y, out)
-
-
-def base_body(step, wave, now, prev, vel, src, coef, coef0, mat_z, mat_y, out):
+    for copy in copies[4:]:
+        copy.wait()
+
+
+def base_first_kernel(wave, now, vel, src, coef, mat_z, out, pad):
+    base_body(0, wave, now, None, vel, src, coef, None, mat_z, out, pad)
+
+
+def base_body(step, wave, now, prev, vel, src, coef, coef0, mat_z, out, pad):
     scale = wave[step] * (STEP_DT * STEP_DT)
-    sx = coef[4]
+    by_z = along_z(now[...].reshape(4 * NY, NZ), mat_z)
+    patterns = y_patterns()
     for k in range(4):
-        u = now[k]
-        pz = dot(u, mat_z[...])
-        py = dot(mat_y[...], u)
-        if k == 0:
-            if coef0 is None:
-                force = 0.5 * lateral(pz, py, [coef[i] for i in range(4)])
+        wrap_rows(pad, k, now[k])
+    for row in range(0, NY, 8):
+        at = slice(row, row + 8)
+        u = [now[k, at, :] for k in range(4)]
+        sx = coef[4, at, :]
+        own = [coef[i, at, :] for i in range(4)]
+        first = own if coef0 is None else [coef0[i, at, :] for i in range(4)]
+        cy = y_coefs(own[2], own[3], patterns)
+        cy0 = cy if coef0 is None else y_coefs(first[2], first[3], patterns)
+        for k in range(4):
+            c = own if k else first
+            z = by_z[NY * k + row : NY * k + row + 8]
+            force = c[0] * z[:, :NZ] + c[1] * z[:, NZ:] + along_y(pad, k, row, cy if k else cy0)
+            if k == 0:
+                force = 0.5 * force if coef0 is None else force + coef0[4, at, :] * u[0]
+            mix = float(AB[k, 0]) * u[0]
+            for m in range(1, 4):
+                mix = mix + float(AB[k, m]) * u[m]
+            force = scale * src[k, at, :] - (force + sx * mix)
+            if prev is None:
+                out[k, at, :] = u[k] + STEP_DT * vel[k, at, :] + force
             else:
-                force = lateral(pz, py, [coef0[i] for i in range(4)]) + coef0[4] * u
-        else:
-            force = lateral(pz, py, [coef[i] for i in range(4)])
-        mix = float(AB[k, 0]) * now[0]
-        for m in range(1, 4):
-            mix = mix + float(AB[k, m]) * now[m]
-        force = force + sx * mix
-        if prev is None:
-            out[k] = u + STEP_DT * vel[k] + (scale * src[k] - force)
-        else:
-            out[k] = 2.0 * u - prev[k] + (scale * src[k] - force)
-
-
-def base_kernel(step, wave, now, prev, src, coef, coef0, mat_z, mat_y, out):
-    base_body(step, wave, now, prev, None, src, coef, coef0, mat_z, mat_y, out)
-
-
-def half_left(plane, coefs, mat_z, mat_y):
-    pz = dot(plane, mat_z)
-    py = dot(mat_y, plane)
-    return 0.5 * lateral(pz, py, coefs) + float(AB[4, 4]) * (coefs[4] * plane)
+                out[k, at, :] = 2.0 * u[k] - prev[k, at, :] + force
+
+
+def base_kernel(step, wave, now, prev, src, coef, coef0, mat_z, out, pad):
+    base_body(step, wave, now, prev, None, src, coef, coef0, mat_z, out, pad)
+
+
+def half_left(plane, coefs, mat_z, pad):
+    by_z = along_z(plane, mat_z)
+    wrap_rows(pad, 0, plane)
+    patterns = y_patterns()
+    tiles = []
+    for row in range(0, NY, 8):
+        c = [x[row : row + 8] for x in coefs]
+        by_y = along_y(pad, 0, row, y_coefs(c[2], c[3], patterns))
+        z = by_z[row : row + 8]
+        tiles.append(0.5 * (c[0] * z[:, :NZ] + c[1] * z[:, NZ:] + by_y))
+    return jnp.concatenate(tiles, 0) + float(AB[4, 4]) * (coefs[4] * plane)
 
 
 def inner_first_kernel(
-    par, base, now, first, recv, speed, coef, left, right, mat_z, mat_y, tent_ref, msg_ref, cleft_ref
+    par, base, now, first, recv, speed, coef, left, right, mat_z, tent_ref, msg_ref, cleft_ref, pad
 ):
     odd = par[0] == 1
-    coefs = expand_speed(jnp.where(odd, recv[NY:], 0.0), left[...], right[...])
+    coefs = expand_speed(jnp.where(odd, recv[NY:, :EZ], 0.0), left[...], right[...])
     for i in range(5):
         cleft_ref[i] = coefs[i]
-    share = half_left(now[0], coefs, mat_z[...], mat_y[...])
+    share = half_left(now[0], coefs, mat_z, pad)
     inner_finish(odd, base, now, first[...], recv[:NY], coef[4], share, tent_ref, msg_ref)
-    msg_ref[2 * NY :] = speed[...]
+    msg_ref[2 * NY :] = jnp.zeros((EY, NZ), FP)
+    msg_ref[2 * NY :, :EZ] = speed[...]
 
 
 def inner_finish(odd, base, now, g_now, inner, sx, share, tent_ref, msg_ref):
@@ -245,15 +317,15 @@
 
 
 def outer_first_kernel(
-    par, tent, now, first, recv, inner, coef, cleft, left, right, mat_z, mat_y,
-    u_ref, msg_ref, outer_ref, coef0_ref, sxl_ref, last_ref,
+    par, tent, now, first, recv, inner, coef, cleft, left, right, mat_z,
+    u_ref, msg_ref, outer_ref, coef0_ref, sxl_ref, last_ref, pad,
 ):
     odd = par[0] == 1
-    theirs = expand_speed(recv[2 * NY :], left[...], right[...])
+    theirs = expand_speed(recv[2 * NY :, :EZ], left[...], right[...])
     coefs = [jnp.where(odd, coef[i], theirs[i]) for i in range(5)]
     recv0 = recv[:NY]
     plane = jnp.where(odd, recv0, now[0])
-    share = half_left(plane, coefs, mat_z[...], mat_y[...])
+    share = half_left(plane, coefs, mat_z, pad)
     on_left = [jnp.where(odd, cleft[i], theirs[i]) for i in range(5)]
     for i in range(4):
         coef0_ref[i] = 0.5 * (coef[i] + on_left[i])
@@ -293,6 +365,14 @@
     g_ref[...] = g
     msg_ref[...] = jnp.where(odd, values[0], g)
     last_ref[...] = last
+
+
+def last_kernel(par, base, inner, outer, coef, u_ref):
+    odd = par[0] == 1
+    pull = coef[4] * jnp.where(odd, outer[...], inner[...])
+    for k in range(4):
+        u_ref[k] = base[k] - float(AB[k, 4]) * pull
+    u_ref[0] = u_ref[0] - jnp.where(odd, inner[...], outer[...])
 
 
 def slots_kernel(elem, weight, pick_ref, spread_ref):
@@ -339,8 +419,12 @@
     out[1:2, :] = sample(u1, l1, pick, spread)
 
 
-def sample_one_kernel(u0, l0, pick, spread, out):
-    out[...] = sample(u0, l0, pick, spread)
+def sample_last_kernel(par, inner, outer, u0, l0, u1, pick, spread, r0, r1, out, last):
+    last[...] = jnp.where(par[0] == 1, outer[...], inner[...])
+    rows = [r0[...], r1[...], sample(u0, l0, pick, spread), sample(u1, last, pick, spread)]
+    rows = jnp.concatenate(rows + [jnp.zeros((2, CAP), FP)], 0)
+    for i in range(out.shape[0]):
+        out[i] = rows
 
 
 def stations_kernel(blocks, stations, row_ref, lane_ref):
@@ -361,27 +445,47 @@
     row_ref[...] = jnp.where(jnp.abs(at - wanted.astype(FP)) < 0.5, 1.0, 0.0)
 
 
-def cross_kernel(gathered, row, lane, table, spread_a, spread_b, out):
-    t_of = lax.broadcasted_iota(jnp.int32, (2 * SB, 128), 1)
+def cross_kernel(gathered, row, lane, table, spread_a, spread_b, out, held, sems):
+    slabs = [gathered[pl.ds(t, 128, stride=8), :] for t in range(NT)]
+    hot = row[...].astype(jnp.bfloat16)
+    found = jnp.dot(
+        jnp.concatenate([hot, hot], 1),
+        jnp.concatenate(parts_of(jnp.concatenate(slabs, 1), 2), 0),
+        preferred_element_type=jnp.float32,
+    )
+    at = lax.broadcasted_iota(jnp.int32, (2 * SB, 128), 1)
     samples = jnp.zeros((2 * SB, 128), FP)
     for t in range(NT):
-        slab = gathered[pl.ds(t, 128, stride=8), :]
-        found = dot(row[...], slab) * lane[...]
-        samples = jnp.where(t_of == t, jnp.sum(found, 1, keepdims=True), samples)
+        one = jnp.sum(found[:, 128 * t : 128 * (t + 1)] * lane[...], 1, keepdims=True)
+        samples = jnp.where(at % 8 == t, one, samples)
+    parts = [part.astype(FP) for part in parts_of(samples, 3)]
+    mixed = jnp.zeros((2 * SB, 128), FP)
+    for group, (part, _) in enumerate(PART_PAIRS):
+        mixed = jnp.where(at // 8 == group, parts[part], mixed)
     spectra = lax.dot_general(
-        table[...], samples, (((1,), (1,)), ((), ())), precision=HIGHEST,
+        table[...], mixed.astype(jnp.bfloat16), (((1,), (1,)), ((), ())),
         preferred_element_type=jnp.float32,
     ).astype(jnp.bfloat16)
     second = jnp.dot(spectra, spread_b[...], preferred_element_type=jnp.float32) * (1.0 / NT)
     b_re = second[:F]
     b_im = second[F:]
-    for i in range(8):
-        cols = slice(128 * i, 128 * (i + 1))
-        first = jnp.dot(spectra, spread_a[:, cols], preferred_element_type=jnp.float32)
-        a_re = first[:F]
-        a_im = first[F:]
-        out[0, 0, :, cols] = (a_re * b_re + a_im * b_im).astype(jnp.bfloat16)
-        out[0, 1, :, cols] = (a_im * b_re - a_re * b_im).astype(jnp.bfloat16)
+    copies = []
+    for i in range(4):
+        first = jnp.dot(
+            spectra, spread_a[:, 256 * i : 256 * (i + 1)], preferred_element_type=jnp.float32
+        )
+        for half in range(2):
+            cols = slice(256 * i + 128 * half, 256 * i + 128 * (half + 1))
+            a_re = first[:F, 128 * half : 128 * (half + 1)]
+            a_im = first[F:, 128 * half : 128 * (half + 1)]
+            held[0, :, cols] = (a_re * b_re + a_im * b_im).astype(jnp.bfloat16)
+            held[1, :, cols] = (a_im * b_re - a_re * b_im).astype(jnp.bfloat16)
+        cols = slice(256 * i, 256 * (i + 1))
+        copy = pltpu.make_async_copy(held.at[:, :, cols], out.at[0, :, :, cols], sems.at[i])
+        copy.start()
+        copies.append(copy)
+    for copy in copies:
+        copy.wait()
 
 
 def body(
@@ -396,7 +500,7 @@
     def swap_outer(x):
         return lax.ppermute(x, AXES, outer_route)
 
-    mat_z, mat_y, left, right = (jnp.asarray(x) for x in tables())
+    mat_z, left, right = (jnp.asarray(x) for x in tables())
     table = jnp.asarray(dft_table())
     reps = np.zeros((2 * SB, SB * SB))
     for i in range(SB):
@@ -406,21 +510,26 @@
         tiles[SB + i % SB, i] = 1.0
     reps = jnp.asarray(reps, jnp.bfloat16)
     tiles = jnp.asarray(tiles, jnp.bfloat16)
+    pads = (pltpu.VMEM((4, NY + 16, NZ), FP),)
+    one_pad = (pltpu.VMEM((1, NY + 16, NZ), FP),)
 
     par = (lax.axis_index("bulk") % 2).astype(jnp.int32).reshape(1)
-    speed = jnp.pad(speed_sq[0], ((0, 0), (0, 128 - EZ)))
-
-    coef, g0, msg = call(
-        start_kernel, [(FIVE, FP), (PLANE, FP), ((NY + EY, NZ), FP)], (par, now, speed, left, right),
-        "start", 1,
+
+    now, vel, src, speed, left, right, mat_z, coef, g0, msg = call(
+        start_kernel,
+        [(FOUR, FP)] * 3
+        + [((EY, EZ), FP), (left.shape, FP), (right.shape, FP), (mat_z.shape, jnp.bfloat16)]
+        + [(FIVE, FP), (PLANE, FP), ((NY + EY, NZ), FP)],
+        (par, *(in_hbm(x) for x in (now, vel, src, speed_sq, left, right, mat_z))), "start",
+        specs=[SMEM] + [HBM] * 7, scratch=(pltpu.SemaphoreType.DMA((7,)),),
     )
     inner0 = swap_inner(msg)
     (base,) = call(
-        base_first_kernel, [(FOUR, FP)], (wavelet, now, vel, src, coef, mat_z, mat_y), "base0", 1
+        base_first_kernel, [(FOUR, FP)], (wavelet, now, vel, src, coef, mat_z), "base0", 1, scratch=pads
     )
     tent, msg, cleft = call(
         inner_first_kernel, [(FOUR, FP), ((2 * NY + EY, NZ), FP), (FIVE, FP)],
-        (par, base, now, g0, inner0, speed, coef, left, right, mat_z, mat_y), "inner0", 1,
+        (par, base, now, g0, inner0, speed, coef, left, right, mat_z), "inner0", 1, scratch=one_pad,
     )
     outer0 = swap_outer(msg)
     pick, spread = call(
@@ -431,11 +540,13 @@
         stations_kernel, [((2 * SB, 128), FP), ((2 * SB, CAP), FP)],
         (pair_blocks, slot_station.reshape(128, CAP)), "stations", 1,
     )
+    outer0, pick, spread, row, lane = lax.optimization_barrier((outer0, pick, spread, row, lane))
     u_a = now
     u_b, msg, outer, coef0, sxl, last_a = call(
         outer_first_kernel,
         [(FOUR, FP), (PLANE, FP), (PLANE, FP), (FIVE, FP), (PLANE, FP), (PLANE, FP)],
-        (par, tent, now, g0, outer0, inner0, coef, cleft, left, right, mat_z, mat_y), "outer0", 1,
+        (par, tent, now, g0, outer0, inner0, coef, cleft, left, right, mat_z), "outer0", 1,
+        scratch=one_pad,
     )
     rows = []
     step = 1
@@ -443,18 +554,18 @@
         inner = swap_inner(msg)
         (base,) = call(
             functools.partial(base_kernel, step), [(FOUR, FP)],
-            (wavelet, u_b, u_a, src, coef, coef0, mat_z, mat_y), "base", 1,
-        )
+            (wavelet, u_b, u_a, src, coef, coef0, mat_z), "base", 1, scratch=pads,
+        )
+        if step == NT - 1:
+            break
         u_c, g_c, msg, last_b = call(
             both_kernel, [(FOUR, FP), (PLANE, FP), (PLANE, FP), (PLANE, FP)],
             (par, base, inner, outer, coef), "both", 1,
         )
-        if step == NT - 1:
-            break
         inner = swap_inner(msg)
         (base,) = call(
             functools.partial(base_kernel, step + 1), [(FOUR, FP)],
-            (wavelet, u_c, u_b, src, coef, coef0, mat_z, mat_y), "base", 1,
+            (wavelet, u_c, u_b, src, coef, coef0, mat_z), "base", 1, scratch=pads,
         )
         tent, msg = call(
             inner_kernel, [(FOUR, FP), ((2 * NY, NZ), FP)],
@@ -464,6 +575,7 @@
         (two,) = call(
             sample_two_kernel, [((2, CAP), FP)], (u_a, last_a, u_b, last_b, pick, spread), "sample2"
         )
+        recv, two = lax.optimization_barrier((recv, two))
         rows.append(two)
         u_a = u_c
         u_b, msg, outer, last_a = call(
@@ -471,19 +583,20 @@
             (par, tent, u_c, g_c, recv, inner, coef, sxl), "outer", 1,
         )
         step += 2
-    (one,) = call(sample_one_kernel, [((1, CAP), FP)], (u_a, last_a, pick, spread), "sample")
-    rows.append(one)
-    (one,) = call(sample_one_kernel, [((1, CAP), FP)], (u_b, last_b, pick, spread), "sample")
-    rows.append(one)
-    mine = jnp.pad(jnp.concatenate(rows, 0), ((0, 2), (0, 0)))
-    gathered = lax.all_to_all(
-        jnp.broadcast_to(mine[None], (devices, 8, CAP)), AXES, 0, 0, tiled=True
-    )
+    (mine,) = call(
+        sample_last_kernel, [((devices, 8, CAP), FP)],
+        (par, inner, outer, u_a, last_a, u_b, pick, spread, *rows), "sample3", 1,
+        scratch=(pltpu.VMEM(PLANE, FP),),
+    )
+    gathered = lax.all_to_all(mine, AXES, 0, 0, tiled=True)
+    (end,) = call(last_kernel, [(FOUR, FP)], (par, base, inner, outer, coef), "last", 1)
     (cross,) = call(
         cross_kernel, [((1, 2, F, SB * SB), jnp.bfloat16)],
         (gathered.reshape(8 * devices, CAP), row, lane, table, reps, tiles), "cross",
-    )
-    return u_c, cross
+        out_specs=[HBM],
+        scratch=(pltpu.VMEM((2, F, SB * SB), jnp.bfloat16), pltpu.SemaphoreType.DMA((4,))),
+    )
+    return end, cross
 
 
 def solution(mesh):

time: 82.9 us -> 69.9 us (0.84)
  local copies, waits for them, and re-layouts: 8.72 us -> 0.7 us
  waiting for transfers between devices: 23.2 us -> 20.5 us
  Pallas kernels: 18.5 us -> 16.8 us
    unnamed x42 -> x18, local copies, waits for them, and re-layouts: 7.14 us -> 0.7 us
    ppermute x3, waiting for transfers between devices: 10.9 us -> 7.8 us  [swap_outer(): return lax.ppermute(x, AXES, outer_route)]
    pallas_call x23 -> x22, Pallas kernels: 18.5 us -> 16.8 us  [call(): pl.pallas_call(kernel, out_shape=[jax.ShapeDtypeStruct(s, d) for s, d in...]
    ppermute x6, waiting for transfers between devices: 0.02 us -> 0.96 us  [swap_inner(): return lax.ppermute(x, AXES, inner_route)]
  transfers between devices with their start and end apart: 10 -> 10, of which waited for: 4 -> 6; matrix products, arithmetic and copies ran while one was open for 0% -> 0% of each run, Pallas kernels for 15% -> 14%
where the time goes in v1:
time: 69.9 us; the launch traced here: 69.7 us
  starting transfers between devices  30.8 us (44%)
  waiting for transfers between devices  20.5 us (29%)
  Pallas kernels  16.8 us (24%)
  between operations  0.86 us (1%)
  local copies, waits for them, and re-layouts  0.7 us (1%)
    ppermute x6, starting transfers between devices, swap_inner(): return lax.ppermute(x, AXES, inner_route)  20.9 us
    pallas_call x22, Pallas kernels, call(): pl.pallas_call(kernel, out_shape=[jax.ShapeDtypeStruct(s, d) for s, d in...  16.8 us
    all_to_all x1, waiting for transfers between devices, body(): gathered = lax.all_to_all(mine, AXES, 0, 0, tiled=True)  11.8 us
    all_to_all x1, starting transfers between devices, body(): gathered = lax.all_to_all(mine, AXES, 0, 0, tiled=True)  8.43 us
    ppermute x3, waiting for transfers between devices, swap_outer(): return lax.ppermute(x, AXES, outer_route)  7.8 us
    ppermute x3, starting transfers between devices, swap_outer(): return lax.ppermute(x, AXES, outer_route)  1.53 us
  transfers between devices with their start and end apart: 10, of which 6 were waited for; matrix products, arithmetic and copies ran while one was open for 0% of the time, Pallas kernels for 14%

profile of v1, /device:TPU:1, one launch (start us, length us, event | category | flops | bytes accessed | tf_op | source)
XLA Modules:
  0.0 69.7 jit_solution(62076665886707487)
XLA Ops:
  0.7 1.6 %start.1 = (f32[4,96,128]{2,1,0:T(8,128)S(1)}, f32[4,96,128]{2,1,0:T(8,128)S(1)}, f32[4,96,128]{2,1,0:T(8,128)S(1)}, f32[24,32]{1,0:T(8,128)S(1)}, f32[288,24]{1...) custom-call(s32[1]{0:T(128)} %bitcast.par, ...), custom_call_target="tpu_custom_call" | custom-call | flops 4000000 | bytes 1000000 | tf_op jit(solution)/shard_map/start/pallas_call | solution.py:117
  2.3 1.5 %collective-permute-start = (f32[120,128]{1,0:T(8,128)S(1)}, f32[120,128]{1,0:T(8,128)S(1)}, u32[]{:S(2)}, u32[]{:S(2)}) collective-permute-start(f32[120,128]{1,0:T(8,128)S(1)} %get-tuple-element.60), channel_id=1, source_target_pairs={{0,1},{1,0},{2,3},{3,2},{4,5},{5,4},{6,7},{7,6},{8,9},{9,8},{10,11... | collective-permute-start | bytes 184328 | tf_op jit(solution)/shard_map/ppermute | solution.py:498
  4.5 1.0 %base0.1.base = f32[4,96,128]{2,1,0:T(8,128)S(1)} custom-call(f32[6]{0:T(128)S(1)} %copy-done.4, f32[4,96,128]{2,1,0:T(8,128)S(1)} %get-tuple-element.54.now.prev.u0, f32[4,96,128]{2,1,0:T(8,128)S(1)} %get-tuple-element.55.vel, f32[4,96,128]{2,1,0:T(8,128)S(1)} %get-tuple-element.56.src, f32[5,96,128]{2,1,0:T(8,128)S(1)} %get-tuple-element.57.coef, ...), custom_call_target="tpu_custom_call" | custom-call | flops 4000000 | bytes 1000000 | tf_op jit(solution)/shard_map/base0/pallas_call | solution.py:117
  5.5 0.7 %inner0.1 = (f32[4,96,128]{2,1,0:T(8,128)S(1)}, f32[216,128]{1,0:T(8,128)S(1)}, f32[5,96,128]{2,1,0:T(8,128)S(1)}) custom-call(s32[1]{0:T(128)} %bitcast.par, f32[4,96,128]{2,1,0:T(8,128)S(1)} %base0.1.base, f32[4,96,128]{2,1,0:T(8,128)S(1)} %get-tuple-element.54.now.prev.u0, f32[96,128]{1,0:T(8,128)S(1)} %get-tuple-element.59.first, ...), custom_call_target="tpu_custom_call" | custom-call | flops 4000000 | bytes 1000000 | tf_op jit(solution)/shard_map/inner0/pallas_call | solution.py:117
  6.2 1.4 %collective-permute-start.1 = (f32[216,128]{1,0:T(8,128)S(1)}, f32[216,128]{1,0:T(8,128)S(1)}, u32[]{:S(2)}, u32[]{:S(2)}) collective-permute-start(f32[216,128]{1,0:T(8,128)S(1)} %get-tuple-element.65), channel_id=1, source_target_pairs={{0,127},{1,2},{2,1},{3,4},{4,3},{5,6},{6,5},{7,8},{8,7},{9,10},{10... | collective-permute-start | bytes 331784 | tf_op jit(solution)/shard_map/ppermute | solution.py:501
  7.6 1.2 %stations.1 = (f32[64,128]{1,0:T(8,128)S(1)}, f32[64,128]{1,0:T(8,128)S(1)}) custom-call(s32[1,2]{1,0:T(1,128)S(1)} %copy-done.7, s32[128,128]{1,0:T(8,128)S(1)} %bitcast.5), custom_call_target="tpu_custom_call" | custom-call | flops 4000000 | bytes 1000000 | tf_op jit(solution)/shard_map/stations/pallas_call | solution.py:117
  9.3 1.2 %collective-permute-done.1.recv = f32[216,128]{1,0:T(8,128)S(1)} collective-permute-done((f32[216,128]{1,0:T(8,128)S(1)}, f32[216,128]{1,0:T(8,128)S(1)}, u32[]{:S(2)}, u32[]{:S(2)}) %collective-permute-start.1) | collective-permute-done | bytes 110624 | tf_op jit(solution)/shard_map/ppermute | solution.py:501
  10.5 0.7 %outer0.1 = (f32[4,96,128]{2,1,0:T(8,128)S(1)}, f32[96,128]{1,0:T(8,128)S(1)}, f32[96,128]{1,0:T(8,128)S(1)}, f32[5,96,128]{2,1,0:T(8,128)S(1)}, f32[96,128]{1,0:T(8,128)S(1)}, /*index=5*/f32[96,128]{1,0:T(8,128)S(1)}) custom-call(s32[1]{0:T(128)} %bitcast.par, f32[4,96,128]{2,1,0:T(8,128)S(1)} %get-tuple-element.64.tent, ...), custom_call_target="tpu_custom_call" | custom-call | flops 4000000 | bytes 1000000 | tf_op jit(solution)/shard_map/outer0/pallas_call | solution.py:117
  11.2 7.2 %collective-permute-start.2 = (f32[96,128]{1,0:T(8,128)S(1)}, f32[96,128]{1,0:T(8,128)S(1)}, u32[]{:S(2)}, u32[]{:S(2)}) collective-permute-start(f32[96,128]{1,0:T(8,128)S(1)} %get-tuple-element.74), channel_id=1, source_target_pairs={{0,1},{1,0},{2,3},{3,2},{4,5},{5,4},{6,7},{7,6},{8,9},{9,8},{10,11... | collective-permute-start | bytes 147464 | tf_op jit(solution)/shard_map/ppermute | solution.py:498
  18.5 1.0 %base.5 = f32[4,96,128]{2,1,0:T(8,128)S(1)} custom-call(f32[6]{0:T(128)S(1)} %copy-done.5, f32[4,96,128]{2,1,0:T(8,128)S(1)} %get-tuple-element.72.now.prev.u1, f32[4,96,128]{2,1,0:T(8,128)S(1)} %get-tuple-element.54.now.prev.u0, f32[4,96,128]{2,1,0:T(8,128)S(1)} %get-tuple-element.56.src, f32[5,96,128]{2,1,0:T(8,128)S(1)} %get-tuple-element.57.coef, ...), custom_call_target="tpu_custom_call" | custom-call | flops 4000000 | bytes 1000000 | tf_op jit(solution)/shard_map/base/pallas_call | solution.py:117
  19.8 1.0 %base.6 = f32[4,96,128]{2,1,0:T(8,128)S(1)} custom-call(f32[6]{0:T(128)S(1)} %copy-done.5, f32[4,96,128]{2,1,0:T(8,128)S(1)} %get-tuple-element.76.now.prev.u0, f32[4,96,128]{2,1,0:T(8,128)S(1)} %get-tuple-element.72.now.prev.u1, f32[4,96,128]{2,1,0:T(8,128)S(1)} %get-tuple-element.56.src, f32[5,96,128]{2,1,0:T(8,128)S(1)} %get-tuple-element.57.coef, ...), custom_call_target="tpu_custom_call" | custom-call | flops 4000000 | bytes 1000000 | tf_op jit(solution)/shard_map/base/pallas_call | solution.py:117
  21.7 3.3 %collective-permute-done.4.recv = f32[192,128]{1,0:T(8,128)S(1)} collective-permute-done((f32[192,128]{1,0:T(8,128)S(1)}, f32[192,128]{1,0:T(8,128)S(1)}, u32[]{:S(2)}, u32[]{:S(2)}) %collective-permute-start.4) | collective-permute-done | bytes 98336 | tf_op jit(solution)/shard_map/ppermute | solution.py:501
  25.1 5.8 %collective-permute-start.5 = (f32[96,128]{1,0:T(8,128)S(1)}, f32[96,128]{1,0:T(8,128)S(1)}, u32[]{:S(2)}, u32[]{:S(2)}) collective-permute-start(f32[96,128]{1,0:T(8,128)S(1)} %get-tuple-element.88), channel_id=1, source_target_pairs={{0,1},{1,0},{2,3},{3,2},{4,5},{5,4},{6,7},{7,6},{8,9},{9,8},{10,11... | collective-permute-start | bytes 147464 | tf_op jit(solution)/shard_map/ppermute | solution.py:498
  30.9 1.0 %base.7 = f32[4,96,128]{2,1,0:T(8,128)S(1)} custom-call(f32[6]{0:T(128)S(1)} %copy-done.5, f32[4,96,128]{2,1,0:T(8,128)S(1)} %get-tuple-element.87.now.prev.u1, f32[4,96,128]{2,1,0:T(8,128)S(1)} %get-tuple-element.76.now.prev.u0, f32[4,96,128]{2,1,0:T(8,128)S(1)} %get-tuple-element.56.src, f32[5,96,128]{2,1,0:T(8,128)S(1)} %get-tuple-element.57.coef, ...), custom_call_target="tpu_custom_call" | custom-call | flops 4000000 | bytes 1000000 | tf_op jit(solution)/shard_map/base/pallas_call | solution.py:117
  32.3 1.0 %base.8 = f32[4,96,128]{2,1,0:T(8,128)S(1)} custom-call(f32[6]{0:T(128)S(1)} %copy-done.5, f32[4,96,128]{2,1,0:T(8,128)S(1)} %get-tuple-element.90.now.prev.u0, f32[4,96,128]{2,1,0:T(8,128)S(1)} %get-tuple-element.87.now.prev.u1, f32[4,96,128]{2,1,0:T(8,128)S(1)} %get-tuple-element.56.src, f32[5,96,128]{2,1,0:T(8,128)S(1)} %get-tuple-element.57.coef, ...), custom_call_target="tpu_custom_call" | custom-call | flops 4000000 | bytes 1000000 | tf_op jit(solution)/shard_map/base/pallas_call | solution.py:117
  33.4 0.7 %sample2.3.r1 = f32[2,128]{1,0:T(2,128)S(1)} custom-call(f32[4,96,128]{2,1,0:T(8,128)S(1)} %get-tuple-element.76.now.prev.u0, f32[96,128]{1,0:T(8,128)S(1)} %get-tuple-element.95.l0, f32[4,96,128]{2,1,0:T(8,128)S(1)} %get-tuple-element.87.now.prev.u1, f32[96,128]{1,0:T(8,128)S(1)} %get-tuple-element.96.l1, bf16[256,640]{1,0:T(8,128)(2,1)S(1)} %get-tuple-element.83.pick, ...), custom_call_target="tpu_custom_call" | custom-call | flops 4000000 | bytes 1000000 | tf_op jit(solution)/shard_map/sample2/pallas_call | solution.py:117
  34.2 3.3 %collective-permute-done.7.recv = f32[192,128]{1,0:T(8,128)S(1)} collective-permute-done((f32[192,128]{1,0:T(8,128)S(1)}, f32[192,128]{1,0:T(8,128)S(1)}, u32[]{:S(2)}, u32[]{:S(2)}) %collective-permute-start.7) | collective-permute-done | bytes 98336 | tf_op jit(solution)/shard_map/ppermute | solution.py:501
  37.5 5.8 %collective-permute-start.8 = (f32[96,128]{1,0:T(8,128)S(1)}, f32[96,128]{1,0:T(8,128)S(1)}, u32[]{:S(2)}, u32[]{:S(2)}) collective-permute-start(f32[96,128]{1,0:T(8,128)S(1)} %get-tuple-element.99), channel_id=1, source_target_pairs={{0,1},{1,0},{2,3},{3,2},{4,5},{5,4},{6,7},{7,6},{8,9},{9,8},{10,11... | collective-permute-start | bytes 147464 | tf_op jit(solution)/shard_map/ppermute | solution.py:498
  43.3 0.9 %collective-permute-done.8.inner = f32[96,128]{1,0:T(8,128)S(1)} collective-permute-done((f32[96,128]{1,0:T(8,128)S(1)}, f32[96,128]{1,0:T(8,128)S(1)}, u32[]{:S(2)}, u32[]{:S(2)}) %collective-permute-start.8) | collective-permute-done | bytes 49184 | tf_op jit(solution)/shard_map/ppermute | solution.py:498
  44.2 1.5 %sample3.1 = f32[128,8,128]{2,1,0:T(8,128)} custom-call(s32[1]{0:T(128)} %bitcast.par, f32[96,128]{1,0:T(8,128)S(1)} %collective-permute-done.8.inner, f32[96,128]{1,0:T(8,128)S(1)} %get-tuple-element.100.outer, f32[4,96,128]{2,1,0:T(8,128)S(1)} %get-tuple-element.90.now.prev.u0, f32[96,128]{1,0:T(8,128)S(1)} %get-tuple-element.101.l0, ...), custom_call_target="tpu_custom_call" | custom-call | flops 4000000 | bytes 1000000 | tf_op jit(solution)/shard_map/sample3/pallas_call | solution.py:117
  45.7 8.4 %all-to-all-start = ((f32[128,8,128]{2,1,0:T(8,128)}), f32[128,8,128]{2,1,0:T(8,128)S(1)}, u32[]{:S(2)}, u32[]{:S(2)}) async-start(f32[128,8,128]{2,1,0:T(8,128)} %sample3.1), calls=%async_computation | async-start | bytes 1048576 | tf_op jit(solution)/shard_map/all_to_all | solution.py:591
  54.2 1.0 %base.9 = f32[4,96,128]{2,1,0:T(8,128)S(1)} custom-call(f32[6]{0:T(128)S(1)} %copy-done.5, f32[4,96,128]{2,1,0:T(8,128)S(1)} %get-tuple-element.98.now.u1, f32[4,96,128]{2,1,0:T(8,128)S(1)} %get-tuple-element.90.now.prev.u0, f32[4,96,128]{2,1,0:T(8,128)S(1)} %get-tuple-element.56.src, f32[5,96,128]{2,1,0:T(8,128)S(1)} %get-tuple-element.57.coef, ...), custom_call_target="tpu_custom_call" | custom-call | flops 4000000 | bytes 1000000 | tf_op jit(solution)/shard_map/base/pallas_call | solution.py:117
  55.9 11.8 %all-to-all-done = f32[128,8,128]{2,1,0:T(8,128)S(1)} async-done(((f32[128,8,128]{2,1,0:T(8,128)}), f32[128,8,128]{2,1,0:T(8,128)S(1)}, u32[]{:S(2)}, u32[]{:S(2)}) %all-to-all-start) | async-done | bytes 524320 | tf_op jit(solution)/shard_map/all_to_all | solution.py:591
  67.7 2.0 %cross.1 = bf16[1,2,256,1024]{3,2,1,0:T(8,128)(2,1)} custom-call(f32[1024,128]{1,0:T(8,128)S(1)} %bitcast.4, f32[64,128]{1,0:T(8,128)S(1)} %get-tuple-element.104.row, f32[64,128]{1,0:T(8,128)S(1)} %get-tuple-element.105.lane, bf16[512,128]{1,0:T(8,128)(2,1)S(1)} %copy-done.1, bf16[64,1024]{1,0:T(8,128)(2,1)S(1)} %copy-done, bf16[64,128]{1,0:T(8,128)(2,1)S(1)} %copy-done.6), custom_call_target="tpu_custom_call" | custom-call | flops 4000000 | bytes 1000000 | tf_op jit(solution)/shard_map/cross/pallas_call | solution.py:117
  (36 shorter events, 3.7 us)
Async XLA Ops:
  0.6 7.0 %copy-start.7 = (s32[1,2]{1,0:T(1,128)S(1)}, s32[1,2]{1,0:T(1,128)}, u32[]{:S(2)}) copy-start(s32[1,2]{1,0:T(1,128)} %blocks.1) | copy-start | bytes 28
  2.3 5.3 %copy-start.2 = (s32[16384]{0:T(1024)S(1)}, s32[16384]{0:T(1024)}, u32[]{:S(2)}) copy-start(s32[16384]{0:T(1024)} %param.21) | copy-start | bytes 196612
  2.3 3.2 %collective-permute-start = (f32[120,128]{1,0:T(8,128)S(1)}, f32[120,128]{1,0:T(8,128)S(1)}, u32[]{:S(2)}, u32[]{:S(2)}) collective-permute-start(f32[120,128]{1,0:T(8,128)S(1)} %get-tuple-element.60), channel_id=1, source_target_pairs={{0,1},{1,0},{2,3},{3,2},{4,5},{5,4},{6,7},{7,6},{8,9},{9,8},{10,11... | collective-permute-start | bytes 184328 | tf_op jit(solution)/shard_map/ppermute | solution.py:498
  3.8 0.7 copy-start.4
  4.5 4.4 %copy-start.3 = (f32[125,128]{1,0:T(8,128)S(1)}, f32[125,128]{1,0:T(8,128)}, u32[]{:S(2)}) copy-start(f32[125,128]{1,0:T(8,128)} %weight.1) | copy-start | bytes 192004
  4.5 4.4 %copy-start.8 = (s32[128]{0:T(128)S(1)}, s32[128]{0:T(128)}, u32[]{:S(2)}) copy-start(s32[128]{0:T(128)} %param.20) | copy-start | bytes 1540
  5.5 13.0 %copy-start.5 = (f32[6]{0:T(128)S(1)}, f32[6]{0:T(128)}, u32[]{:S(2)}) copy-start(f32[6]{0:T(128)} %wave.11) | copy-start | bytes 76
  6.2 4.3 %collective-permute-start.1 = (f32[216,128]{1,0:T(8,128)S(1)}, f32[216,128]{1,0:T(8,128)S(1)}, u32[]{:S(2)}, u32[]{:S(2)}) collective-permute-start(f32[216,128]{1,0:T(8,128)S(1)} %get-tuple-element.65), channel_id=1, source_target_pairs={{0,127},{1,2},{2,1},{3,4},{4,3},{5,6},{6,5},{7,8},{8,7},{9,10},{10... | collective-permute-start | bytes 331784 | tf_op jit(solution)/shard_map/ppermute | solution.py:501
  11.2 8.2 %collective-permute-start.2 = (f32[96,128]{1,0:T(8,128)S(1)}, f32[96,128]{1,0:T(8,128)S(1)}, u32[]{:S(2)}, u32[]{:S(2)}) collective-permute-start(f32[96,128]{1,0:T(8,128)S(1)} %get-tuple-element.74), channel_id=1, source_target_pairs={{0,1},{1,0},{2,3},{3,2},{4,5},{5,4},{6,7},{7,6},{8,9},{9,8},{10,11... | collective-permute-start | bytes 147464 | tf_op jit(solution)/shard_map/ppermute | solution.py:498
  19.5 1.3 %collective-permute-start.3 = (f32[96,128]{1,0:T(8,128)S(1)}, f32[96,128]{1,0:T(8,128)S(1)}, u32[]{:S(2)}, u32[]{:S(2)}) collective-permute-start(f32[96,128]{1,0:T(8,128)S(1)} %get-tuple-element.78), channel_id=1, source_target_pairs={{0,1},{1,0},{2,3},{3,2},{4,5},{5,4},{6,7},{7,6},{8,9},{9,8},{10,11... | collective-permute-start | bytes 147464 | tf_op jit(solution)/shard_map/ppermute | solution.py:498
  20.9 4.1 %collective-permute-start.4 = (f32[192,128]{1,0:T(8,128)S(1)}, f32[192,128]{1,0:T(8,128)S(1)}, u32[]{:S(2)}, u32[]{:S(2)}) collective-permute-start(f32[192,128]{1,0:T(8,128)S(1)} %get-tuple-element.80), channel_id=1, source_target_pairs={{0,127},{1,2},{2,1},{3,4},{4,3},{5,6},{6,5},{7,8},{8,7},{9,10},{10... | collective-permute-start | bytes 294920 | tf_op jit(solution)/shard_map/ppermute | solution.py:501
  25.1 6.9 %collective-permute-start.5 = (f32[96,128]{1,0:T(8,128)S(1)}, f32[96,128]{1,0:T(8,128)S(1)}, u32[]{:S(2)}, u32[]{:S(2)}) collective-permute-start(f32[96,128]{1,0:T(8,128)S(1)} %get-tuple-element.88), channel_id=1, source_target_pairs={{0,1},{1,0},{2,3},{3,2},{4,5},{5,4},{6,7},{7,6},{8,9},{9,8},{10,11... | collective-permute-start | bytes 147464 | tf_op jit(solution)/shard_map/ppermute | solution.py:498
  32.0 1.3 %collective-permute-start.6 = (f32[96,128]{1,0:T(8,128)S(1)}, f32[96,128]{1,0:T(8,128)S(1)}, u32[]{:S(2)}, u32[]{:S(2)}) collective-permute-start(f32[96,128]{1,0:T(8,128)S(1)} %get-tuple-element.92), channel_id=1, source_target_pairs={{0,1},{1,0},{2,3},{3,2},{4,5},{5,4},{6,7},{7,6},{8,9},{9,8},{10,11... | collective-permute-start | bytes 147464 | tf_op jit(solution)/shard_map/ppermute | solution.py:498
  33.4 4.1 %collective-permute-start.7 = (f32[192,128]{1,0:T(8,128)S(1)}, f32[192,128]{1,0:T(8,128)S(1)}, u32[]{:S(2)}, u32[]{:S(2)}) collective-permute-start(f32[192,128]{1,0:T(8,128)S(1)} %get-tuple-element.94), channel_id=1, source_target_pairs={{0,127},{1,2},{2,1},{3,4},{4,3},{5,6},{6,5},{7,8},{8,7},{9,10},{10... | collective-permute-start | bytes 294920 | tf_op jit(solution)/shard_map/ppermute | solution.py:501
  37.5 6.7 %collective-permute-start.8 = (f32[96,128]{1,0:T(8,128)S(1)}, f32[96,128]{1,0:T(8,128)S(1)}, u32[]{:S(2)}, u32[]{:S(2)}) collective-permute-start(f32[96,128]{1,0:T(8,128)S(1)} %get-tuple-element.99), channel_id=1, source_target_pairs={{0,1},{1,0},{2,3},{3,2},{4,5},{5,4},{6,7},{7,6},{8,9},{9,8},{10,11... | collective-permute-start | bytes 147464 | tf_op jit(solution)/shard_map/ppermute | solution.py:498
  45.7 21.9 %all-to-all-start = ((f32[128,8,128]{2,1,0:T(8,128)}), f32[128,8,128]{2,1,0:T(8,128)S(1)}, u32[]{:S(2)}, u32[]{:S(2)}) async-start(f32[128,8,128]{2,1,0:T(8,128)} %sample3.1), calls=%async_computation | async-start | bytes 1048576 | tf_op jit(solution)/shard_map/all_to_all | solution.py:591
  54.2 13.5 %copy-start = (bf16[64,1024]{1,0:T(8,128)(2,1)S(1)}, bf16[64,1024]{1,0:T(8,128)(2,1)}, u32[]{:S(2)}) copy-start(bf16[64,1024]{1,0:T(8,128)(2,1)} %constant.33.clone.spread_a) | copy-start | bytes 393220
  54.2 13.5 %copy-start.1 = (bf16[512,128]{1,0:T(8,128)(2,1)S(1)}, bf16[512,128]{1,0:T(8,128)(2,1)}, u32[]{:S(2)}) copy-start(bf16[512,128]{1,0:T(8,128)(2,1)} %constant.32.clone.table) | copy-start | bytes 393220
  54.2 13.5 %copy-start.6 = (bf16[64,128]{1,0:T(8,128)(2,1)S(1)}, bf16[64,128]{1,0:T(8,128)(2,1)}, u32[]{:S(2)}) copy-start(bf16[64,128]{1,0:T(8,128)(2,1)} %constant.34.clone.spread_b) | copy-start | bytes 49156

commit v2 on v1

--- a/solution.py
+++ b/solution.py
@@ -130,6 +130,8 @@
     return pltpu.with_memory_space_constraint(x, pltpu.HBM)
 
 
+PACK = 32
+ROWS = 9
 PLANE = (NY, NZ)
 FOUR = (4, NY, NZ)
 FIVE = (5, NY, NZ)
@@ -191,12 +193,12 @@
 
 
 def start_kernel(
-    par, now_in, vel_in, src_in, speed_in, left_in, right_in, mat_in,
-    now, vel, src, speed, left, right, mat, coef_ref, first_ref, msg_ref, sems,
+    par, now_in, vel_in, src_in, speed_in, left_in, right_in, mat_in, elem_in, weight_in,
+    now, vel, src, speed, left, right, mat, elem, weight, coef_ref, first_ref, msg_ref, sems,
 ):
     pairs = (
         (speed_in.at[0], speed), (left_in, left), (right_in, right), (now_in, now), (vel_in, vel),
-        (src_in, src), (mat_in, mat),
+        (elem_in, elem), (weight_in, weight), (src_in, src), (mat_in, mat),
     )
     copies = [pltpu.make_async_copy(a, b, sems.at[i]) for i, (a, b) in enumerate(pairs)]
     for copy in copies:
@@ -206,14 +208,16 @@
     coefs = expand_speed(speed[...], left[...], right[...])
     for i in range(5):
         coef_ref[i] = coefs[i]
-    msg_ref[NY:] = jnp.zeros((EY, NZ), FP)
-    msg_ref[NY:, :EZ] = speed[...]
+    msg_ref[NY:] = jnp.zeros((EY + PACK, NZ), FP)
+    msg_ref[NY : NY + EY, :EZ] = speed[...]
     copies[3].wait()
     g = to_right(coefs[4], [now[k] for k in range(4)])
     first_ref[...] = g
     msg_ref[:NY] = jnp.where(par[0] == 1, now[0], g)
     for copy in copies[4:]:
         copy.wait()
+    msg_ref[NY + EY : NY + EY + 25] = weight[100:125]
+    msg_ref[NY + EY + PACK - 1 :] = elem[...].astype(FP)
 
 
 def base_first_kernel(wave, now, vel, src, coef, mat_z, out, pad):
@@ -268,16 +272,28 @@
 
 
 def inner_first_kernel(
-    par, base, now, first, recv, speed, coef, left, right, mat_z, tent_ref, msg_ref, cleft_ref, pad
+    par, base, now, first, recv, speed, elem, weight, coef, left, right, mat_z,
+    tent_ref, msg_ref, cleft_ref, pad,
 ):
     odd = par[0] == 1
-    coefs = expand_speed(jnp.where(odd, recv[NY:, :EZ], 0.0), left[...], right[...])
+    coefs = expand_speed(jnp.where(odd, recv[NY : NY + EY, :EZ], 0.0), left[...], right[...])
     for i in range(5):
         cleft_ref[i] = coefs[i]
     share = half_left(now[0], coefs, mat_z, pad)
     inner_finish(odd, base, now, first[...], recv[:NY], coef[4], share, tent_ref, msg_ref)
-    msg_ref[2 * NY :] = jnp.zeros((EY, NZ), FP)
-    msg_ref[2 * NY :, :EZ] = speed[...]
+    at = 2 * NY
+    msg_ref[at:] = jnp.zeros((EY + 3 * PACK, NZ), FP)
+    msg_ref[at : at + EY, :EZ] = speed[...]
+    at += EY
+    msg_ref[at : at + 25] = jnp.where(odd, weight[100:125], weight[:25])
+    msg_ref[at + PACK - 1 : at + PACK] = elem[...].astype(FP)
+    at += PACK
+    pulled = -float(AB[0, 4]) * weight[:25]
+    for k in range(1, 4):
+        pulled = pulled - float(AB[k, 4]) * weight[25 * k : 25 * k + 25]
+    msg_ref[at : at + 25] = pulled
+    at += PACK
+    msg_ref[at:] = recv[NY + EY :]
 
 
 def inner_finish(odd, base, now, g_now, inner, sx, share, tent_ref, msg_ref):
@@ -321,7 +337,7 @@
     u_ref, msg_ref, outer_ref, coef0_ref, sxl_ref, last_ref, pad,
 ):
     odd = par[0] == 1
-    theirs = expand_speed(recv[2 * NY :, :EZ], left[...], right[...])
+    theirs = expand_speed(recv[2 * NY : 2 * NY + EY, :EZ], left[...], right[...])
     coefs = [jnp.where(odd, coef[i], theirs[i]) for i in range(5)]
     recv0 = recv[:NY]
     plane = jnp.where(odd, recv0, now[0])
@@ -375,56 +391,113 @@
     u_ref[0] = u_ref[0] - jnp.where(odd, inner[...], outer[...])
 
 
-def slots_kernel(elem, weight, pick_ref, spread_ref):
-    e = elem[...]
-    ey = e // EZ
-    ez = e - ey * EZ
+def pick_nodes(ez, pick_ref):
     z = lax.broadcasted_iota(jnp.int32, (NZ, CAP), 0)
     for c in range(5):
         hot = (z == 4 * ez + c).astype(FP).astype(jnp.bfloat16)
         for half in range(2):
             pick_ref[half * NZ : (half + 1) * NZ, c * CAP : (c + 1) * CAP] = hot
+
+
+def y_masks(ey):
     y = lax.broadcasted_iota(jnp.int32, (NY, CAP), 0)
     masks = []
     for b in range(5):
         row = 4 * ey + b
-        row = jnp.where(row >= NY, row - NY, row)
-        masks.append(y == row)
+        masks.append(y == jnp.where(row >= NY, row - NY, row))
+    return masks
+
+
+def spread_nodes(masks, weight, c):
+    total = jnp.zeros((NY, CAP), FP)
+    for b in range(5):
+        total = jnp.where(masks[b], weight[5 * b + c : 5 * b + c + 1, :], total)
+    return total
+
+
+def slots_kernel(elem, weight, pick_ref, spread_ref):
+    ey = elem[...] // EZ
+    pick_nodes(elem[...] - ey * EZ, pick_ref)
+    masks = y_masks(ey)
     for a in range(5):
+        plane = weight[25 * a : 25 * a + 25, :]
         for c in range(5):
-            total = jnp.zeros((NY, CAP), FP)
-            for b in range(5):
-                at = 25 * a + 5 * b + c
-                total = jnp.where(masks[b], weight[at : at + 1, :], total)
-            spread_ref[c, a * NY : (a + 1) * NY, :] = total
-
-
-def sample(u, last, pick, spread):
-    acc = jnp.zeros((8, CAP), FP)
-    for a in range(5):
-        plane = last[...] if a == 4 else u[a]
-        high = plane.astype(jnp.bfloat16)
-        low = (plane - high.astype(FP)).astype(jnp.bfloat16)
-        got = jnp.dot(
-            jnp.concatenate([high, low], 1), pick[...], preferred_element_type=jnp.float32
-        )
+            spread_ref[c, a * NY : (a + 1) * NY, :] = spread_nodes(masks, plane, c)
+
+
+def others_kernel(par, inner, outer, pick_l_ref, pick_2_ref, spread_ref):
+    odd = par[0] == 1
+    at = 2 * NY + EY
+    from_inner = inner[NY + EY :]
+    from_outer = outer[at : at + PACK]
+    relayed = outer[at + 2 * PACK :]
+    on_left = jnp.where(odd, from_inner, from_outer)
+    second = jnp.where(odd, from_outer, relayed)
+    pulled = jnp.where(odd, 0.0, outer[at + PACK : at + 2 * PACK])
+    for group, (package, pick_ref) in enumerate(((on_left, pick_l_ref), (second, pick_2_ref))):
+        elem = package[PACK - 1 :].astype(jnp.int32)
+        ey = elem // EZ
+        pick_nodes(elem - ey * EZ, pick_ref)
+        masks = y_masks(ey)
         for c in range(5):
-            part = got[:, c * CAP : (c + 1) * CAP] * spread[c, a * NY : (a + 1) * NY, :]
-            acc = acc + jnp.sum(part.reshape(NY // 8, 8, CAP), 0)
-    return jnp.sum(acc, 0, keepdims=True)
+            spread_ref[2 * group, c] = spread_nodes(masks, package, c)
+            if group == 0:
+                spread_ref[1, c] = spread_nodes(masks, pulled, c)
+
+
+def picked(planes, pick):
+    high, low = parts_of(jnp.concatenate(planes, 0), 2)
+    return jnp.dot(
+        jnp.concatenate([high, low], 1), pick[...], preferred_element_type=jnp.float32
+    )
+
+
+def weighted(got, spread):
+    total = None
+    for c in range(5):
+        term = got[:, c * CAP : (c + 1) * CAP] * spread(c)
+        total = term if total is None else total + term
+    return jnp.sum(jnp.sum(total.reshape(-1, 8, CAP), 0), 0, keepdims=True)
+
+
+def sample(planes, pick, spread):
+    rows = NY * len(planes)
+    return weighted(picked(planes, pick), lambda c: spread[c, :rows, :])
+
+
+def all_planes(u, last):
+    return [u[0], u[1], u[2], u[3], last]
 
 
 def sample_two_kernel(u0, l0, u1, l1, pick, spread, out):
-    out[0:1, :] = sample(u0, l0, pick, spread)
-    out[1:2, :] = sample(u1, l1, pick, spread)
-
-
-def sample_last_kernel(par, inner, outer, u0, l0, u1, pick, spread, r0, r1, out, last):
-    last[...] = jnp.where(par[0] == 1, outer[...], inner[...])
-    rows = [r0[...], r1[...], sample(u0, l0, pick, spread), sample(u1, last, pick, spread)]
-    rows = jnp.concatenate(rows + [jnp.zeros((2, CAP), FP)], 0)
-    for i in range(out.shape[0]):
-        out[i] = rows
+    out[0:1, :] = sample(all_planes(u0, l0[...]), pick, spread)
+    out[1:2, :] = sample(all_planes(u1, l1[...]), pick, spread)
+
+
+def sample_last_kernel(
+    par, u2, l2, u3, l3, u4, inner, tent, g, sxl, pick, spread, pick_l, pick_2, spread_o, first, out
+):
+    odd = par[0] == 1
+    own_g = jnp.where(odd, -g[...], 0.0)
+    face = u4[0]
+    x = sxl[...] * face
+    left = picked([tent[0], x, face], pick_l)
+    rows = [
+        first[...],
+        sample(all_planes(u2, l2[...]), pick, spread),
+        sample(all_planes(u3, l3[...]), pick, spread),
+        sample(all_planes(u4, jnp.where(odd, 0.0, inner[...])), pick, spread),
+        sample(all_planes(tent, own_g), pick, spread),
+        weighted(left[:NY], lambda c: spread_o[0, c])
+        + weighted(left[NY : 2 * NY], lambda c: spread_o[1, c]),
+        weighted(
+            picked([jnp.where(odd, -g[...], -float(AB[0, 4]) * x)], pick_2), lambda c: spread_o[2, c]
+        ),
+        jnp.where(odd, 0.0, weighted(left[2 * NY :], lambda c: spread_o[0, c])),
+    ]
+    rows = jnp.concatenate(rows, 0)
+    for i in range(out.shape[0] // ROWS):
+        out[ROWS * i : ROWS * (i + 1), :] = rows
 
 
 def stations_kernel(blocks, stations, row_ref, lane_ref):
@@ -442,21 +515,34 @@
     )
     j = lax.broadcasted_iota(jnp.int32, (2 * SB, 128), 0)
     wanted = jnp.where(j < SB, blocks[0, 0] * SB + j, blocks[0, 1] * SB + (j - SB))
-    row_ref[...] = jnp.where(jnp.abs(at - wanted.astype(FP)) < 0.5, 1.0, 0.0)
+    row = jnp.where(jnp.abs(at - wanted.astype(FP)) < 0.5, 1.0, 0.0)
+    device = lax.broadcasted_iota(jnp.int32, (2 * SB, 128), 1)
+    even = jnp.where(device % 2 == 0, row, 0.0)
+    row_ref[0] = row
+    row_ref[1] = pltpu.roll(row, 1, 1)
+    row_ref[2] = pltpu.roll(even, 2, 1) + pltpu.roll(even, 127, 1)
 
 
 def cross_kernel(gathered, row, lane, table, spread_a, spread_b, out, held, sems):
-    slabs = [gathered[pl.ds(t, 128, stride=8), :] for t in range(NT)]
-    hot = row[...].astype(jnp.bfloat16)
-    found = jnp.dot(
-        jnp.concatenate([hot, hot], 1),
-        jnp.concatenate(parts_of(jnp.concatenate(slabs, 1), 2), 0),
-        preferred_element_type=jnp.float32,
-    )
+    slabs = [gathered[pl.ds(t, 128, stride=ROWS), :] for t in range(ROWS)]
+
+    def select(which, slabs):
+        hot = row[which].astype(jnp.bfloat16)
+        parts = jnp.concatenate(parts_of(jnp.concatenate(slabs, 1), 2), 0)
+        return jnp.dot(
+            jnp.concatenate([hot, hot], 1), parts, preferred_element_type=jnp.float32
+        )
+
+    found = select(0, slabs[:6])
+    more = select(1, [slabs[8], slabs[6]])
+    last = select(2, [slabs[7]])
+    found = [found[:, 128 * t : 128 * (t + 1)] for t in range(NT)]
+    found[4] = found[4] + more[:, :128]
+    found[5] = found[5] + more[:, 128:] + last
     at = lax.broadcasted_iota(jnp.int32, (2 * SB, 128), 1)
     samples = jnp.zeros((2 * SB, 128), FP)
     for t in range(NT):
-        one = jnp.sum(found[:, 128 * t : 128 * (t + 1)] * lane[...], 1, keepdims=True)
+        one = jnp.sum(found[t] * lane[...], 1, keepdims=True)
         samples = jnp.where(at % 8 == t, one, samples)
     parts = [part.astype(FP) for part in parts_of(samples, 3)]
     mixed = jnp.zeros((2 * SB, 128), FP)
@@ -515,84 +601,92 @@
 
     par = (lax.axis_index("bulk") % 2).astype(jnp.int32).reshape(1)
 
-    now, vel, src, speed, left, right, mat_z, coef, g0, msg = call(
+    inputs = (now, vel, src, speed_sq, left, right, mat_z, slot_elem.reshape(1, CAP), slot_weight)
+    now, vel, src, speed, left, right, mat_z, elem, weight, coef, g0, msg = call(
         start_kernel,
         [(FOUR, FP)] * 3
         + [((EY, EZ), FP), (left.shape, FP), (right.shape, FP), (mat_z.shape, jnp.bfloat16)]
-        + [(FIVE, FP), (PLANE, FP), ((NY + EY, NZ), FP)],
-        (par, *(in_hbm(x) for x in (now, vel, src, speed_sq, left, right, mat_z))), "start",
-        specs=[SMEM] + [HBM] * 7, scratch=(pltpu.SemaphoreType.DMA((7,)),),
+        + [((1, CAP), jnp.int32), ((125, CAP), FP)]
+        + [(FIVE, FP), (PLANE, FP), ((NY + EY + PACK, NZ), FP)],
+        (par, *(in_hbm(x) for x in inputs)), "start",
+        specs=[SMEM] + [HBM] * 9, scratch=(pltpu.SemaphoreType.DMA((9,)),),
     )
     inner0 = swap_inner(msg)
     (base,) = call(
         base_first_kernel, [(FOUR, FP)], (wavelet, now, vel, src, coef, mat_z), "base0", 1, scratch=pads
     )
     tent, msg, cleft = call(
-        inner_first_kernel, [(FOUR, FP), ((2 * NY + EY, NZ), FP), (FIVE, FP)],
-        (par, base, now, g0, inner0, speed, coef, left, right, mat_z), "inner0", 1, scratch=one_pad,
+        inner_first_kernel, [(FOUR, FP), ((2 * NY + EY + 3 * PACK, NZ), FP), (FIVE, FP)],
+        (par, base, now, g0, inner0, speed, elem, weight, coef, left, right, mat_z), "inner0", 1,
+        scratch=one_pad,
     )
     outer0 = swap_outer(msg)
-    pick, spread = call(
-        slots_kernel, [((2 * NZ, 5 * CAP), jnp.bfloat16), ((5, 5 * NY, CAP), FP)],
-        (slot_elem.reshape(1, CAP), slot_weight), "slots",
-    )
+    pick_shape = ((2 * NZ, 5 * CAP), jnp.bfloat16)
+    pick, spread = call(slots_kernel, [pick_shape, ((5, 5 * NY, CAP), FP)], (elem, weight), "slots")
     row, lane = call(
-        stations_kernel, [((2 * SB, 128), FP), ((2 * SB, CAP), FP)],
+        stations_kernel, [((3, 2 * SB, 128), FP), ((2 * SB, CAP), FP)],
         (pair_blocks, slot_station.reshape(128, CAP)), "stations", 1,
     )
     outer0, pick, spread, row, lane = lax.optimization_barrier((outer0, pick, spread, row, lane))
-    u_a = now
-    u_b, msg, outer, coef0, sxl, last_a = call(
+    u1, msg, outer, coef0, sxl, last0 = call(
         outer_first_kernel,
         [(FOUR, FP), (PLANE, FP), (PLANE, FP), (FIVE, FP), (PLANE, FP), (PLANE, FP)],
         (par, tent, now, g0, outer0, inner0, coef, cleft, left, right, mat_z), "outer0", 1,
         scratch=one_pad,
     )
-    rows = []
-    step = 1
-    while True:
+
+    def base_of(step, u, before):
+        return call(
+            functools.partial(base_kernel, step), [(FOUR, FP)],
+            (wavelet, u, before, src, coef, coef0, mat_z), "base", 1, scratch=pads,
+        )[0]
+
+    def two_steps(step, u_b, u_a, msg, outer):
         inner = swap_inner(msg)
-        (base,) = call(
-            functools.partial(base_kernel, step), [(FOUR, FP)],
-            (wavelet, u_b, u_a, src, coef, coef0, mat_z), "base", 1, scratch=pads,
-        )
-        if step == NT - 1:
-            break
-        u_c, g_c, msg, last_b = call(
+        base = base_of(step, u_b, u_a)
+        u_c, g, msg, last = call(
             both_kernel, [(FOUR, FP), (PLANE, FP), (PLANE, FP), (PLANE, FP)],
             (par, base, inner, outer, coef), "both", 1,
         )
         inner = swap_inner(msg)
-        (base,) = call(
-            functools.partial(base_kernel, step + 1), [(FOUR, FP)],
-            (wavelet, u_c, u_b, src, coef, coef0, mat_z), "base", 1, scratch=pads,
-        )
+        base = base_of(step + 1, u_c, u_b)
         tent, msg = call(
             inner_kernel, [(FOUR, FP), ((2 * NY, NZ), FP)],
-            (par, base, u_c, g_c, inner, coef), "inner", 1,
+            (par, base, u_c, g, inner, coef), "inner", 1,
         )
-        recv = swap_outer(msg)
-        (two,) = call(
-            sample_two_kernel, [((2, CAP), FP)], (u_a, last_a, u_b, last_b, pick, spread), "sample2"
+        return u_c, g, last, inner, tent, msg
+
+    def complete(tent, u, g, recv, inner):
+        return call(
+            outer_kernel, [(FOUR, FP), (PLANE, FP), (PLANE, FP), (PLANE, FP)],
+            (par, tent, u, g, recv, inner, coef, sxl), "outer", 1,
         )
-        recv, two = lax.optimization_barrier((recv, two))
-        rows.append(two)
-        u_a = u_c
-        u_b, msg, outer, last_a = call(
-            outer_kernel, [(FOUR, FP), (PLANE, FP), (PLANE, FP), (PLANE, FP)],
-            (par, tent, u_c, g_c, recv, inner, coef, sxl), "outer", 1,
-        )
-        step += 2
+
+    u2, g2, last1, inner2, tent, msg = two_steps(1, u1, now, msg, outer)
+    recv = swap_outer(msg)
+    (rows,) = call(
+        sample_two_kernel, [((2, CAP), FP)], (now, last0, u1, last1, pick, spread), "sample2"
+    )
+    others = call(
+        others_kernel, [pick_shape, pick_shape, ((3, 5, NY, CAP), FP)], (par, inner0, outer0), "others", 1
+    )
+    recv, rows, *others = lax.optimization_barrier((recv, rows, *others))
+    u3, msg, outer, last2 = complete(tent, u2, g2, recv, inner2)
+    u4, g4, last3, inner4, tent, msg = two_steps(3, u3, u2, msg, outer)
     (mine,) = call(
-        sample_last_kernel, [((devices, 8, CAP), FP)],
-        (par, inner, outer, u_a, last_a, u_b, pick, spread, *rows), "sample3", 1,
-        scratch=(pltpu.VMEM(PLANE, FP),),
-    )
-    gathered = lax.all_to_all(mine, AXES, 0, 0, tiled=True)
-    (end,) = call(last_kernel, [(FOUR, FP)], (par, base, inner, outer, coef), "last", 1)
+        sample_last_kernel, [((devices * ROWS, CAP), FP)],
+        (par, u2, last2, u3, last3, u4, inner4, tent, g4, sxl, pick, spread, *others, rows), "sample4", 1,
+    )
+    gathered = lax.all_to_all(mine.reshape(devices, 1, ROWS * CAP), AXES, 0, 0, tiled=True)
+    recv = swap_outer(msg)
+    u5, msg, outer, _ = complete(tent, u4, g4, recv, inner4)
+    inner = swap_inner(msg)
+    (end,) = call(
+        last_kernel, [(FOUR, FP)], (par, base_of(5, u5, u4), inner, outer, coef), "last", 1
+    )
     (cross,) = call(
         cross_kernel, [((1, 2, F, SB * SB), jnp.bfloat16)],
-        (gathered.reshape(8 * devices, CAP), row, lane, table, reps, tiles), "cross",
+        (gathered.reshape(devices * ROWS, CAP), row, lane, table, reps, tiles), "cross",
         out_specs=[HBM],
         scratch=(pltpu.VMEM((2, F, SB * SB), jnp.bfloat16), pltpu.SemaphoreType.DMA((4,))),
     )

time: 69.9 us -> 65.2 us (0.933)
  waiting for transfers between devices: 20.5 us -> 10.6 us
  starting transfers between devices: 30.8 us -> 35.2 us
  Pallas kernels: 16.8 us -> 17.6 us
    all_to_all x1, waiting for transfers between devices: 11.8 us -> 0.01 us  [body(): lax.all_to_all(mine.reshape(devices, 1, ROWS * CAP), AXES, 0, 0, tiled=True)]
    ppermute x6, starting transfers between devices: 20.9 us -> 23.6 us  [swap_inner(): return lax.ppermute(x, AXES, inner_route)]
    ppermute x3, waiting for transfers between devices: 7.8 us -> 10.5 us  [swap_outer(): return lax.ppermute(x, AXES, outer_route)]
    ppermute x3, starting transfers between devices: 1.53 us -> 3.16 us  [swap_outer(): return lax.ppermute(x, AXES, outer_route)]
    ppermute x6, waiting for transfers between devices: 0.96 us -> 0.09 us  [swap_inner(): return lax.ppermute(x, AXES, inner_route)]
    pallas_call x22, Pallas kernels: 16.8 us -> 17.6 us  [call(): pl.pallas_call(kernel, out_shape=[jax.ShapeDtypeStruct(s, d) for s, d in...]
  transfers between devices with their start and end apart: 10 -> 10, of which waited for: 6 -> 4; matrix products, arithmetic and copies ran while one was open for 0% -> 0% of each run, Pallas kernels for 14% -> 16%
where the time goes in v2:
time: 65.2 us; the launch traced here: 64.9 us
  starting transfers between devices  35.2 us (54%)
  Pallas kernels  17.6 us (27%)
  waiting for transfers between devices  10.6 us (16%)
  between operations  0.82 us (1%)
  local copies, waits for them, and re-layouts  0.68 us (1%)
    ppermute x6, starting transfers between devices, swap_inner(): return lax.ppermute(x, AXES, inner_route)  23.6 us
    pallas_call x22, Pallas kernels, call(): pl.pallas_call(kernel, out_shape=[jax.ShapeDtypeStruct(s, d) for s, d in...  17.6 us
    ppermute x3, waiting for transfers between devices, swap_outer(): return lax.ppermute(x, AXES, outer_route)  10.5 us
    all_to_all x1, starting transfers between devices, body(): lax.all_to_all(mine.reshape(devices, 1, ROWS * CAP), AXES, 0, 0, tiled=True)  8.42 us
    ppermute x3, starting transfers between devices, swap_outer(): return lax.ppermute(x, AXES, outer_route)  3.16 us
  transfers between devices with their start and end apart: 10, of which 4 were waited for; matrix products, arithmetic and copies ran while one was open for 0% of the time, Pallas kernels for 16%

profile of v2, /device:TPU:1, one launch (start us, length us, event | category | flops | bytes accessed | tf_op | source)
XLA Modules:
  0.0 64.9 jit_solution(8223522380927275231)
XLA Ops:
  0.6 1.7 %start.1 = (f32[4,96,128]{2,1,0:T(8,128)S(1)}, f32[4,96,128]{2,1,0:T(8,128)S(1)}, f32[4,96,128]{2,1,0:T(8,128)S(1)}, f32[24,32]{1,0:T(8,128)S(1)}, f32[288,24]{1...) custom-call(s32[1]{0:T(128)} %bitcast.par, ...), custom_call_target="tpu_custom_call" | custom-call | flops 4000000 | bytes 1000000 | tf_op jit(solution)/shard_map/start/pallas_call | solution.py:117
  2.3 1.5 %collective-permute-start = (f32[152,128]{1,0:T(8,128)S(1)}, f32[152,128]{1,0:T(8,128)S(1)}, u32[]{:S(2)}, u32[]{:S(2)}) collective-permute-start(f32[152,128]{1,0:T(8,128)S(1)} %get-tuple-element.65), channel_id=1, source_target_pairs={{0,1},{1,0},{2,3},{3,2},{4,5},{5,4},{6,7},{7,6},{8,9},{9,8},{10,11... | collective-permute-start | bytes 233480 | tf_op jit(solution)/shard_map/ppermute | solution.py:584
  3.8 0.7 %copy-done.3 = f32[6]{0:T(128)S(1)} copy-done((f32[6]{0:T(128)S(1)}, f32[6]{0:T(128)}, u32[]{:S(2)}) %copy-start.3) | copy-done | bytes 48
  4.5 1.0 %base0.1.base = f32[4,96,128]{2,1,0:T(8,128)S(1)} custom-call(f32[6]{0:T(128)S(1)} %copy-done.3, f32[4,96,128]{2,1,0:T(8,128)S(1)} %get-tuple-element.59.now.prev.u0, f32[4,96,128]{2,1,0:T(8,128)S(1)} %get-tuple-element.60.vel, f32[4,96,128]{2,1,0:T(8,128)S(1)} %get-tuple-element.61.src, f32[5,96,128]{2,1,0:T(8,128)S(1)} %get-tuple-element.62.coef, ...), custom_call_target="tpu_custom_call" | custom-call | flops 4000000 | bytes 1000000 | tf_op jit(solution)/shard_map/base0/pallas_call | solution.py:117
  5.5 0.7 %inner0.1 = (f32[4,96,128]{2,1,0:T(8,128)S(1)}, f32[312,128]{1,0:T(8,128)S(1)}, f32[5,96,128]{2,1,0:T(8,128)S(1)}) custom-call(s32[1]{0:T(128)} %bitcast.par, f32[4,96,128]{2,1,0:T(8,128)S(1)} %base0.1.base, f32[4,96,128]{2,1,0:T(8,128)S(1)} %get-tuple-element.59.now.prev.u0, f32[96,128]{1,0:T(8,128)S(1)} %get-tuple-element.64.first, ...), custom_call_target="tpu_custom_call" | custom-call | flops 4000000 | bytes 1000000 | tf_op jit(solution)/shard_map/inner0/pallas_call | solution.py:117
  6.2 1.4 %collective-permute-start.1 = (f32[312,128]{1,0:T(8,128)S(1)}, f32[312,128]{1,0:T(8,128)S(1)}, u32[]{:S(2)}, u32[]{:S(2)}) collective-permute-start(f32[312,128]{1,0:T(8,128)S(1)} %get-tuple-element.72), channel_id=1, source_target_pairs={{0,127},{1,2},{2,1},{3,4},{4,3},{5,6},{6,5},{7,8},{8,7},{9,10},{10... | collective-permute-start | bytes 479240 | tf_op jit(solution)/shard_map/ppermute | solution.py:587
  8.1 1.3 %stations.1 = (f32[3,64,128]{2,1,0:T(8,128)S(1)}, f32[64,128]{1,0:T(8,128)S(1)}) custom-call(s32[1,2]{1,0:T(1,128)S(1)} %copy-done.6, s32[128,128]{1,0:T(8,128)S(1)} %bitcast.6), custom_call_target="tpu_custom_call" | custom-call | flops 4000000 | bytes 1000000 | tf_op jit(solution)/shard_map/stations/pallas_call | solution.py:117
  9.4 1.6 %collective-permute-done.1.recv.outer = f32[312,128]{1,0:T(8,128)S(1)} collective-permute-done((f32[312,128]{1,0:T(8,128)S(1)}, f32[312,128]{1,0:T(8,128)S(1)}, u32[]{:S(2)}, u32[]{:S(2)}) %collective-permute-start.1) | collective-permute-done | bytes 159776 | tf_op jit(solution)/shard_map/ppermute | solution.py:587
  11.0 0.7 %outer0.1 = (f32[4,96,128]{2,1,0:T(8,128)S(1)}, f32[96,128]{1,0:T(8,128)S(1)}, f32[96,128]{1,0:T(8,128)S(1)}, f32[5,96,128]{2,1,0:T(8,128)S(1)}, f32[96,128]{1,0:T(8,128)S(1)}, /*index=5*/f32[96,128]{1,0:T(8,128)S(1)}) custom-call(s32[1]{0:T(128)} %bitcast.par, f32[4,96,128]{2,1,0:T(8,128)S(1)} %get-tuple-element.71.tent, ...), custom_call_target="tpu_custom_call" | custom-call | flops 4000000 | bytes 1000000 | tf_op jit(solution)/shard_map/outer0/pallas_call | solution.py:117
  11.7 7.2 %collective-permute-start.2 = (f32[96,128]{1,0:T(8,128)S(1)}, f32[96,128]{1,0:T(8,128)S(1)}, u32[]{:S(2)}, u32[]{:S(2)}) collective-permute-start(f32[96,128]{1,0:T(8,128)S(1)} %get-tuple-element.81), channel_id=1, source_target_pairs={{0,1},{1,0},{2,3},{3,2},{4,5},{5,4},{6,7},{7,6},{8,9},{9,8},{10,11... | collective-permute-start | bytes 147464 | tf_op jit(solution)/shard_map/ppermute | solution.py:584
  19.0 1.0 %base.5 = f32[4,96,128]{2,1,0:T(8,128)S(1)} custom-call(f32[6]{0:T(128)S(1)} %copy-done.3, f32[4,96,128]{2,1,0:T(8,128)S(1)} %get-tuple-element.79.now.prev.u1, f32[4,96,128]{2,1,0:T(8,128)S(1)} %get-tuple-element.59.now.prev.u0, f32[4,96,128]{2,1,0:T(8,128)S(1)} %get-tuple-element.61.src, f32[5,96,128]{2,1,0:T(8,128)S(1)} %get-tuple-element.62.coef, ...), custom_call_target="tpu_custom_call" | custom-call | flops 4000000 | bytes 1000000 | tf_op jit(solution)/shard_map/base/pallas_call | solution.py:117
  20.3 1.0 %base.6 = f32[4,96,128]{2,1,0:T(8,128)S(1)} custom-call(f32[6]{0:T(128)S(1)} %copy-done.4, f32[4,96,128]{2,1,0:T(8,128)S(1)} %get-tuple-element.83.now.prev.u2, f32[4,96,128]{2,1,0:T(8,128)S(1)} %get-tuple-element.79.now.prev.u1, f32[4,96,128]{2,1,0:T(8,128)S(1)} %get-tuple-element.61.src, f32[5,96,128]{2,1,0:T(8,128)S(1)} %get-tuple-element.62.coef, ...), custom_call_target="tpu_custom_call" | custom-call | flops 4000000 | bytes 1000000 | tf_op jit(solution)/shard_map/base/pallas_call | solution.py:117
  22.5 3.1 %collective-permute-done.4.recv = f32[192,128]{1,0:T(8,128)S(1)} collective-permute-done((f32[192,128]{1,0:T(8,128)S(1)}, f32[192,128]{1,0:T(8,128)S(1)}, u32[]{:S(2)}, u32[]{:S(2)}) %collective-permute-start.4) | collective-permute-done | bytes 98336 | tf_op jit(solution)/shard_map/ppermute | solution.py:587
  25.6 5.8 %collective-permute-start.5 = (f32[96,128]{1,0:T(8,128)S(1)}, f32[96,128]{1,0:T(8,128)S(1)}, u32[]{:S(2)}, u32[]{:S(2)}) collective-permute-start(f32[96,128]{1,0:T(8,128)S(1)} %get-tuple-element.98), channel_id=1, source_target_pairs={{0,1},{1,0},{2,3},{3,2},{4,5},{5,4},{6,7},{7,6},{8,9},{9,8},{10,11... | collective-permute-start | bytes 147464 | tf_op jit(solution)/shard_map/ppermute | solution.py:584
  31.4 1.0 %base.7 = f32[4,96,128]{2,1,0:T(8,128)S(1)} custom-call(f32[6]{0:T(128)S(1)} %copy-done.4, f32[4,96,128]{2,1,0:T(8,128)S(1)} %get-tuple-element.97.now.prev.u3, f32[4,96,128]{2,1,0:T(8,128)S(1)} %get-tuple-element.83.now.prev.u2, f32[4,96,128]{2,1,0:T(8,128)S(1)} %get-tuple-element.61.src, f32[5,96,128]{2,1,0:T(8,128)S(1)} %get-tuple-element.62.coef, ...), custom_call_target="tpu_custom_call" | custom-call | flops 4000000 | bytes 1000000 | tf_op jit(solution)/shard_map/base/pallas_call | solution.py:117
  32.8 1.0 %base.8 = f32[4,96,128]{2,1,0:T(8,128)S(1)} custom-call(f32[6]{0:T(128)S(1)} %copy-done.4, f32[4,96,128]{2,1,0:T(8,128)S(1)} %get-tuple-element.100.now.prev.u4, f32[4,96,128]{2,1,0:T(8,128)S(1)} %get-tuple-element.97.now.prev.u3, f32[4,96,128]{2,1,0:T(8,128)S(1)} %get-tuple-element.61.src, f32[5,96,128]{2,1,0:T(8,128)S(1)} %get-tuple-element.62.coef, ...), custom_call_target="tpu_custom_call" | custom-call | flops 4000000 | bytes 1000000 | tf_op jit(solution)/shard_map/base/pallas_call | solution.py:117
  33.9 2.1 %sample4.1 = f32[1152,128]{1,0:T(8,128)} custom-call(s32[1]{0:T(128)} %bitcast.par, f32[4,96,128]{2,1,0:T(8,128)S(1)} %get-tuple-element.83.now.prev.u2, f32[96,128]{1,0:T(8,128)S(1)} %get-tuple-element.108.l2, f32[4,96,128]{2,1,0:T(8,128)S(1)} %get-tuple-element.97.now.prev.u3, f32[96,128]{1,0:T(8,128)S(1)} %get-tuple-element.109.l3, ...), custom_call_target="tpu_custom_call" | custom-call | flops 4000000 | bytes 1000000 | tf_op jit(solution)/shard_map/sample4/pallas_call | solution.py:117
  36.0 8.4 %all-to-all-start = ((f32[128,1,1152]{2,1,0:T(1,128)}), f32[128,1,1152]{2,1,0:T(1,128)S(1)}, u32[]{:S(2)}, u32[]{:S(2)}) async-start(f32[128,1,1152]{2,1,0:T(1,128)} %bitcast.3), calls=%async_computation | async-start | bytes 1179648 | tf_op jit(solution)/shard_map/all_to_all | solution.py:680
  44.4 1.7 %collective-permute-start.7 = (f32[192,128]{1,0:T(8,128)S(1)}, f32[192,128]{1,0:T(8,128)S(1)}, u32[]{:S(2)}, u32[]{:S(2)}) collective-permute-start(f32[192,128]{1,0:T(8,128)S(1)} %get-tuple-element.104), channel_id=1, source_target_pairs={{0,127},{1,2},{2,1},{3,4},{4,3},{5,6},{6,5},{7,8},{8,7},{9,10},{10... | collective-permute-start | bytes 294920 | tf_op jit(solution)/shard_map/ppermute | solution.py:587
  46.1 5.8 %collective-permute-done.7.recv = f32[192,128]{1,0:T(8,128)S(1)} collective-permute-done((f32[192,128]{1,0:T(8,128)S(1)}, f32[192,128]{1,0:T(8,128)S(1)}, u32[]{:S(2)}, u32[]{:S(2)}) %collective-permute-start.7) | collective-permute-done | bytes 98336 | tf_op jit(solution)/shard_map/ppermute | solution.py:587
  52.6 8.5 %collective-permute-start.8 = (f32[96,128]{1,0:T(8,128)S(1)}, f32[96,128]{1,0:T(8,128)S(1)}, u32[]{:S(2)}, u32[]{:S(2)}) collective-permute-start(f32[96,128]{1,0:T(8,128)S(1)} %get-tuple-element.106), channel_id=1, source_target_pairs={{0,1},{1,0},{2,3},{3,2},{4,5},{5,4},{6,7},{7,6},{8,9},{9,8},{10,11... | collective-permute-start | bytes 147464 | tf_op jit(solution)/shard_map/ppermute | solution.py:584
  61.1 1.0 %base.9 = f32[4,96,128]{2,1,0:T(8,128)S(1)} custom-call(f32[6]{0:T(128)S(1)} %copy-done.4, f32[4,96,128]{2,1,0:T(8,128)S(1)} %get-tuple-element.105.now, f32[4,96,128]{2,1,0:T(8,128)S(1)} %get-tuple-element.100.now.prev.u4, f32[4,96,128]{2,1,0:T(8,128)S(1)} %get-tuple-element.61.src, f32[5,96,128]{2,1,0:T(8,128)S(1)} %get-tuple-element.62.coef, ...), custom_call_target="tpu_custom_call" | custom-call | flops 4000000 | bytes 1000000 | tf_op jit(solution)/shard_map/base/pallas_call | solution.py:117
  62.2 0.7 %last.1 = f32[4,96,128]{2,1,0:T(8,128)} custom-call(s32[1]{0:T(128)} %bitcast.par, f32[4,96,128]{2,1,0:T(8,128)S(1)} %base.9, f32[96,128]{1,0:T(8,128)S(1)} %collective-permute-done.8.inner, f32[96,128]{1,0:T(8,128)S(1)} %get-tuple-element.107.outer, f32[5,96,128]{2,1,0:T(8,128)S(1)} %get-tuple-element.62.coef), custom_call_target="tpu_custom_call" | custom-call | flops 4000000 | bytes 1000000 | tf_op jit(solution)/shard_map/last/pallas_call | solution.py:117
  62.9 2.0 %cross.1 = bf16[1,2,256,1024]{3,2,1,0:T(8,128)(2,1)} custom-call(f32[1152,128]{1,0:T(8,128)S(1)} %bitcast.5, f32[3,64,128]{2,1,0:T(8,128)S(1)} %get-tuple-element.114.row, f32[64,128]{1,0:T(8,128)S(1)} %get-tuple-element.115.lane, bf16[512,128]{1,0:T(8,128)(2,1)S(1)} %copy-done, bf16[64,1024]{1,0:T(8,128)(2,1)S(1)} %copy-done.1, bf16[64,128]{1,0:T(8,128)(2,1)S(1)} %copy-done.5), custom_call_target="tpu_custom_call" | custom-call | flops 4000000 | bytes 1000000 | tf_op jit(solution)/shard_map/cross/pallas_call | solution.py:117
  (32 shorter events, 3.0 us)
Async XLA Ops:
  2.3 3.2 %collective-permute-start = (f32[152,128]{1,0:T(8,128)S(1)}, f32[152,128]{1,0:T(8,128)S(1)}, u32[]{:S(2)}, u32[]{:S(2)}) collective-permute-start(f32[152,128]{1,0:T(8,128)S(1)} %get-tuple-element.65), channel_id=1, source_target_pairs={{0,1},{1,0},{2,3},{3,2},{4,5},{5,4},{6,7},{7,6},{8,9},{9,8},{10,11... | collective-permute-start | bytes 233480 | tf_op jit(solution)/shard_map/ppermute | solution.py:584
  3.8 0.7 %copy-start.3 = (f32[6]{0:T(128)S(1)}, f32[6]{0:T(128)}, u32[]{:S(2)}) copy-start(f32[6]{0:T(128)} %wave.11) | copy-start | bytes 76
  4.5 3.6 %copy-start.2 = (s32[16384]{0:T(1024)S(1)}, s32[16384]{0:T(1024)}, u32[]{:S(2)}) copy-start(s32[16384]{0:T(1024)} %param.21) | copy-start | bytes 196612
  4.5 3.6 %copy-start.6 = (s32[1,2]{1,0:T(1,128)S(1)}, s32[1,2]{1,0:T(1,128)}, u32[]{:S(2)}) copy-start(s32[1,2]{1,0:T(1,128)} %blocks.1) | copy-start | bytes 28
  6.2 4.8 %collective-permute-start.1 = (f32[312,128]{1,0:T(8,128)S(1)}, f32[312,128]{1,0:T(8,128)S(1)}, u32[]{:S(2)}, u32[]{:S(2)}) collective-permute-start(f32[312,128]{1,0:T(8,128)S(1)} %get-tuple-element.72), channel_id=1, source_target_pairs={{0,127},{1,2},{2,1},{3,4},{4,3},{5,6},{6,5},{7,8},{8,7},{9,10},{10... | collective-permute-start | bytes 479240 | tf_op jit(solution)/shard_map/ppermute | solution.py:587
  11.7 8.6 %copy-start.4 = (f32[6]{0:T(128)S(1)}, f32[6]{0:T(128)}, u32[]{:S(2)}) copy-start(f32[6]{0:T(128)} %wave.11) | copy-start | bytes 76
  11.7 8.2 %collective-permute-start.2 = (f32[96,128]{1,0:T(8,128)S(1)}, f32[96,128]{1,0:T(8,128)S(1)}, u32[]{:S(2)}, u32[]{:S(2)}) collective-permute-start(f32[96,128]{1,0:T(8,128)S(1)} %get-tuple-element.81), channel_id=1, source_target_pairs={{0,1},{1,0},{2,3},{3,2},{4,5},{5,4},{6,7},{7,6},{8,9},{9,8},{10,11... | collective-permute-start | bytes 147464 | tf_op jit(solution)/shard_map/ppermute | solution.py:584
  20.1 1.3 %collective-permute-start.3 = (f32[96,128]{1,0:T(8,128)S(1)}, f32[96,128]{1,0:T(8,128)S(1)}, u32[]{:S(2)}, u32[]{:S(2)}) collective-permute-start(f32[96,128]{1,0:T(8,128)S(1)} %get-tuple-element.85), channel_id=1, source_target_pairs={{0,1},{1,0},{2,3},{3,2},{4,5},{5,4},{6,7},{7,6},{8,9},{9,8},{10,11... | collective-permute-start | bytes 147464 | tf_op jit(solution)/shard_map/ppermute | solution.py:584
  21.4 4.1 %collective-permute-start.4 = (f32[192,128]{1,0:T(8,128)S(1)}, f32[192,128]{1,0:T(8,128)S(1)}, u32[]{:S(2)}, u32[]{:S(2)}) collective-permute-start(f32[192,128]{1,0:T(8,128)S(1)} %get-tuple-element.87), channel_id=1, source_target_pairs={{0,127},{1,2},{2,1},{3,4},{4,3},{5,6},{6,5},{7,8},{8,7},{9,10},{10... | collective-permute-start | bytes 294920 | tf_op jit(solution)/shard_map/ppermute | solution.py:587
  25.6 6.9 %collective-permute-start.5 = (f32[96,128]{1,0:T(8,128)S(1)}, f32[96,128]{1,0:T(8,128)S(1)}, u32[]{:S(2)}, u32[]{:S(2)}) collective-permute-start(f32[96,128]{1,0:T(8,128)S(1)} %get-tuple-element.98), channel_id=1, source_target_pairs={{0,1},{1,0},{2,3},{3,2},{4,5},{5,4},{6,7},{7,6},{8,9},{9,8},{10,11... | collective-permute-start | bytes 147464 | tf_op jit(solution)/shard_map/ppermute | solution.py:584
  32.5 1.3 %collective-permute-start.6 = (f32[96,128]{1,0:T(8,128)S(1)}, f32[96,128]{1,0:T(8,128)S(1)}, u32[]{:S(2)}, u32[]{:S(2)}) collective-permute-start(f32[96,128]{1,0:T(8,128)S(1)} %get-tuple-element.102), channel_id=1, source_target_pairs={{0,1},{1,0},{2,3},{3,2},{4,5},{5,4},{6,7},{7,6},{8,9},{9,8},{10,11... | collective-permute-start | bytes 147464 | tf_op jit(solution)/shard_map/ppermute | solution.py:584
  36.0 26.9 %all-to-all-start = ((f32[128,1,1152]{2,1,0:T(1,128)}), f32[128,1,1152]{2,1,0:T(1,128)S(1)}, u32[]{:S(2)}, u32[]{:S(2)}) async-start(f32[128,1,1152]{2,1,0:T(1,128)} %bitcast.3), calls=%async_computation | async-start | bytes 1179648 | tf_op jit(solution)/shard_map/all_to_all | solution.py:680
  44.4 7.5 %collective-permute-start.7 = (f32[192,128]{1,0:T(8,128)S(1)}, f32[192,128]{1,0:T(8,128)S(1)}, u32[]{:S(2)}, u32[]{:S(2)}) collective-permute-start(f32[192,128]{1,0:T(8,128)S(1)} %get-tuple-element.104), channel_id=1, source_target_pairs={{0,127},{1,2},{2,1},{3,4},{4,3},{5,6},{6,5},{7,8},{8,7},{9,10},{10... | collective-permute-start | bytes 294920 | tf_op jit(solution)/shard_map/ppermute | solution.py:587
  52.6 10.3 %copy-start = (bf16[512,128]{1,0:T(8,128)(2,1)S(1)}, bf16[512,128]{1,0:T(8,128)(2,1)}, u32[]{:S(2)}) copy-start(bf16[512,128]{1,0:T(8,128)(2,1)} %constant.32.clone.table) | copy-start | bytes 393220
  52.6 10.3 %copy-start.1 = (bf16[64,1024]{1,0:T(8,128)(2,1)S(1)}, bf16[64,1024]{1,0:T(8,128)(2,1)}, u32[]{:S(2)}) copy-start(bf16[64,1024]{1,0:T(8,128)(2,1)} %constant.33.clone.spread_a) | copy-start | bytes 393220
  52.6 10.3 %copy-start.5 = (bf16[64,128]{1,0:T(8,128)(2,1)S(1)}, bf16[64,128]{1,0:T(8,128)(2,1)}, u32[]{:S(2)}) copy-start(bf16[64,128]{1,0:T(8,128)(2,1)} %constant.34.clone.spread_b) | copy-start | bytes 49156
  52.6 9.6 %collective-permute-start.8 = (f32[96,128]{1,0:T(8,128)S(1)}, f32[96,128]{1,0:T(8,128)S(1)}, u32[]{:S(2)}, u32[]{:S(2)}) collective-permute-start(f32[96,128]{1,0:T(8,128)S(1)} %get-tuple-element.106), channel_id=1, source_target_pairs={{0,1},{1,0},{2,3},{3,2},{4,5},{5,4},{6,7},{7,6},{8,9},{9,8},{10,11... | collective-permute-start | bytes 147464 | tf_op jit(solution)/shard_map/ppermute | solution.py:584

commit v3 on v2

--- a/solution.py
+++ b/solution.py
@@ -18,7 +18,7 @@
 EY = 24
 EZ = 32
 CAP = 128
-AXES = ("pair", "bulk")
+AXES = ("pair", "chip", "core")
 HIGHEST = lax.Precision.HIGHEST
 W1 = np.array([0.1, 49.0 / 90.0, 32.0 / 45.0, 49.0 / 90.0, 0.1])
 
@@ -66,7 +66,7 @@
         if b == 0:
             left[y, (e - 1) % EY] += W1[4]
             left[2 * NY + y, (e - 1) % EY] += 1.0
-    left = left / np.tile(my, 3)[:, None]
+    left[:NY] /= my[:, None]
     right = np.zeros((EZ, 3 * NZ))
     for z in range(NZ):
         e, c = divmod(z, 4)
@@ -75,11 +75,15 @@
         if c == 0 and e > 0:
             right[e - 1, NZ + z] += 1.0
             right[e - 1, 2 * NZ + z] += W1[4]
-    right = right / np.tile(mz, 3)[None, :] * (STEP_DT * STEP_DT)
+    right[:, 2 * NZ :] /= mz[None, :]
+    over_z = np.broadcast_to(1.0 / mz, (8, NZ)) * (STEP_DT * STEP_DT)
+    over_y = np.broadcast_to(1.0 / my[:8, None], (8, NZ)) * (STEP_DT * STEP_DT)
+    left = np.tile(left, (1, 3)).astype(jnp.bfloat16)
+    right = np.tile(right, (3, 1)).astype(jnp.bfloat16)
     high = mat_z.astype(jnp.bfloat16).astype(np.float64)
     low = (mat_z - high).astype(jnp.bfloat16)
     stack = np.concatenate([mat_z, mat_z], 0).astype(jnp.bfloat16)
-    return np.concatenate([stack, low], 0), f32(left), f32(right)
+    return np.concatenate([stack, low], 0), left, right, f32(np.concatenate([over_y, over_z], 0))
 
 
 PART_PAIRS = ((0, 0), (1, 0), (0, 1), (1, 1), (2, 0), (0, 2))
@@ -138,11 +142,18 @@
 FP = jnp.float32
 
 
-def expand_speed(speed, left, right):
-    rows = dot(left, speed)
-    by_z = dot(rows[:NY], right)
-    by_y = dot(rows[NY:], right[:, 2 * NZ :])
-    return by_z[:, :NZ], by_z[:, NZ : 2 * NZ], by_y[:NY], by_y[NY:], by_z[:, 2 * NZ :]
+def expand_speed(speed, left, right, over):
+    parts = jnp.concatenate(parts_of(speed, 3), 0)
+    rows = jnp.dot(left, parts, preferred_element_type=jnp.float32)
+    parts = jnp.concatenate(parts_of(rows, 3), 1)
+    by_z = jnp.dot(parts[:NY], right, preferred_element_type=jnp.float32)
+    by_y = jnp.dot(parts[NY:], right[:, 2 * NZ :], preferred_element_type=jnp.float32)
+    over_y = jnp.concatenate([over[:8]] * (NY // 8), 0)
+    over_z = over[8:9]
+    return (
+        by_z[:, :NZ] * over_z, by_z[:, NZ : 2 * NZ] * over_z, by_y[:NY] * over_y, by_y[NY:] * over_y,
+        by_z[:, 2 * NZ :] * (STEP_DT * STEP_DT),
+    )
 
 
 def along_z(u, mat_z):
@@ -193,28 +204,29 @@
 
 
 def start_kernel(
-    par, now_in, vel_in, src_in, speed_in, left_in, right_in, mat_in, elem_in, weight_in,
-    now, vel, src, speed, left, right, mat, elem, weight, coef_ref, first_ref, msg_ref, sems,
+    par, now_in, vel_in, src_in, speed_in, left_in, right_in, over_in, mat_in, elem_in, weight_in, wave_in,
+    now, vel, src, speed, left, right, over, mat, elem, weight, wave, coef_ref, first_ref, msg_ref, sems,
 ):
     pairs = (
-        (speed_in.at[0], speed), (left_in, left), (right_in, right), (now_in, now), (vel_in, vel),
-        (elem_in, elem), (weight_in, weight), (src_in, src), (mat_in, mat),
+        (speed_in.at[0], speed), (left_in, left), (right_in, right), (over_in, over), (now_in, now),
+        (elem_in, elem), (weight_in, weight), (vel_in, vel), (src_in, src), (mat_in, mat),
+        (wave_in, wave),
     )
     copies = [pltpu.make_async_copy(a, b, sems.at[i]) for i, (a, b) in enumerate(pairs)]
     for copy in copies:
         copy.start()
-    for copy in copies[:3]:
+    for copy in copies[:4]:
         copy.wait()
-    coefs = expand_speed(speed[...], left[...], right[...])
+    coefs = expand_speed(speed[...], left[...], right[...], over[...])
     for i in range(5):
         coef_ref[i] = coefs[i]
     msg_ref[NY:] = jnp.zeros((EY + PACK, NZ), FP)
     msg_ref[NY : NY + EY, :EZ] = speed[...]
-    copies[3].wait()
+    copies[4].wait()
     g = to_right(coefs[4], [now[k] for k in range(4)])
     first_ref[...] = g
     msg_ref[:NY] = jnp.where(par[0] == 1, now[0], g)
-    for copy in copies[4:]:
+    for copy in copies[5:]:
         copy.wait()
     msg_ref[NY + EY : NY + EY + 25] = weight[100:125]
     msg_ref[NY + EY + PACK - 1 :] = elem[...].astype(FP)
@@ -225,7 +237,7 @@
 
 
 def base_body(step, wave, now, prev, vel, src, coef, coef0, mat_z, out, pad):
-    scale = wave[step] * (STEP_DT * STEP_DT)
+    scale = jnp.broadcast_to(wave[:, step : step + 1] * (STEP_DT * STEP_DT), (8, NZ))
     by_z = along_z(now[...].reshape(4 * NY, NZ), mat_z)
     patterns = y_patterns()
     for k in range(4):
@@ -272,11 +284,11 @@
 
 
 def inner_first_kernel(
-    par, base, now, first, recv, speed, elem, weight, coef, left, right, mat_z,
+    par, base, now, first, recv, speed, elem, weight, coef, left, right, over, mat_z,
     tent_ref, msg_ref, cleft_ref, pad,
 ):
     odd = par[0] == 1
-    coefs = expand_speed(jnp.where(odd, recv[NY : NY + EY, :EZ], 0.0), left[...], right[...])
+    coefs = expand_speed(jnp.where(odd, recv[NY : NY + EY, :EZ], 0.0), left[...], right[...], over[...])
     for i in range(5):
         cleft_ref[i] = coefs[i]
     share = half_left(now[0], coefs, mat_z, pad)
@@ -333,11 +345,11 @@
 
 
 def outer_first_kernel(
-    par, tent, now, first, recv, inner, coef, cleft, left, right, mat_z,
+    par, tent, now, first, recv, inner, coef, cleft, left, right, over, mat_z,
     u_ref, msg_ref, outer_ref, coef0_ref, sxl_ref, last_ref, pad,
 ):
     odd = par[0] == 1
-    theirs = expand_speed(recv[2 * NY : 2 * NY + EY, :EZ], left[...], right[...])
+    theirs = expand_speed(recv[2 * NY : 2 * NY + EY, :EZ], left[...], right[...], over[...])
     coefs = [jnp.where(odd, coef[i], theirs[i]) for i in range(5)]
     recv0 = recv[:NY]
     plane = jnp.where(odd, recv0, now[0])
@@ -383,12 +395,11 @@
     last_ref[...] = last
 
 
-def last_kernel(par, base, inner, outer, coef, u_ref):
-    odd = par[0] == 1
-    pull = coef[4] * jnp.where(odd, outer[...], inner[...])
-    for k in range(4):
-        u_ref[k] = base[k] - float(AB[k, 4]) * pull
-    u_ref[0] = u_ref[0] - jnp.where(odd, inner[...], outer[...])
+def outer_last_kernel(par, tent, now, g_now, recv, inner, coef, sxl, u_ref, msg_ref, outer_ref):
+    outer_finish(
+        par[0] == 1, tent, coef[4], sxl[...], recv[:NY], recv[NY:], g_now[...], now[0], None,
+        (u_ref, msg_ref, outer_ref),
+    )
 
 
 def pick_nodes(ez, pick_ref):
@@ -469,39 +480,70 @@
     return [u[0], u[1], u[2], u[3], last]
 
 
-def sample_two_kernel(u0, l0, u1, l1, pick, spread, out):
+def sample_first_kernel(u0, l0, u1, l1, u2, pick, spread, out):
     out[0:1, :] = sample(all_planes(u0, l0[...]), pick, spread)
     out[1:2, :] = sample(all_planes(u1, l1[...]), pick, spread)
-
-
-def sample_last_kernel(
-    par, u2, l2, u3, l3, u4, inner, tent, g, sxl, pick, spread, pick_l, pick_2, spread_o, first, out
+    out[2:3, :] = sample([u2[k] for k in range(4)], pick, spread)
+
+
+def sample_second_kernel(first, l2, u3, pick, spread, out):
+    got = picked(all_planes(u3, l2[...]), pick)
+    rest = 4 * NY
+    out[0:2, :] = first[0:2, :]
+    out[2:3, :] = first[2:3, :] + weighted(got[rest:], lambda c: spread[c, rest:, :])
+    out[3:4, :] = weighted(got[:rest], lambda c: spread[c, :rest, :])
+
+
+def sample_third_kernel(
+    par, before, l3, u4, g, sxl, pick, spread, pick_l, pick_2, spread_o, out
 ):
     odd = par[0] == 1
-    own_g = jnp.where(odd, -g[...], 0.0)
+    got = picked(all_planes(u4, l3[...]), pick)
+    rest = 4 * NY
     face = u4[0]
     x = sxl[...] * face
-    left = picked([tent[0], x, face], pick_l)
+    left = picked([x, face], pick_l)
+    second = picked([jnp.where(odd, -g[...], -float(AB[0, 4]) * x)], pick_2)
+    out[0:3, :] = before[0:3, :]
+    out[3:4, :] = before[3:4, :] + weighted(got[rest:], lambda c: spread[c, rest:, :])
+    out[4:5, :] = weighted(got[:rest], lambda c: spread[c, :rest, :])
+    out[5:6, :] = weighted(left[:NY], lambda c: spread_o[1, c])
+    out[6:7, :] = weighted(second, lambda c: spread_o[2, c])
+    out[7:8, :] = jnp.where(odd, 0.0, weighted(left[NY:], lambda c: spread_o[0, c]))
+
+
+def sample_last_kernel(
+    par, before, inner, tent, g, pick, spread, pick_l, spread_o, out, block, sems
+):
+    odd = par[0] == 1
+    own_g = jnp.where(odd, -g[...], 0.0)
+    last = jnp.where(odd, 0.0, inner[...])
+    got = picked(all_planes(tent, own_g) + [last], pick)
+    face = picked([tent[0]], pick_l)
+    rest = 4 * NY
     rows = [
-        first[...],
-        sample(all_planes(u2, l2[...]), pick, spread),
-        sample(all_planes(u3, l3[...]), pick, spread),
-        sample(all_planes(u4, jnp.where(odd, 0.0, inner[...])), pick, spread),
-        sample(all_planes(tent, own_g), pick, spread),
-        weighted(left[:NY], lambda c: spread_o[0, c])
-        + weighted(left[NY : 2 * NY], lambda c: spread_o[1, c]),
-        weighted(
-            picked([jnp.where(odd, -g[...], -float(AB[0, 4]) * x)], pick_2), lambda c: spread_o[2, c]
-        ),
-        jnp.where(odd, 0.0, weighted(left[2 * NY :], lambda c: spread_o[0, c])),
+        before[0:4, :],
+        before[4:5, :] + weighted(got[5 * NY :], lambda c: spread[c, rest:, :]),
+        weighted(got[: 5 * NY], lambda c: spread[c]),
+        before[5:6, :] + weighted(face, lambda c: spread_o[0, c]),
+        before[6:8, :],
     ]
     rows = jnp.concatenate(rows, 0)
-    for i in range(out.shape[0] // ROWS):
-        out[ROWS * i : ROWS * (i + 1), :] = rows
-
-
-def stations_kernel(blocks, stations, row_ref, lane_ref):
-    lanes = []
+    for i in range(8):
+        block[ROWS * i : ROWS * (i + 1), :] = rows
+    size = 8 * ROWS
+    copies = [
+        pltpu.make_async_copy(block, out.at[pl.ds(size * i, size), :], sems.at[i])
+        for i in range(out.shape[0] // size)
+    ]
+    for copy in copies:
+        copy.start()
+    for copy in copies:
+        copy.wait()
+
+
+def stations_kernel(par, blocks, stations, row_ref, lane_ref):
+    odd = par[0] == 1
     for j in range(2 * SB):
         wanted = blocks[0, j // SB] * SB + j % SB
         hit = jnp.zeros((8, CAP), FP)
@@ -515,16 +557,27 @@
     )
     j = lax.broadcasted_iota(jnp.int32, (2 * SB, 128), 0)
     wanted = jnp.where(j < SB, blocks[0, 0] * SB + j, blocks[0, 1] * SB + (j - SB))
-    row = jnp.where(jnp.abs(at - wanted.astype(FP)) < 0.5, 1.0, 0.0)
-    device = lax.broadcasted_iota(jnp.int32, (2 * SB, 128), 1)
-    even = jnp.where(device % 2 == 0, row, 0.0)
-    row_ref[0] = row
-    row_ref[1] = pltpu.roll(row, 1, 1)
-    row_ref[2] = pltpu.roll(even, 2, 1) + pltpu.roll(even, 127, 1)
-
-
-def cross_kernel(gathered, row, lane, table, spread_a, spread_b, out, held, sems):
-    slabs = [gathered[pl.ds(t, 128, stride=ROWS), :] for t in range(ROWS)]
+    place = lax.broadcasted_iota(jnp.int32, (2 * SB, 128), 1)
+    hit = jnp.where(jnp.abs(at - wanted.astype(FP)) < 0.5, place.astype(FP), 0.0)
+    device = jnp.sum(hit, 1, keepdims=True).astype(jnp.int32)
+    first = jnp.where(odd, 1, 0)
+
+    def one_hot(device):
+        device = jnp.bitwise_and(device, 127)
+        side = jnp.where(jnp.bitwise_and(device, 1) == first, 0, 64)
+        return jnp.where(place == side + jnp.right_shift(device, 1), 1.0, 0.0)
+
+    row_ref[0] = one_hot(device)
+    row_ref[1] = one_hot(device + 1)
+    even = jnp.where(jnp.bitwise_and(device, 1) == 0, 1.0, 0.0)
+    row_ref[2] = even * (one_hot(device + 2) + one_hot(device + 127))
+
+
+def spectra_kernel(near, far, row, lane, table, out):
+    slabs = [
+        jnp.concatenate([half[pl.ds(t, 64, stride=ROWS), :] for half in (near, far)], 0)
+        for t in range(ROWS)
+    ]
 
     def select(which, slabs):
         hot = row[which].astype(jnp.bfloat16)
@@ -548,14 +601,26 @@
     mixed = jnp.zeros((2 * SB, 128), FP)
     for group, (part, _) in enumerate(PART_PAIRS):
         mixed = jnp.where(at // 8 == group, parts[part], mixed)
-    spectra = lax.dot_general(
+    out[...] = lax.dot_general(
         table[...], mixed.astype(jnp.bfloat16), (((1,), (1,)), ((), ())),
         preferred_element_type=jnp.float32,
     ).astype(jnp.bfloat16)
+
+
+def cross_kernel(
+    par, base, inner, outer, coef, spectra_in, spread_a, spread_b, end, out, held_end, held, sems
+):
+    odd = par[0] == 1
+    pull = coef[4] * jnp.where(odd, outer[...], inner[...])
+    for k in range(4):
+        value = base[k] - float(AB[k, 4]) * pull
+        held_end[k] = value - jnp.where(odd, inner[...], outer[...]) if k == 0 else value
+    copies = [pltpu.make_async_copy(held_end, end, sems.at[4])]
+    copies[0].start()
+    spectra = spectra_in[...]
     second = jnp.dot(spectra, spread_b[...], preferred_element_type=jnp.float32) * (1.0 / NT)
     b_re = second[:F]
     b_im = second[F:]
-    copies = []
     for i in range(4):
         first = jnp.dot(
             spectra, spread_a[:, 256 * i : 256 * (i + 1)], preferred_element_type=jnp.float32
@@ -586,7 +651,7 @@
     def swap_outer(x):
         return lax.ppermute(x, AXES, outer_route)
 
-    mat_z, left, right = (jnp.asarray(x) for x in tables())
+    mat_z, left, right, over = (jnp.asarray(x) for x in tables())
     table = jnp.asarray(dft_table())
     reps = np.zeros((2 * SB, SB * SB))
     for i in range(SB):
@@ -599,25 +664,28 @@
     pads = (pltpu.VMEM((4, NY + 16, NZ), FP),)
     one_pad = (pltpu.VMEM((1, NY + 16, NZ), FP),)
 
-    par = (lax.axis_index("bulk") % 2).astype(jnp.int32).reshape(1)
-
-    inputs = (now, vel, src, speed_sq, left, right, mat_z, slot_elem.reshape(1, CAP), slot_weight)
-    now, vel, src, speed, left, right, mat_z, elem, weight, coef, g0, msg = call(
+    par = lax.axis_index("core").astype(jnp.int32).reshape(1)
+
+    inputs = (
+        now, vel, src, speed_sq, left, right, over, mat_z, slot_elem.reshape(1, CAP), slot_weight,
+        wavelet.reshape(1, NT),
+    )
+    kept = [jax.ShapeDtypeStruct(x.shape, x.dtype) for x in inputs]
+    kept[3] = jax.ShapeDtypeStruct((EY, EZ), FP)
+    now, vel, src, speed, left, right, over, mat_z, elem, weight, wavelet, coef, g0, msg = call(
         start_kernel,
-        [(FOUR, FP)] * 3
-        + [((EY, EZ), FP), (left.shape, FP), (right.shape, FP), (mat_z.shape, jnp.bfloat16)]
-        + [((1, CAP), jnp.int32), ((125, CAP), FP)]
+        [(x.shape, x.dtype) for x in kept]
         + [(FIVE, FP), (PLANE, FP), ((NY + EY + PACK, NZ), FP)],
         (par, *(in_hbm(x) for x in inputs)), "start",
-        specs=[SMEM] + [HBM] * 9, scratch=(pltpu.SemaphoreType.DMA((9,)),),
+        specs=[SMEM] + [HBM] * len(inputs), scratch=(pltpu.SemaphoreType.DMA((len(inputs),)),),
     )
     inner0 = swap_inner(msg)
     (base,) = call(
-        base_first_kernel, [(FOUR, FP)], (wavelet, now, vel, src, coef, mat_z), "base0", 1, scratch=pads
+        base_first_kernel, [(FOUR, FP)], (wavelet, now, vel, src, coef, mat_z), "base0", scratch=pads
     )
     tent, msg, cleft = call(
         inner_first_kernel, [(FOUR, FP), ((2 * NY + EY + 3 * PACK, NZ), FP), (FIVE, FP)],
-        (par, base, now, g0, inner0, speed, elem, weight, coef, left, right, mat_z), "inner0", 1,
+        (par, base, now, g0, inner0, speed, elem, weight, coef, left, right, over, mat_z), "inner0", 1,
         scratch=one_pad,
     )
     outer0 = swap_outer(msg)
@@ -625,36 +693,41 @@
     pick, spread = call(slots_kernel, [pick_shape, ((5, 5 * NY, CAP), FP)], (elem, weight), "slots")
     row, lane = call(
         stations_kernel, [((3, 2 * SB, 128), FP), ((2 * SB, CAP), FP)],
-        (pair_blocks, slot_station.reshape(128, CAP)), "stations", 1,
+        (par, pair_blocks, slot_station.reshape(128, CAP)), "stations", 2,
     )
     outer0, pick, spread, row, lane = lax.optimization_barrier((outer0, pick, spread, row, lane))
     u1, msg, outer, coef0, sxl, last0 = call(
         outer_first_kernel,
         [(FOUR, FP), (PLANE, FP), (PLANE, FP), (FIVE, FP), (PLANE, FP), (PLANE, FP)],
-        (par, tent, now, g0, outer0, inner0, coef, cleft, left, right, mat_z), "outer0", 1,
+        (par, tent, now, g0, outer0, inner0, coef, cleft, left, right, over, mat_z), "outer0", 1,
         scratch=one_pad,
     )
 
     def base_of(step, u, before):
         return call(
             functools.partial(base_kernel, step), [(FOUR, FP)],
-            (wavelet, u, before, src, coef, coef0, mat_z), "base", 1, scratch=pads,
+            (wavelet, u, before, src, coef, coef0, mat_z), "base", scratch=pads,
         )[0]
 
-    def two_steps(step, u_b, u_a, msg, outer):
+    def two_steps(step, u_b, u_a, msg, outer, fill=(None, None)):
         inner = swap_inner(msg)
         base = base_of(step, u_b, u_a)
+        more = None
+        if fill[0]:
+            inner, base, more = lax.optimization_barrier((inner, base, fill[0]()))
         u_c, g, msg, last = call(
             both_kernel, [(FOUR, FP), (PLANE, FP), (PLANE, FP), (PLANE, FP)],
             (par, base, inner, outer, coef), "both", 1,
         )
         inner = swap_inner(msg)
         base = base_of(step + 1, u_c, u_b)
+        if fill[1]:
+            inner, base, more = lax.optimization_barrier((inner, base, fill[1](more, u_c, g, last)))
         tent, msg = call(
             inner_kernel, [(FOUR, FP), ((2 * NY, NZ), FP)],
             (par, base, u_c, g, inner, coef), "inner", 1,
         )
-        return u_c, g, last, inner, tent, msg
+        return u_c, g, last, inner, tent, msg, more
 
     def complete(tent, u, g, recv, inner):
         return call(
@@ -662,33 +735,63 @@
             (par, tent, u, g, recv, inner, coef, sxl), "outer", 1,
         )
 
-    u2, g2, last1, inner2, tent, msg = two_steps(1, u1, now, msg, outer)
+    u2, g2, last1, inner2, tent, msg, _ = two_steps(1, u1, now, msg, outer)
     recv = swap_outer(msg)
     (rows,) = call(
-        sample_two_kernel, [((2, CAP), FP)], (now, last0, u1, last1, pick, spread), "sample2"
+        sample_first_kernel, [((3, CAP), FP)], (now, last0, u1, last1, u2, pick, spread), "sample3"
     )
     others = call(
         others_kernel, [pick_shape, pick_shape, ((3, 5, NY, CAP), FP)], (par, inner0, outer0), "others", 1
     )
     recv, rows, *others = lax.optimization_barrier((recv, rows, *others))
     u3, msg, outer, last2 = complete(tent, u2, g2, recv, inner2)
-    u4, g4, last3, inner4, tent, msg = two_steps(3, u3, u2, msg, outer)
+
+    def second_rows():
+        return call(
+            sample_second_kernel, [((4, CAP), FP)], (rows, last2, u3, pick, spread), "sample5"
+        )[0]
+
+    def third_rows(before, u, g, last):
+        return call(
+            sample_third_kernel, [((8, CAP), FP)],
+            (par, before, last, u, g, sxl, pick, spread, *others), "sample8", 1,
+        )[0]
+
+    u4, g4, _, inner4, tent, msg, rows = two_steps(3, u3, u2, msg, outer, (second_rows, third_rows))
+    pick_l, _, spread_o = others
     (mine,) = call(
-        sample_last_kernel, [((devices * ROWS, CAP), FP)],
-        (par, u2, last2, u3, last3, u4, inner4, tent, g4, sxl, pick, spread, *others, rows), "sample4", 1,
-    )
-    gathered = lax.all_to_all(mine.reshape(devices, 1, ROWS * CAP), AXES, 0, 0, tiled=True)
+        sample_last_kernel, [((devices // 2 * ROWS, CAP), FP)],
+        (par, rows, inner4, tent, g4, pick, spread, pick_l, spread_o), "sample7", 1,
+        out_specs=[HBM],
+        scratch=(
+            pltpu.VMEM((8 * ROWS, CAP), FP), pltpu.SemaphoreType.DMA((devices // 16,)),
+        ),
+    )
+    near = lax.all_to_all(
+        mine.reshape(devices // 2, 1, ROWS * CAP), ("pair", "chip"), 0, 0, tiled=True
+    ).reshape(devices // 2 * ROWS, CAP)
     recv = swap_outer(msg)
-    u5, msg, outer, _ = complete(tent, u4, g4, recv, inner4)
+    recv, near = lax.optimization_barrier((recv, near))
+    far = swap_inner(near)
+    u5, msg, outer = call(
+        outer_last_kernel, [(FOUR, FP), (PLANE, FP), (PLANE, FP)],
+        (par, tent, u4, g4, recv, inner4, coef, sxl), "outer", 1,
+    )
     inner = swap_inner(msg)
-    (end,) = call(
-        last_kernel, [(FOUR, FP)], (par, base_of(5, u5, u4), inner, outer, coef), "last", 1
-    )
-    (cross,) = call(
-        cross_kernel, [((1, 2, F, SB * SB), jnp.bfloat16)],
-        (gathered.reshape(devices * ROWS, CAP), row, lane, table, reps, tiles), "cross",
-        out_specs=[HBM],
-        scratch=(pltpu.VMEM((2, F, SB * SB), jnp.bfloat16), pltpu.SemaphoreType.DMA((4,))),
+    base = base_of(5, u5, u4)
+    (spectra,) = call(
+        spectra_kernel, [((2 * F, 2 * SB), jnp.bfloat16)],
+        (near, far, row, lane, table), "spectra",
+    )
+    inner, base, spectra = lax.optimization_barrier((inner, base, spectra))
+    end, cross = call(
+        cross_kernel, [(FOUR, FP), ((1, 2, F, SB * SB), jnp.bfloat16)],
+        (par, base, inner, outer, coef, spectra, reps, tiles), "cross", 1,
+        out_specs=[HBM, HBM],
+        scratch=(
+            pltpu.VMEM(FOUR, FP), pltpu.VMEM((2, F, SB * SB), jnp.bfloat16),
+            pltpu.SemaphoreType.DMA((5,)),
+        ),
     )
     return end, cross
 
@@ -700,6 +803,8 @@
         P(), split, P(), P(None, AXES), P(AXES, None),
     )
     out_specs = (P(AXES, None, None), P(AXES, None, None, None))
-    devices = math.prod(mesh.shape.values())
+    grid = mesh.devices.reshape(mesh.shape["pair"], -1, 2)
+    mesh = jax.sharding.Mesh(grid, AXES)
+    devices = grid.size
     run = functools.partial(body, devices=devices)
     return jax.shard_map(run, mesh=mesh, in_specs=in_specs, out_specs=out_specs, check_vma=False)

time: 65.2 us -> 58.9 us (0.903)
  Pallas kernels: 17.6 us -> 12.8 us
  starting transfers between devices: 35.2 us -> 30.5 us
  waiting for transfers between devices: 10.6 us -> 14.5 us
    ppermute x6 -> x7, starting transfers between devices: 23.6 us -> 17.6 us  [swap_inner(): return lax.ppermute(x, AXES, inner_route)]
    pallas_call x22 -> x24, Pallas kernels: 17.6 us -> 12.8 us  [call(): pl.pallas_call(kernel, out_shape=[jax.ShapeDtypeStruct(s, d) for s, d in...]
    all_to_all x1, waiting for transfers between devices: 0.01 us -> 3.74 us  [body(): lax.all_to_all(mine.reshape(devices // 2, 1, ROWS * CAP), ('pair', 'chip'...]
    ppermute x6 -> x7, waiting for transfers between devices: 0.09 us -> 1.84 us  [swap_inner(): return lax.ppermute(x, AXES, inner_route)]
    ppermute x3, waiting for transfers between devices: 10.5 us -> 8.88 us  [swap_outer(): return lax.ppermute(x, AXES, outer_route)]
    all_to_all x1, starting transfers between devices: 8.42 us -> 9.32 us  [body(): lax.all_to_all(mine.reshape(devices // 2, 1, ROWS * CAP), ('pair', 'chip'...]
  transfers between devices with their start and end apart: 10 -> 11, of which waited for: 4 -> 8; matrix products, arithmetic and copies ran while one was open for 0% -> 0% of each run, Pallas kernels for 16% -> 12%
where the time goes in v3:
time: 58.9 us; the launch traced here: 58.6 us
  starting transfers between devices  30.5 us (52%)
  waiting for transfers between devices  14.5 us (25%)
  Pallas kernels  12.8 us (22%)
  between operations  0.85 us (1%)
    ppermute x7, starting transfers between devices, swap_inner(): return lax.ppermute(x, AXES, inner_route)  17.6 us
    pallas_call x24, Pallas kernels, call(): pl.pallas_call(kernel, out_shape=[jax.ShapeDtypeStruct(s, d) for s, d in...  12.8 us
    all_to_all x1, starting transfers between devices, body(): lax.all_to_all(mine.reshape(devices // 2, 1, ROWS * CAP), ('pair', 'chip'...  9.32 us
    ppermute x3, waiting for transfers between devices, swap_outer(): return lax.ppermute(x, AXES, outer_route)  8.88 us
    all_to_all x1, waiting for transfers between devices, body(): lax.all_to_all(mine.reshape(devices // 2, 1, ROWS * CAP), ('pair', 'chip'...  3.74 us
    ppermute x3, starting transfers between devices, swap_outer(): return lax.ppermute(x, AXES, outer_route)  3.57 us
    ppermute x7, waiting for transfers between devices, swap_inner(): return lax.ppermute(x, AXES, inner_route)  1.84 us
  transfers between devices with their start and end apart: 11, of which 8 were waited for; matrix products, arithmetic and copies ran while one was open for 0% of the time, Pallas kernels for 12%

profile of v3, /device:TPU:1, one launch (start us, length us, event | category | flops | bytes accessed | tf_op | source)
XLA Modules:
  0.0 58.6 jit_solution(4032312424297685498)
XLA Ops:
  0.6 1.5 %start.1 = (f32[4,96,128]{2,1,0:T(8,128)S(1)}, f32[4,96,128]{2,1,0:T(8,128)S(1)}, f32[4,96,128]{2,1,0:T(8,128)S(1)}, f32[24,32]{1,0:T(8,128)S(1)}, bf16[288,72]{...) custom-call(s32[1]{0:T(128)} %bitcast.par, ...), custom_call_target="tpu_custom_call" | custom-call | flops 4000000 | bytes 1000000 | tf_op jit(solution)/shard_map/start/pallas_call | solution.py:121
  2.1 1.5 %collective-permute-start = (f32[152,128]{1,0:T(8,128)S(1)}, f32[152,128]{1,0:T(8,128)S(1)}, u32[]{:S(2)}, u32[]{:S(2)}) collective-permute-start(f32[152,128]{1,0:T(8,128)S(1)} %get-tuple-element.79), channel_id=1, source_target_pairs={{0,1},{1,0},{2,3},{3,2},{4,5},{5,4},{6,7},{7,6},{8,9},{9,8},{10,11... | collective-permute-start | bytes 233480 | tf_op jit(solution)/shard_map/ppermute | solution.py:649
  4.5 0.5 inner0.1
  5.0 1.7 %collective-permute-start.1 = (f32[312,128]{1,0:T(8,128)S(1)}, f32[312,128]{1,0:T(8,128)S(1)}, u32[]{:S(2)}, u32[]{:S(2)}) collective-permute-start(f32[312,128]{1,0:T(8,128)S(1)} %get-tuple-element.87), channel_id=1, source_target_pairs={{0,127},{1,2},{2,1},{3,4},{4,3},{5,6},{6,5},{7,8},{8,7},{9,10},{10... | collective-permute-start | bytes 479240 | tf_op jit(solution)/shard_map/ppermute | solution.py:652
  7.2 1.3 %stations.1 = (f32[3,64,128]{2,1,0:T(8,128)S(1)}, f32[64,128]{1,0:T(8,128)S(1)}) custom-call(s32[1]{0:T(128)} %bitcast.par, s32[1,2]{1,0:T(1,128)S(1)} %copy-done.4, s32[128,128]{1,0:T(8,128)S(1)} %bitcast.8), custom_call_target="tpu_custom_call" | custom-call | flops 4000000 | bytes 1000000 | tf_op jit(solution)/shard_map/stations/pallas_call | solution.py:121
  8.5 1.3 %collective-permute-done.1.recv.outer = f32[312,128]{1,0:T(8,128)S(1)} collective-permute-done((f32[312,128]{1,0:T(8,128)S(1)}, f32[312,128]{1,0:T(8,128)S(1)}, u32[]{:S(2)}, u32[]{:S(2)}) %collective-permute-start.1) | collective-permute-done | bytes 159776 | tf_op jit(solution)/shard_map/ppermute | solution.py:652
  9.8 0.5 outer0.1
  10.3 7.2 %collective-permute-start.2 = (f32[96,128]{1,0:T(8,128)S(1)}, f32[96,128]{1,0:T(8,128)S(1)}, u32[]{:S(2)}, u32[]{:S(2)}) collective-permute-start(f32[96,128]{1,0:T(8,128)S(1)} %get-tuple-element.96), channel_id=1, source_target_pairs={{0,1},{1,0},{2,3},{3,2},{4,5},{5,4},{6,7},{7,6},{8,9},{9,8},{10,11... | collective-permute-start | bytes 147464 | tf_op jit(solution)/shard_map/ppermute | solution.py:649
  17.5 0.5 base.5
  18.9 0.5 base.6
  20.3 0.7 %sample3.1.first = f32[3,128]{1,0:T(4,128)S(1)} custom-call(f32[4,96,128]{2,1,0:T(8,128)S(1)} %get-tuple-element.73.now.prev.u0, f32[96,128]{1,0:T(8,128)S(1)} %get-tuple-element.103.l0, f32[4,96,128]{2,1,0:T(8,128)S(1)} %get-tuple-element.94.now.prev.u1, f32[96,128]{1,0:T(8,128)S(1)} %get-tuple-element.104.l1, ...), custom_call_target="tpu_custom_call" | custom-call | flops 4000000 | bytes 1000000 | tf_op jit(solution)/shard_map/sample3/pallas_call | solution.py:121
  21.0 2.9 %collective-permute-done.4.recv = f32[192,128]{1,0:T(8,128)S(1)} collective-permute-done((f32[192,128]{1,0:T(8,128)S(1)}, f32[192,128]{1,0:T(8,128)S(1)}, u32[]{:S(2)}, u32[]{:S(2)}) %collective-permute-start.4) | collective-permute-done | bytes 98336 | tf_op jit(solution)/shard_map/ppermute | solution.py:652
  24.0 5.9 %collective-permute-start.5 = (f32[96,128]{1,0:T(8,128)S(1)}, f32[96,128]{1,0:T(8,128)S(1)}, u32[]{:S(2)}, u32[]{:S(2)}) collective-permute-start(f32[96,128]{1,0:T(8,128)S(1)} %get-tuple-element.112), channel_id=1, source_target_pairs={{0,1},{1,0},{2,3},{3,2},{4,5},{5,4},{6,7},{7,6},{8,9},{9,8},{10,11... | collective-permute-start | bytes 147464 | tf_op jit(solution)/shard_map/ppermute | solution.py:649
  31.7 0.5 sample8.1.before
  32.2 1.3 %sample7.1 = f32[576,128]{1,0:T(8,128)} custom-call(s32[1]{0:T(128)} %bitcast.par, f32[8,128]{1,0:T(8,128)S(1)} %sample8.1.before, f32[96,128]{1,0:T(8,128)S(1)} %collective-permute-done.6.recv.inner, f32[4,96,128]{2,1,0:T(8,128)S(1)} %get-tuple-element.129.tent, f32[96,128]{1,0:T(8,128)S(1)} %get-tuple-element.123.g.g_now, ...), custom_call_target="tpu_custom_call" | custom-call | flops 4000000 | bytes 1000000 | tf_op jit(solution)/shard_map/sample7/pallas_call | solution.py:121
  33.5 9.3 %all-to-all-start = ((f32[64,1,1152]{2,1,0:T(1,128)}), f32[64,1,1152]{2,1,0:T(1,128)S(1)}, u32[]{:S(2)}, u32[]{:S(2)}) async-start(f32[64,1,1152]{2,1,0:T(1,128)} %bitcast.4), calls=%async_computation | async-start | bytes 589824 | tf_op jit(solution)/shard_map/all_to_all | solution.py:770
  42.9 1.8 %collective-permute-start.7 = (f32[192,128]{1,0:T(8,128)S(1)}, f32[192,128]{1,0:T(8,128)S(1)}, u32[]{:S(2)}, u32[]{:S(2)}) collective-permute-start(f32[192,128]{1,0:T(8,128)S(1)} %get-tuple-element.130), channel_id=1, source_target_pairs={{0,127},{1,2},{2,1},{3,4},{4,3},{5,6},{6,5},{7,8},{8,7},{9,10},{10... | collective-permute-start | bytes 294920 | tf_op jit(solution)/shard_map/ppermute | solution.py:652
  44.7 4.7 %collective-permute-done.7.recv = f32[192,128]{1,0:T(8,128)S(1)} collective-permute-done((f32[192,128]{1,0:T(8,128)S(1)}, f32[192,128]{1,0:T(8,128)S(1)}, u32[]{:S(2)}, u32[]{:S(2)}) %collective-permute-start.7) | collective-permute-done | bytes 98336 | tf_op jit(solution)/shard_map/ppermute | solution.py:652
  49.4 3.7 %all-to-all-done = f32[64,1,1152]{2,1,0:T(1,128)S(1)} async-done(((f32[64,1,1152]{2,1,0:T(1,128)}), f32[64,1,1152]{2,1,0:T(1,128)S(1)}, u32[]{:S(2)}, u32[]{:S(2)}) %all-to-all-start) | async-done | bytes 294944 | tf_op jit(solution)/shard_map/all_to_all | solution.py:770
  53.1 2.1 %collective-permute-start.9 = (f32[576,128]{1,0:T(8,128)S(1)}, f32[576,128]{1,0:T(8,128)S(1)}, u32[]{:S(2)}, u32[]{:S(2)}) collective-permute-start(f32[576,128]{1,0:T(8,128)S(1)} %bitcast.6), channel_id=1, source_target_pairs={{0,1},{1,0},{2,3},{3,2},{4,5},{5,4},{6,7},{7,6},{8,9},{9,8},{10,11... | collective-permute-start | bytes 884744 | tf_op jit(solution)/shard_map/ppermute | solution.py:649
  55.4 0.5 base.9
  55.9 0.6 collective-permute-done.9.far
  56.4 0.5 spectra.1.spectra_in
  57.0 1.6 %cross.1 = (f32[4,96,128]{2,1,0:T(8,128)}, bf16[1,2,256,1024]{3,2,1,0:T(8,128)(2,1)}) custom-call(s32[1]{0:T(128)} %bitcast.par, f32[4,96,128]{2,1,0:T(8,128)S(1)} %base.9, f32[96,128]{1,0:T(8,128)S(1)} %collective-permute-done.8.inner, f32[96,128]{1,0:T(8,128)S(1)} %get-tuple-element.140.outer, f32[5,96,128]{2,1,0:T(8,128)S(1)} %get-tuple-element.76.coef, ...), custom_call_target="tpu_custom_call" | custom-call | flops 4000000 | bytes 1000000 | tf_op jit(solution)/shard_map/cross/pallas_call | solution.py:121
  (32 shorter events, 5.2 us)
Async XLA Ops:
  2.1 2.4 %collective-permute-start = (f32[152,128]{1,0:T(8,128)S(1)}, f32[152,128]{1,0:T(8,128)S(1)}, u32[]{:S(2)}, u32[]{:S(2)}) collective-permute-start(f32[152,128]{1,0:T(8,128)S(1)} %get-tuple-element.79), channel_id=1, source_target_pairs={{0,1},{1,0},{2,3},{3,2},{4,5},{5,4},{6,7},{7,6},{8,9},{9,8},{10,11... | collective-permute-start | bytes 233480 | tf_op jit(solution)/shard_map/ppermute | solution.py:649
  3.6 3.6 %copy-start.2 = (s32[16384]{0:T(1024)S(1)}, s32[16384]{0:T(1024)}, u32[]{:S(2)}) copy-start(s32[16384]{0:T(1024)} %param.22) | copy-start | bytes 196612
  3.6 3.6 %copy-start.4 = (s32[1,2]{1,0:T(1,128)S(1)}, s32[1,2]{1,0:T(1,128)}, u32[]{:S(2)}) copy-start(s32[1,2]{1,0:T(1,128)} %blocks.1) | copy-start | bytes 28
  5.0 4.8 %collective-permute-start.1 = (f32[312,128]{1,0:T(8,128)S(1)}, f32[312,128]{1,0:T(8,128)S(1)}, u32[]{:S(2)}, u32[]{:S(2)}) collective-permute-start(f32[312,128]{1,0:T(8,128)S(1)} %get-tuple-element.87), channel_id=1, source_target_pairs={{0,127},{1,2},{2,1},{3,4},{4,3},{5,6},{6,5},{7,8},{8,7},{9,10},{10... | collective-permute-start | bytes 479240 | tf_op jit(solution)/shard_map/ppermute | solution.py:652
  10.3 8.1 %collective-permute-start.2 = (f32[96,128]{1,0:T(8,128)S(1)}, f32[96,128]{1,0:T(8,128)S(1)}, u32[]{:S(2)}, u32[]{:S(2)}) collective-permute-start(f32[96,128]{1,0:T(8,128)S(1)} %get-tuple-element.96), channel_id=1, source_target_pairs={{0,1},{1,0},{2,3},{3,2},{4,5},{5,4},{6,7},{7,6},{8,9},{9,8},{10,11... | collective-permute-start | bytes 147464 | tf_op jit(solution)/shard_map/ppermute | solution.py:649
  18.5 1.3 %collective-permute-start.3 = (f32[96,128]{1,0:T(8,128)S(1)}, f32[96,128]{1,0:T(8,128)S(1)}, u32[]{:S(2)}, u32[]{:S(2)}) collective-permute-start(f32[96,128]{1,0:T(8,128)S(1)} %get-tuple-element.100), channel_id=1, source_target_pairs={{0,1},{1,0},{2,3},{3,2},{4,5},{5,4},{6,7},{7,6},{8,9},{9,8},{10,11... | collective-permute-start | bytes 147464 | tf_op jit(solution)/shard_map/ppermute | solution.py:649
  19.8 4.1 %collective-permute-start.4 = (f32[192,128]{1,0:T(8,128)S(1)}, f32[192,128]{1,0:T(8,128)S(1)}, u32[]{:S(2)}, u32[]{:S(2)}) collective-permute-start(f32[192,128]{1,0:T(8,128)S(1)} %get-tuple-element.102), channel_id=1, source_target_pairs={{0,127},{1,2},{2,1},{3,4},{4,3},{5,6},{6,5},{7,8},{8,7},{9,10},{10... | collective-permute-start | bytes 294920 | tf_op jit(solution)/shard_map/ppermute | solution.py:652
  24.0 6.7 %collective-permute-start.5 = (f32[96,128]{1,0:T(8,128)S(1)}, f32[96,128]{1,0:T(8,128)S(1)}, u32[]{:S(2)}, u32[]{:S(2)}) collective-permute-start(f32[96,128]{1,0:T(8,128)S(1)} %get-tuple-element.112), channel_id=1, source_target_pairs={{0,1},{1,0},{2,3},{3,2},{4,5},{5,4},{6,7},{7,6},{8,9},{9,8},{10,11... | collective-permute-start | bytes 147464 | tf_op jit(solution)/shard_map/ppermute | solution.py:649
  30.8 1.4 %collective-permute-start.6 = (f32[96,128]{1,0:T(8,128)S(1)}, f32[96,128]{1,0:T(8,128)S(1)}, u32[]{:S(2)}, u32[]{:S(2)}) collective-permute-start(f32[96,128]{1,0:T(8,128)S(1)} %get-tuple-element.119), channel_id=1, source_target_pairs={{0,1},{1,0},{2,3},{3,2},{4,5},{5,4},{6,7},{7,6},{8,9},{9,8},{10,11... | collective-permute-start | bytes 147464 | tf_op jit(solution)/shard_map/ppermute | solution.py:649
  33.5 19.6 %all-to-all-start = ((f32[64,1,1152]{2,1,0:T(1,128)}), f32[64,1,1152]{2,1,0:T(1,128)S(1)}, u32[]{:S(2)}, u32[]{:S(2)}) async-start(f32[64,1,1152]{2,1,0:T(1,128)} %bitcast.4), calls=%async_computation | async-start | bytes 589824 | tf_op jit(solution)/shard_map/all_to_all | solution.py:770
  42.9 13.6 %copy-start = (bf16[512,128]{1,0:T(8,128)(2,1)S(1)}, bf16[512,128]{1,0:T(8,128)(2,1)}, u32[]{:S(2)}) copy-start(bf16[512,128]{1,0:T(8,128)(2,1)} %constant.22.clone.table) | copy-start | bytes 393220
  42.9 6.5 %collective-permute-start.7 = (f32[192,128]{1,0:T(8,128)S(1)}, f32[192,128]{1,0:T(8,128)S(1)}, u32[]{:S(2)}, u32[]{:S(2)}) collective-permute-start(f32[192,128]{1,0:T(8,128)S(1)} %get-tuple-element.130), channel_id=1, source_target_pairs={{0,127},{1,2},{2,1},{3,4},{4,3},{5,6},{6,5},{7,8},{8,7},{9,10},{10... | collective-permute-start | bytes 294920 | tf_op jit(solution)/shard_map/ppermute | solution.py:652
  53.1 3.3 %collective-permute-start.9 = (f32[576,128]{1,0:T(8,128)S(1)}, f32[576,128]{1,0:T(8,128)S(1)}, u32[]{:S(2)}, u32[]{:S(2)}) collective-permute-start(f32[576,128]{1,0:T(8,128)S(1)} %bitcast.6), channel_id=1, source_target_pairs={{0,1},{1,0},{2,3},{3,2},{4,5},{5,4},{6,7},{7,6},{8,9},{9,8},{10,11... | collective-permute-start | bytes 884744 | tf_op jit(solution)/shard_map/ppermute | solution.py:649
  55.3 1.7 %collective-permute-start.8 = (f32[96,128]{1,0:T(8,128)S(1)}, f32[96,128]{1,0:T(8,128)S(1)}, u32[]{:S(2)}, u32[]{:S(2)}) collective-permute-start(f32[96,128]{1,0:T(8,128)S(1)} %get-tuple-element.133), channel_id=1, source_target_pairs={{0,1},{1,0},{2,3},{3,2},{4,5},{5,4},{6,7},{7,6},{8,9},{9,8},{10,11... | collective-permute-start | bytes 147464 | tf_op jit(solution)/shard_map/ppermute | solution.py:649
  55.4 1.6 %copy-start.1 = (bf16[64,1024]{1,0:T(8,128)(2,1)S(1)}, bf16[64,1024]{1,0:T(8,128)(2,1)}, u32[]{:S(2)}) copy-start(bf16[64,1024]{1,0:T(8,128)(2,1)} %constant.23.clone.spread_a) | copy-start | bytes 393220
  55.4 1.6 %copy-start.3 = (bf16[64,128]{1,0:T(8,128)(2,1)S(1)}, bf16[64,128]{1,0:T(8,128)(2,1)}, u32[]{:S(2)}) copy-start(bf16[64,128]{1,0:T(8,128)(2,1)} %constant.24.clone.spread_b) | copy-start | bytes 49156

commit v4 on v3

--- a/solution.py
+++ b/solution.py
@@ -136,14 +136,14 @@
 
 PACK = 32
 ROWS = 9
+PACK_AT = 2 * NY + 2 * EY
 PLANE = (NY, NZ)
 FOUR = (4, NY, NZ)
 FIVE = (5, NY, NZ)
 FP = jnp.float32
 
 
-def expand_speed(speed, left, right, over):
-    parts = jnp.concatenate(parts_of(speed, 3), 0)
+def expand_speed(parts, left, right, over):
     rows = jnp.dot(left, parts, preferred_element_type=jnp.float32)
     parts = jnp.concatenate(parts_of(rows, 3), 1)
     by_z = jnp.dot(parts[:NY], right, preferred_element_type=jnp.float32)
@@ -154,6 +154,10 @@
         by_z[:, :NZ] * over_z, by_z[:, NZ : 2 * NZ] * over_z, by_y[:NY] * over_y, by_y[NY:] * over_y,
         by_z[:, 2 * NZ :] * (STEP_DT * STEP_DT),
     )
+
+
+def speed_parts(speed, count=3):
+    return jnp.concatenate(parts_of(speed, count), 0)
 
 
 def along_z(u, mat_z):
@@ -205,35 +209,35 @@
 
 def start_kernel(
     par, now_in, vel_in, src_in, speed_in, left_in, right_in, over_in, mat_in, elem_in, weight_in, wave_in,
-    now, vel, src, speed, left, right, over, mat, elem, weight, wave, coef_ref, first_ref, msg_ref, sems,
+    now, vel, src, speed, left, right, over, mat, elem, weight, wave, msg_ref, sems,
 ):
     pairs = (
-        (speed_in.at[0], speed), (left_in, left), (right_in, right), (over_in, over), (now_in, now),
-        (elem_in, elem), (weight_in, weight), (vel_in, vel), (src_in, src), (mat_in, mat),
-        (wave_in, wave),
+        (now_in, now), (speed_in.at[0], speed), (elem_in, elem), (weight_in, weight), (vel_in, vel),
+        (src_in, src), (left_in, left), (right_in, right), (over_in, over), (mat_in, mat), (wave_in, wave),
     )
     copies = [pltpu.make_async_copy(a, b, sems.at[i]) for i, (a, b) in enumerate(pairs)]
     for copy in copies:
         copy.start()
-    for copy in copies[:4]:
+    msg_ref[NY:] = jnp.zeros((EY + PACK, NZ), FP)
+    copies[0].wait()
+    msg_ref[:NY] = jnp.where(par[0] == 1, now[0], to_right(1.0, [now[k] for k in range(4)]))
+    for copy in copies[1:4]:
         copy.wait()
-    coefs = expand_speed(speed[...], left[...], right[...], over[...])
+    msg_ref[NY : NY + EY, :EZ] = speed[...]
+    msg_ref[NY + EY : NY + EY + 25] = weight[100:125]
+    msg_ref[NY + EY + PACK - 1 :] = elem[...].astype(FP)
+    for copy in copies[4:]:
+        copy.wait()
+
+
+def base_first_kernel(
+    wave, now, vel, src, speed, left, right, over, mat_z, out, coef_ref, first_ref, pad
+):
+    coefs = expand_speed(speed_parts(speed[...]), left[...], right[...], over[...])
     for i in range(5):
         coef_ref[i] = coefs[i]
-    msg_ref[NY:] = jnp.zeros((EY + PACK, NZ), FP)
-    msg_ref[NY : NY + EY, :EZ] = speed[...]
-    copies[4].wait()
-    g = to_right(coefs[4], [now[k] for k in range(4)])
-    first_ref[...] = g
-    msg_ref[:NY] = jnp.where(par[0] == 1, now[0], g)
-    for copy in copies[5:]:
-        copy.wait()
-    msg_ref[NY + EY : NY + EY + 25] = weight[100:125]
-    msg_ref[NY + EY + PACK - 1 :] = elem[...].astype(FP)
-
-
-def base_first_kernel(wave, now, vel, src, coef, mat_z, out, pad):
-    base_body(0, wave, now, None, vel, src, coef, None, mat_z, out, pad)
+    first_ref[...] = to_right(coefs[4], [now[k] for k in range(4)])
+    base_body(0, wave, now, None, vel, src, coef_ref, None, mat_z, out, pad)
 
 
 def base_body(step, wave, now, prev, vel, src, coef, coef0, mat_z, out, pad):
@@ -288,24 +292,30 @@
     tent_ref, msg_ref, cleft_ref, pad,
 ):
     odd = par[0] == 1
-    coefs = expand_speed(jnp.where(odd, recv[NY : NY + EY, :EZ], 0.0), left[...], right[...], over[...])
+    their_speed = jnp.where(odd, recv[NY : NY + EY, :EZ], 0.0)
+    coefs = expand_speed(speed_parts(their_speed), left[...], right[...], over[...])
     for i in range(5):
         cleft_ref[i] = coefs[i]
     share = half_left(now[0], coefs, mat_z, pad)
-    inner_finish(odd, base, now, first[...], recv[:NY], coef[4], share, tent_ref, msg_ref)
-    at = 2 * NY
-    msg_ref[at:] = jnp.zeros((EY + 3 * PACK, NZ), FP)
-    msg_ref[at : at + EY, :EZ] = speed[...]
-    at += EY
-    msg_ref[at : at + 25] = jnp.where(odd, weight[100:125], weight[:25])
-    msg_ref[at + PACK - 1 : at + PACK] = elem[...].astype(FP)
-    at += PACK
+    inner = jnp.where(odd, coefs[4] * recv[:NY], recv[:NY])
+    inner_finish(odd, base, now, first[...], inner, coef[4], share, tent_ref, msg_ref)
+    own_speed = jnp.concatenate([speed[...], jnp.zeros((EY, NZ - EZ), FP)], 1)
+    msg_ref[2 * NY : PACK_AT] = speed_parts(own_speed, 2)
     pulled = -float(AB[0, 4]) * weight[:25]
     for k in range(1, 4):
         pulled = pulled - float(AB[k, 4]) * weight[25 * k : 25 * k + 25]
-    msg_ref[at : at + 25] = pulled
-    at += PACK
-    msg_ref[at:] = recv[NY + EY :]
+    slots = elem[...].astype(FP)
+    theirs = recv[NY + EY :]
+    packages = (
+        (jnp.where(odd, weight[100:125], weight[:25]), slots),
+        (pulled, slots),
+        (theirs[:25], theirs[PACK - 1 :]),
+    )
+    for group, (rows, slots) in enumerate(packages):
+        eights = jnp.floor(slots * 0.125)
+        package = [rows, jnp.zeros((PACK - 27, CAP), FP), eights, slots - 8.0 * eights]
+        at = PACK_AT + 2 * PACK * group
+        msg_ref[at : at + 2 * PACK] = jnp.concatenate(parts_of(jnp.concatenate(package, 0), 2), 0)
 
 
 def inner_finish(odd, base, now, g_now, inner, sx, share, tent_ref, msg_ref):
@@ -319,8 +329,8 @@
                 value = value - share
         tent_ref[k] = value
         tent.append(value)
-    msg_ref[:NY] = jnp.where(odd, g_now, now[0])
-    msg_ref[NY : 2 * NY] = jnp.where(odd, to_right(sx, tent), tent[0])
+    msg_ref[:NY] = jnp.where(odd, g_now, now[0]).astype(jnp.bfloat16)
+    msg_ref[NY : 2 * NY] = jnp.where(odd, to_right(sx, tent), tent[0]).astype(jnp.bfloat16)
 
 
 def inner_kernel(par, base, now, g_now, recv, coef, tent_ref, msg_ref):
@@ -349,9 +359,10 @@
     u_ref, msg_ref, outer_ref, coef0_ref, sxl_ref, last_ref, pad,
 ):
     odd = par[0] == 1
-    theirs = expand_speed(recv[2 * NY : 2 * NY + EY, :EZ], left[...], right[...], over[...])
+    parts = jnp.concatenate([recv[2 * NY : PACK_AT, :EZ], jnp.zeros((EY, EZ), jnp.bfloat16)], 0)
+    theirs = expand_speed(parts, left[...], right[...], over[...])
     coefs = [jnp.where(odd, coef[i], theirs[i]) for i in range(5)]
-    recv0 = recv[:NY]
+    recv0 = recv[:NY].astype(FP)
     plane = jnp.where(odd, recv0, now[0])
     share = half_left(plane, coefs, mat_z, pad)
     on_left = [jnp.where(odd, cleft[i], theirs[i]) for i in range(5)]
@@ -361,17 +372,17 @@
     sxl_ref[...] = on_left[4]
     last_ref[...] = jnp.where(odd, recv0, inner[:NY])
     outer_finish(
-        odd, tent, coef[4], on_left[4], recv0, recv[NY : 2 * NY], first[...], now[0], share,
+        odd, tent, coef[4], on_left[4], recv0, recv[NY : 2 * NY].astype(FP), first[...], now[0], share,
         (u_ref, msg_ref, outer_ref),
     )
 
 
 def outer_kernel(par, tent, now, g_now, recv, inner, coef, sxl, u_ref, msg_ref, outer_ref, last_ref):
     odd = par[0] == 1
-    recv0 = recv[:NY]
+    recv0 = recv[:NY].astype(FP)
     last_ref[...] = jnp.where(odd, recv0, inner[...])
     outer_finish(
-        odd, tent, coef[4], sxl[...], recv0, recv[NY:], g_now[...], now[0], None,
+        odd, tent, coef[4], sxl[...], recv0, recv[NY:].astype(FP), g_now[...], now[0], None,
         (u_ref, msg_ref, outer_ref),
     )
 
@@ -397,7 +408,8 @@
 
 def outer_last_kernel(par, tent, now, g_now, recv, inner, coef, sxl, u_ref, msg_ref, outer_ref):
     outer_finish(
-        par[0] == 1, tent, coef[4], sxl[...], recv[:NY], recv[NY:], g_now[...], now[0], None,
+        par[0] == 1, tent, coef[4], sxl[...], recv[:NY].astype(FP), recv[NY:].astype(FP), g_now[...],
+        now[0], None,
         (u_ref, msg_ref, outer_ref),
     )
 
@@ -438,20 +450,35 @@
 
 def others_kernel(par, inner, outer, pick_l_ref, pick_2_ref, spread_ref):
     odd = par[0] == 1
-    at = 2 * NY + EY
     from_inner = inner[NY + EY :]
-    from_outer = outer[at : at + PACK]
-    relayed = outer[at + 2 * PACK :]
-    on_left = jnp.where(odd, from_inner, from_outer)
-    second = jnp.where(odd, from_outer, relayed)
-    pulled = jnp.where(odd, 0.0, outer[at + PACK : at + 2 * PACK])
-    for group, (package, pick_ref) in enumerate(((on_left, pick_l_ref), (second, pick_2_ref))):
-        elem = package[PACK - 1 :].astype(jnp.int32)
+    halves = [
+        outer[PACK_AT + PACK * i : PACK_AT + PACK * (i + 1)].astype(FP) for i in range(6)
+    ]
+    from_outer, pulled, relayed = (halves[2 * i] + halves[2 * i + 1] for i in range(3))
+    pulled = jnp.where(odd, 0.0, pulled)
+
+    def number(package):
+        return 8.0 * package[PACK - 2 : PACK - 1] + package[PACK - 1 :]
+
+    groups = (
+        (
+            jnp.where(odd, from_inner[:25], from_outer[:25]),
+            jnp.where(odd, from_inner[PACK - 1 :], number(from_outer)),
+            pick_l_ref,
+        ),
+        (
+            jnp.where(odd, from_outer[:25], relayed[:25]),
+            jnp.where(odd, number(from_outer), number(relayed)),
+            pick_2_ref,
+        ),
+    )
+    for group, (rows, elem, pick_ref) in enumerate(groups):
+        elem = elem.astype(jnp.int32)
         ey = elem // EZ
         pick_nodes(elem - ey * EZ, pick_ref)
         masks = y_masks(ey)
         for c in range(5):
-            spread_ref[2 * group, c] = spread_nodes(masks, package, c)
+            spread_ref[2 * group, c] = spread_nodes(masks, rows, c)
             if group == 0:
                 spread_ref[1, c] = spread_nodes(masks, pulled, c)
 
@@ -615,7 +642,7 @@
     for k in range(4):
         value = base[k] - float(AB[k, 4]) * pull
         held_end[k] = value - jnp.where(odd, inner[...], outer[...]) if k == 0 else value
-    copies = [pltpu.make_async_copy(held_end, end, sems.at[4])]
+    copies = [pltpu.make_async_copy(held_end, end, sems.at[8])]
     copies[0].start()
     spectra = spectra_in[...]
     second = jnp.dot(spectra, spread_b[...], preferred_element_type=jnp.float32) * (1.0 / NT)
@@ -626,15 +653,15 @@
             spectra, spread_a[:, 256 * i : 256 * (i + 1)], preferred_element_type=jnp.float32
         )
         for half in range(2):
-            cols = slice(256 * i + 128 * half, 256 * i + 128 * (half + 1))
+            at = 2 * i + half
+            cols = slice(128 * at, 128 * (at + 1))
             a_re = first[:F, 128 * half : 128 * (half + 1)]
             a_im = first[F:, 128 * half : 128 * (half + 1)]
             held[0, :, cols] = (a_re * b_re + a_im * b_im).astype(jnp.bfloat16)
             held[1, :, cols] = (a_im * b_re - a_re * b_im).astype(jnp.bfloat16)
-        cols = slice(256 * i, 256 * (i + 1))
-        copy = pltpu.make_async_copy(held.at[:, :, cols], out.at[0, :, :, cols], sems.at[i])
-        copy.start()
-        copies.append(copy)
+            copy = pltpu.make_async_copy(held.at[:, :, cols], out.at[0, :, :, cols], sems.at[at])
+            copy.start()
+            copies.append(copy)
     for copy in copies:
         copy.wait()
 
@@ -672,19 +699,20 @@
     )
     kept = [jax.ShapeDtypeStruct(x.shape, x.dtype) for x in inputs]
     kept[3] = jax.ShapeDtypeStruct((EY, EZ), FP)
-    now, vel, src, speed, left, right, over, mat_z, elem, weight, wavelet, coef, g0, msg = call(
+    now, vel, src, speed, left, right, over, mat_z, elem, weight, wavelet, msg = call(
         start_kernel,
-        [(x.shape, x.dtype) for x in kept]
-        + [(FIVE, FP), (PLANE, FP), ((NY + EY + PACK, NZ), FP)],
+        [(x.shape, x.dtype) for x in kept] + [((NY + EY + PACK, NZ), FP)],
         (par, *(in_hbm(x) for x in inputs)), "start",
         specs=[SMEM] + [HBM] * len(inputs), scratch=(pltpu.SemaphoreType.DMA((len(inputs),)),),
     )
     inner0 = swap_inner(msg)
-    (base,) = call(
-        base_first_kernel, [(FOUR, FP)], (wavelet, now, vel, src, coef, mat_z), "base0", scratch=pads
+    base, coef, g0 = call(
+        base_first_kernel, [(FOUR, FP), (FIVE, FP), (PLANE, FP)],
+        (wavelet, now, vel, src, speed, left, right, over, mat_z), "base0", scratch=pads,
     )
     tent, msg, cleft = call(
-        inner_first_kernel, [(FOUR, FP), ((2 * NY + EY + 3 * PACK, NZ), FP), (FIVE, FP)],
+        inner_first_kernel,
+        [(FOUR, FP), ((PACK_AT + 6 * PACK, NZ), jnp.bfloat16), (FIVE, FP)],
         (par, base, now, g0, inner0, speed, elem, weight, coef, left, right, over, mat_z), "inner0", 1,
         scratch=one_pad,
     )
@@ -724,7 +752,7 @@
         if fill[1]:
             inner, base, more = lax.optimization_barrier((inner, base, fill[1](more, u_c, g, last)))
         tent, msg = call(
-            inner_kernel, [(FOUR, FP), ((2 * NY, NZ), FP)],
+            inner_kernel, [(FOUR, FP), ((2 * NY, NZ), jnp.bfloat16)],
             (par, base, u_c, g, inner, coef), "inner", 1,
         )
         return u_c, g, last, inner, tent, msg, more
@@ -790,7 +818,7 @@
         out_specs=[HBM, HBM],
         scratch=(
             pltpu.VMEM(FOUR, FP), pltpu.VMEM((2, F, SB * SB), jnp.bfloat16),
-            pltpu.SemaphoreType.DMA((5,)),
+            pltpu.SemaphoreType.DMA((9,)),
         ),
     )
     return end, cross

time: 58.9 us -> 57.5 us (0.976)
  waiting for transfers between devices: 14.5 us -> 13.1 us
    ppermute x3, waiting for transfers between devices: 8.88 us -> 5.72 us  [swap_outer(): return lax.ppermute(x, AXES, outer_route)]
    all_to_all x1, waiting for transfers between devices: 3.74 us -> 5.82 us  [body(): lax.all_to_all(mine.reshape(devices // 2, 1, ROWS * CAP), ('pair', 'chip'...]
  transfers between devices with their start and end apart: 11 -> 11, of which waited for: 8 -> 8; matrix products, arithmetic and copies ran while one was open for 0% -> 0% of each run, Pallas kernels for 12% -> 13%
where the time goes in v4:
time: 57.5 us; the launch traced here: 57.3 us
  starting transfers between devices  30.1 us (52%)
  Pallas kernels  13.2 us (23%)
  waiting for transfers between devices  13.1 us (23%)
  between operations  0.87 us (2%)
    ppermute x7, starting transfers between devices, swap_inner(): return lax.ppermute(x, AXES, inner_route)  17.2 us
    pallas_call x24, Pallas kernels, call(): pl.pallas_call(kernel, out_shape=[jax.ShapeDtypeStruct(s, d) for s, d in...  13.2 us
    all_to_all x1, starting transfers between devices, body(): lax.all_to_all(mine.reshape(devices // 2, 1, ROWS * CAP), ('pair', 'chip'...  9.3 us
    all_to_all x1, waiting for transfers between devices, body(): lax.all_to_all(mine.reshape(devices // 2, 1, ROWS * CAP), ('pair', 'chip'...  5.82 us
    ppermute x3, waiting for transfers between devices, swap_outer(): return lax.ppermute(x, AXES, outer_route)  5.72 us
    ppermute x3, starting transfers between devices, swap_outer(): return lax.ppermute(x, AXES, outer_route)  3.6 us
    ppermute x7, waiting for transfers between devices, swap_inner(): return lax.ppermute(x, AXES, inner_route)  1.54 us
  transfers between devices with their start and end apart: 11, of which 8 were waited for; matrix products, arithmetic and copies ran while one was open for 0% of the time, Pallas kernels for 13%

profile of v4, /device:TPU:1, one launch (start us, length us, event | category | flops | bytes accessed | tf_op | source)
XLA Modules:
  0.0 57.3 jit_solution(6997310192908386794)
XLA Ops:
  0.6 1.4 %start.1 = (f32[4,96,128]{2,1,0:T(8,128)S(1)}, f32[4,96,128]{2,1,0:T(8,128)S(1)}, f32[4,96,128]{2,1,0:T(8,128)S(1)}, f32[24,32]{1,0:T(8,128)S(1)}, bf16[288,72]{...) custom-call(s32[1]{0:T(128)} %bitcast.par, ...), custom_call_target="tpu_custom_call" | custom-call | flops 4000000 | bytes 1000000 | tf_op jit(solution)/shard_map/start/pallas_call | solution.py:121
  2.1 1.5 %collective-permute-start = (f32[152,128]{1,0:T(8,128)S(1)}, f32[152,128]{1,0:T(8,128)S(1)}, u32[]{:S(2)}, u32[]{:S(2)}) collective-permute-start(f32[152,128]{1,0:T(8,128)S(1)} %get-tuple-element.84), channel_id=1, source_target_pairs={{0,1},{1,0},{2,3},{3,2},{4,5},{5,4},{6,7},{7,6},{8,9},{9,8},{10,11... | collective-permute-start | bytes 233480 | tf_op jit(solution)/shard_map/ppermute | solution.py:676
  3.6 0.7 %base0.1 = (f32[4,96,128]{2,1,0:T(8,128)S(1)}, f32[5,96,128]{2,1,0:T(8,128)S(1)}, f32[96,128]{1,0:T(8,128)S(1)}) custom-call(f32[1,6]{1,0:T(1,128)S(1)} %get-tuple-element.73.wave, f32[4,96,128]{2,1,0:T(8,128)S(1)} %get-tuple-element.74.now.prev.u0, f32[4,96,128]{2,1,0:T(8,128)S(1)} %get-tuple-element.75.vel, f32[4,96,128]{2,1,0:T(8,128)S(1)} %get-tuple-element.76.src, ...), custom_call_target="tpu_custom_call" | custom-call | flops 4000000 | bytes 1000000 | tf_op jit(solution)/shard_map/base0/pallas_call | solution.py:121
  4.5 0.5 inner0.1
  5.0 1.7 %collective-permute-start.1 = (bf16[432,128]{1,0:T(8,128)(2,1)S(1)}, bf16[432,128]{1,0:T(8,128)(2,1)S(1)}, u32[]{:S(2)}, u32[]{:S(2)}) collective-permute-start(bf16[432,128]{1,0:T(8,128)(2,1)S(1)} %get-tuple-element.89), channel_id=1, source_target_pairs={{0,127},{1,2},{2,1},{3,4},{4,3},{5,6},{6,5},{7,8},{8,7},{9,10},{10... | collective-permute-start | bytes 331784 | tf_op jit(solution)/shard_map/ppermute | solution.py:679
  7.2 1.3 %stations.1 = (f32[3,64,128]{2,1,0:T(8,128)S(1)}, f32[64,128]{1,0:T(8,128)S(1)}) custom-call(s32[1]{0:T(128)} %bitcast.par, s32[1,2]{1,0:T(1,128)S(1)} %copy-done.4, s32[128,128]{1,0:T(8,128)S(1)} %bitcast.8), custom_call_target="tpu_custom_call" | custom-call | flops 4000000 | bytes 1000000 | tf_op jit(solution)/shard_map/stations/pallas_call | solution.py:121
  8.5 0.7 %collective-permute-done.1.recv.outer = bf16[432,128]{1,0:T(8,128)(2,1)S(1)} collective-permute-done((bf16[432,128]{1,0:T(8,128)(2,1)S(1)}, bf16[432,128]{1,0:T(8,128)(2,1)S(1)}, u32[]{:S(2)}, u32[]{:S(2)}) %collective-permute-start.1) | collective-permute-done | bytes 110624 | tf_op jit(solution)/shard_map/ppermute | solution.py:679
  9.3 0.5 outer0.1
  9.8 7.2 %collective-permute-start.2 = (f32[96,128]{1,0:T(8,128)S(1)}, f32[96,128]{1,0:T(8,128)S(1)}, u32[]{:S(2)}, u32[]{:S(2)}) collective-permute-start(f32[96,128]{1,0:T(8,128)S(1)} %get-tuple-element.98), channel_id=1, source_target_pairs={{0,1},{1,0},{2,3},{3,2},{4,5},{5,4},{6,7},{7,6},{8,9},{9,8},{10,11... | collective-permute-start | bytes 147464 | tf_op jit(solution)/shard_map/ppermute | solution.py:676
  18.4 0.5 base.6
  19.8 0.7 %sample3.1.first = f32[3,128]{1,0:T(4,128)S(1)} custom-call(f32[4,96,128]{2,1,0:T(8,128)S(1)} %get-tuple-element.74.now.prev.u0, f32[96,128]{1,0:T(8,128)S(1)} %get-tuple-element.105.l0, f32[4,96,128]{2,1,0:T(8,128)S(1)} %get-tuple-element.96.now.prev.u1, f32[96,128]{1,0:T(8,128)S(1)} %get-tuple-element.106.l1, ...), custom_call_target="tpu_custom_call" | custom-call | flops 4000000 | bytes 1000000 | tf_op jit(solution)/shard_map/sample3/pallas_call | solution.py:121
  20.6 2.4 %collective-permute-done.4.recv = bf16[192,128]{1,0:T(8,128)(2,1)S(1)} collective-permute-done((bf16[192,128]{1,0:T(8,128)(2,1)S(1)}, bf16[192,128]{1,0:T(8,128)(2,1)S(1)}, u32[]{:S(2)}, u32[]{:S(2)}) %collective-permute-start.4) | collective-permute-done | bytes 49184 | tf_op jit(solution)/shard_map/ppermute | solution.py:679
  23.0 5.9 %collective-permute-start.5 = (f32[96,128]{1,0:T(8,128)S(1)}, f32[96,128]{1,0:T(8,128)S(1)}, u32[]{:S(2)}, u32[]{:S(2)}) collective-permute-start(f32[96,128]{1,0:T(8,128)S(1)} %get-tuple-element.114), channel_id=1, source_target_pairs={{0,1},{1,0},{2,3},{3,2},{4,5},{5,4},{6,7},{7,6},{8,9},{9,8},{10,11... | collective-permute-start | bytes 147464 | tf_op jit(solution)/shard_map/ppermute | solution.py:676
  28.8 0.5 base.7
  30.6 0.5 sample8.1.before
  31.2 1.3 %sample7.1 = f32[576,128]{1,0:T(8,128)} custom-call(s32[1]{0:T(128)} %bitcast.par, f32[8,128]{1,0:T(8,128)S(1)} %sample8.1.before, f32[96,128]{1,0:T(8,128)S(1)} %collective-permute-done.6.recv.inner, f32[4,96,128]{2,1,0:T(8,128)S(1)} %get-tuple-element.131.tent, f32[96,128]{1,0:T(8,128)S(1)} %get-tuple-element.125.g.g_now, ...), custom_call_target="tpu_custom_call" | custom-call | flops 4000000 | bytes 1000000 | tf_op jit(solution)/shard_map/sample7/pallas_call | solution.py:121
  32.5 9.3 %all-to-all-start = ((f32[64,1,1152]{2,1,0:T(1,128)}), f32[64,1,1152]{2,1,0:T(1,128)S(1)}, u32[]{:S(2)}, u32[]{:S(2)}) async-start(f32[64,1,1152]{2,1,0:T(1,128)} %bitcast.4), calls=%async_computation | async-start | bytes 589824 | tf_op jit(solution)/shard_map/all_to_all | solution.py:798
  41.8 1.8 %collective-permute-start.7 = (bf16[192,128]{1,0:T(8,128)(2,1)S(1)}, bf16[192,128]{1,0:T(8,128)(2,1)S(1)}, u32[]{:S(2)}, u32[]{:S(2)}) collective-permute-start(bf16[192,128]{1,0:T(8,128)(2,1)S(1)} %get-tuple-element.132), channel_id=1, source_target_pairs={{0,127},{1,2},{2,1},{3,4},{4,3},{5,6},{6,5},{7,8},{8,7},{9,10},{10... | collective-permute-start | bytes 147464 | tf_op jit(solution)/shard_map/ppermute | solution.py:679
  43.7 2.6 %collective-permute-done.7.recv = bf16[192,128]{1,0:T(8,128)(2,1)S(1)} collective-permute-done((bf16[192,128]{1,0:T(8,128)(2,1)S(1)}, bf16[192,128]{1,0:T(8,128)(2,1)S(1)}, u32[]{:S(2)}, u32[]{:S(2)}) %collective-permute-start.7) | collective-permute-done | bytes 49184 | tf_op jit(solution)/shard_map/ppermute | solution.py:679
  46.3 5.8 %all-to-all-done = f32[64,1,1152]{2,1,0:T(1,128)S(1)} async-done(((f32[64,1,1152]{2,1,0:T(1,128)}), f32[64,1,1152]{2,1,0:T(1,128)S(1)}, u32[]{:S(2)}, u32[]{:S(2)}) %all-to-all-start) | async-done | bytes 294944 | tf_op jit(solution)/shard_map/all_to_all | solution.py:798
  52.1 1.7 %collective-permute-start.9 = (f32[576,128]{1,0:T(8,128)S(1)}, f32[576,128]{1,0:T(8,128)S(1)}, u32[]{:S(2)}, u32[]{:S(2)}) collective-permute-start(f32[576,128]{1,0:T(8,128)S(1)} %bitcast.6), channel_id=1, source_target_pairs={{0,1},{1,0},{2,3},{3,2},{4,5},{5,4},{6,7},{7,6},{8,9},{9,8},{10,11... | collective-permute-start | bytes 884744 | tf_op jit(solution)/shard_map/ppermute | solution.py:676
  54.5 0.6 collective-permute-done.9.far
  55.0 0.5 spectra.1.spectra_in
  55.6 1.7 %cross.1 = (f32[4,96,128]{2,1,0:T(8,128)}, bf16[1,2,256,1024]{3,2,1,0:T(8,128)(2,1)}) custom-call(s32[1]{0:T(128)} %bitcast.par, f32[4,96,128]{2,1,0:T(8,128)S(1)} %base.9, f32[96,128]{1,0:T(8,128)S(1)} %collective-permute-done.8.inner, f32[96,128]{1,0:T(8,128)S(1)} %get-tuple-element.142.outer, f32[5,96,128]{2,1,0:T(8,128)S(1)} %get-tuple-element.87.coef, ...), custom_call_target="tpu_custom_call" | custom-call | flops 4000000 | bytes 1000000 | tf_op jit(solution)/shard_map/cross/pallas_call | solution.py:121
  (32 shorter events, 4.9 us)
Async XLA Ops:
  2.1 5.1 %copy-start.2 = (s32[16384]{0:T(1024)S(1)}, s32[16384]{0:T(1024)}, u32[]{:S(2)}) copy-start(s32[16384]{0:T(1024)} %param.22) | copy-start | bytes 196612
  2.1 5.1 %copy-start.4 = (s32[1,2]{1,0:T(1,128)S(1)}, s32[1,2]{1,0:T(1,128)}, u32[]{:S(2)}) copy-start(s32[1,2]{1,0:T(1,128)} %blocks.1) | copy-start | bytes 28
  2.1 2.4 %collective-permute-start = (f32[152,128]{1,0:T(8,128)S(1)}, f32[152,128]{1,0:T(8,128)S(1)}, u32[]{:S(2)}, u32[]{:S(2)}) collective-permute-start(f32[152,128]{1,0:T(8,128)S(1)} %get-tuple-element.84), channel_id=1, source_target_pairs={{0,1},{1,0},{2,3},{3,2},{4,5},{5,4},{6,7},{7,6},{8,9},{9,8},{10,11... | collective-permute-start | bytes 233480 | tf_op jit(solution)/shard_map/ppermute | solution.py:676
  5.0 4.3 %collective-permute-start.1 = (bf16[432,128]{1,0:T(8,128)(2,1)S(1)}, bf16[432,128]{1,0:T(8,128)(2,1)S(1)}, u32[]{:S(2)}, u32[]{:S(2)}) collective-permute-start(bf16[432,128]{1,0:T(8,128)(2,1)S(1)} %get-tuple-element.89), channel_id=1, source_target_pairs={{0,127},{1,2},{2,1},{3,4},{4,3},{5,6},{6,5},{7,8},{8,7},{9,10},{10... | collective-permute-start | bytes 331784 | tf_op jit(solution)/shard_map/ppermute | solution.py:679
  9.8 8.1 %collective-permute-start.2 = (f32[96,128]{1,0:T(8,128)S(1)}, f32[96,128]{1,0:T(8,128)S(1)}, u32[]{:S(2)}, u32[]{:S(2)}) collective-permute-start(f32[96,128]{1,0:T(8,128)S(1)} %get-tuple-element.98), channel_id=1, source_target_pairs={{0,1},{1,0},{2,3},{3,2},{4,5},{5,4},{6,7},{7,6},{8,9},{9,8},{10,11... | collective-permute-start | bytes 147464 | tf_op jit(solution)/shard_map/ppermute | solution.py:676
  17.9 1.3 %collective-permute-start.3 = (f32[96,128]{1,0:T(8,128)S(1)}, f32[96,128]{1,0:T(8,128)S(1)}, u32[]{:S(2)}, u32[]{:S(2)}) collective-permute-start(f32[96,128]{1,0:T(8,128)S(1)} %get-tuple-element.102), channel_id=1, source_target_pairs={{0,1},{1,0},{2,3},{3,2},{4,5},{5,4},{6,7},{7,6},{8,9},{9,8},{10,11... | collective-permute-start | bytes 147464 | tf_op jit(solution)/shard_map/ppermute | solution.py:676
  19.3 3.6 %collective-permute-start.4 = (bf16[192,128]{1,0:T(8,128)(2,1)S(1)}, bf16[192,128]{1,0:T(8,128)(2,1)S(1)}, u32[]{:S(2)}, u32[]{:S(2)}) collective-permute-start(bf16[192,128]{1,0:T(8,128)(2,1)S(1)} %get-tuple-element.104), channel_id=1, source_target_pairs={{0,127},{1,2},{2,1},{3,4},{4,3},{5,6},{6,5},{7,8},{8,7},{9,10},{10... | collective-permute-start | bytes 147464 | tf_op jit(solution)/shard_map/ppermute | solution.py:679
  23.0 6.7 %collective-permute-start.5 = (f32[96,128]{1,0:T(8,128)S(1)}, f32[96,128]{1,0:T(8,128)S(1)}, u32[]{:S(2)}, u32[]{:S(2)}) collective-permute-start(f32[96,128]{1,0:T(8,128)S(1)} %get-tuple-element.114), channel_id=1, source_target_pairs={{0,1},{1,0},{2,3},{3,2},{4,5},{5,4},{6,7},{7,6},{8,9},{9,8},{10,11... | collective-permute-start | bytes 147464 | tf_op jit(solution)/shard_map/ppermute | solution.py:676
  29.8 1.4 %collective-permute-start.6 = (f32[96,128]{1,0:T(8,128)S(1)}, f32[96,128]{1,0:T(8,128)S(1)}, u32[]{:S(2)}, u32[]{:S(2)}) collective-permute-start(f32[96,128]{1,0:T(8,128)S(1)} %get-tuple-element.121), channel_id=1, source_target_pairs={{0,1},{1,0},{2,3},{3,2},{4,5},{5,4},{6,7},{7,6},{8,9},{9,8},{10,11... | collective-permute-start | bytes 147464 | tf_op jit(solution)/shard_map/ppermute | solution.py:676
  32.5 19.6 %all-to-all-start = ((f32[64,1,1152]{2,1,0:T(1,128)}), f32[64,1,1152]{2,1,0:T(1,128)S(1)}, u32[]{:S(2)}, u32[]{:S(2)}) async-start(f32[64,1,1152]{2,1,0:T(1,128)} %bitcast.4), calls=%async_computation | async-start | bytes 589824 | tf_op jit(solution)/shard_map/all_to_all | solution.py:798
  41.8 13.2 %copy-start = (bf16[512,128]{1,0:T(8,128)(2,1)S(1)}, bf16[512,128]{1,0:T(8,128)(2,1)}, u32[]{:S(2)}) copy-start(bf16[512,128]{1,0:T(8,128)(2,1)} %constant.22.clone.table) | copy-start | bytes 393220
  41.8 4.5 %collective-permute-start.7 = (bf16[192,128]{1,0:T(8,128)(2,1)S(1)}, bf16[192,128]{1,0:T(8,128)(2,1)S(1)}, u32[]{:S(2)}, u32[]{:S(2)}) collective-permute-start(bf16[192,128]{1,0:T(8,128)(2,1)S(1)} %get-tuple-element.132), channel_id=1, source_target_pairs={{0,127},{1,2},{2,1},{3,4},{4,3},{5,6},{6,5},{7,8},{8,7},{9,10},{10... | collective-permute-start | bytes 147464 | tf_op jit(solution)/shard_map/ppermute | solution.py:679
  52.1 2.9 %collective-permute-start.9 = (f32[576,128]{1,0:T(8,128)S(1)}, f32[576,128]{1,0:T(8,128)S(1)}, u32[]{:S(2)}, u32[]{:S(2)}) collective-permute-start(f32[576,128]{1,0:T(8,128)S(1)} %bitcast.6), channel_id=1, source_target_pairs={{0,1},{1,0},{2,3},{3,2},{4,5},{5,4},{6,7},{7,6},{8,9},{9,8},{10,11... | collective-permute-start | bytes 884744 | tf_op jit(solution)/shard_map/ppermute | solution.py:676
  53.9 1.7 %collective-permute-start.8 = (f32[96,128]{1,0:T(8,128)S(1)}, f32[96,128]{1,0:T(8,128)S(1)}, u32[]{:S(2)}, u32[]{:S(2)}) collective-permute-start(f32[96,128]{1,0:T(8,128)S(1)} %get-tuple-element.135), channel_id=1, source_target_pairs={{0,1},{1,0},{2,3},{3,2},{4,5},{5,4},{6,7},{7,6},{8,9},{9,8},{10,11... | collective-permute-start | bytes 147464 | tf_op jit(solution)/shard_map/ppermute | solution.py:676
  54.0 1.6 %copy-start.1 = (bf16[64,1024]{1,0:T(8,128)(2,1)S(1)}, bf16[64,1024]{1,0:T(8,128)(2,1)}, u32[]{:S(2)}) copy-start(bf16[64,1024]{1,0:T(8,128)(2,1)} %constant.23.clone.spread_a) | copy-start | bytes 393220
  54.0 1.6 %copy-start.3 = (bf16[64,128]{1,0:T(8,128)(2,1)S(1)}, bf16[64,128]{1,0:T(8,128)(2,1)}, u32[]{:S(2)}) copy-start(bf16[64,128]{1,0:T(8,128)(2,1)} %constant.24.clone.spread_b) | copy-start | bytes 49156

commit v5 on v4

--- a/solution.py
+++ b/solution.py
@@ -600,7 +600,7 @@
     row_ref[2] = even * (one_hot(device + 2) + one_hot(device + 127))
 
 
-def spectra_kernel(near, far, row, lane, table, out):
+def station_spectra(near, far, row, lane, table):
     slabs = [
         jnp.concatenate([half[pl.ds(t, 64, stride=ROWS), :] for half in (near, far)], 0)
         for t in range(ROWS)
@@ -628,40 +628,42 @@
     mixed = jnp.zeros((2 * SB, 128), FP)
     for group, (part, _) in enumerate(PART_PAIRS):
         mixed = jnp.where(at // 8 == group, parts[part], mixed)
-    out[...] = lax.dot_general(
+    return lax.dot_general(
         table[...], mixed.astype(jnp.bfloat16), (((1,), (1,)), ((), ())),
         preferred_element_type=jnp.float32,
     ).astype(jnp.bfloat16)
 
 
 def cross_kernel(
-    par, base, inner, outer, coef, spectra_in, spread_a, spread_b, end, out, held_end, held, sems
+    par, base, inner, outer, coef, near, far, row, lane, table, spread_a, spread_b,
+    end, out, held_end, held, sems,
 ):
     odd = par[0] == 1
     pull = coef[4] * jnp.where(odd, outer[...], inner[...])
     for k in range(4):
         value = base[k] - float(AB[k, 4]) * pull
         held_end[k] = value - jnp.where(odd, inner[...], outer[...]) if k == 0 else value
-    copies = [pltpu.make_async_copy(held_end, end, sems.at[8])]
+    copies = [pltpu.make_async_copy(held_end, end, sems.at[4])]
     copies[0].start()
-    spectra = spectra_in[...]
+    spectra = station_spectra(near, far, row, lane, table)
     second = jnp.dot(spectra, spread_b[...], preferred_element_type=jnp.float32) * (1.0 / NT)
     b_re = second[:F]
     b_im = second[F:]
+    size = F // 4
     for i in range(4):
+        rows = slice(size * i, size * (i + 1))
         first = jnp.dot(
-            spectra, spread_a[:, 256 * i : 256 * (i + 1)], preferred_element_type=jnp.float32
+            jnp.concatenate([spectra[rows], spectra[F + size * i : F + size * (i + 1)]], 0), spread_a[...],
+            preferred_element_type=jnp.float32,
         )
-        for half in range(2):
-            at = 2 * i + half
-            cols = slice(128 * at, 128 * (at + 1))
-            a_re = first[:F, 128 * half : 128 * (half + 1)]
-            a_im = first[F:, 128 * half : 128 * (half + 1)]
-            held[0, :, cols] = (a_re * b_re + a_im * b_im).astype(jnp.bfloat16)
-            held[1, :, cols] = (a_im * b_re - a_re * b_im).astype(jnp.bfloat16)
-            copy = pltpu.make_async_copy(held.at[:, :, cols], out.at[0, :, :, cols], sems.at[at])
-            copy.start()
-            copies.append(copy)
+        for at in range(0, SB * SB, 128):
+            a_re = first[:size, at : at + 128]
+            a_im = first[size:, at : at + 128]
+            held[0, rows, at : at + 128] = (a_re * b_re[rows] + a_im * b_im[rows]).astype(jnp.bfloat16)
+            held[1, rows, at : at + 128] = (a_im * b_re[rows] - a_re * b_im[rows]).astype(jnp.bfloat16)
+        copy = pltpu.make_async_copy(held.at[:, rows, :], out.at[0, :, rows, :], sems.at[i])
+        copy.start()
+        copies.append(copy)
     for copy in copies:
         copy.wait()
 
@@ -807,18 +809,13 @@
     )
     inner = swap_inner(msg)
     base = base_of(5, u5, u4)
-    (spectra,) = call(
-        spectra_kernel, [((2 * F, 2 * SB), jnp.bfloat16)],
-        (near, far, row, lane, table), "spectra",
-    )
-    inner, base, spectra = lax.optimization_barrier((inner, base, spectra))
     end, cross = call(
         cross_kernel, [(FOUR, FP), ((1, 2, F, SB * SB), jnp.bfloat16)],
-        (par, base, inner, outer, coef, spectra, reps, tiles), "cross", 1,
+        (par, base, inner, outer, coef, near, far, row, lane, table, reps, tiles), "cross", 1,
         out_specs=[HBM, HBM],
         scratch=(
             pltpu.VMEM(FOUR, FP), pltpu.VMEM((2, F, SB * SB), jnp.bfloat16),
-            pltpu.SemaphoreType.DMA((9,)),
+            pltpu.SemaphoreType.DMA((5,)),
         ),
     )
     return end, cross

time: 57.5 us -> 57.3 us (level)
    pallas_call x24 -> x23, Pallas kernels: 13.2 us -> 12.8 us  [call(): pl.pallas_call(kernel, out_shape=[jax.ShapeDtypeStruct(s, d) for s, d in...]
  transfers between devices with their start and end apart: 11 -> 11, of which waited for: 8 -> 8; matrix products, arithmetic and copies ran while one was open for 0% -> 0% of each run, Pallas kernels for 13% -> 12%
where the time goes in v5:
time: 57.3 us; the launch traced here: 57.1 us
  starting transfers between devices  30.1 us (53%)
  waiting for transfers between devices  13.2 us (23%)
  Pallas kernels  12.8 us (22%)
  between operations  0.85 us (1%)
    ppermute x7, starting transfers between devices, swap_inner(): return lax.ppermute(x, AXES, inner_route)  17.2 us
    pallas_call x23, Pallas kernels, call(): pl.pallas_call(kernel, out_shape=[jax.ShapeDtypeStruct(s, d) for s, d in...  12.8 us
    all_to_all x1, starting transfers between devices, body(): lax.all_to_all(mine.reshape(devices // 2, 1, ROWS * CAP), ('pair', 'chip'...  9.3 us
    all_to_all x1, waiting for transfers between devices, body(): lax.all_to_all(mine.reshape(devices // 2, 1, ROWS * CAP), ('pair', 'chip'...  5.82 us
    ppermute x3, waiting for transfers between devices, swap_outer(): return lax.ppermute(x, AXES, outer_route)  5.69 us
    ppermute x3, starting transfers between devices, swap_outer(): return lax.ppermute(x, AXES, outer_route)  3.6 us
    ppermute x7, waiting for transfers between devices, swap_inner(): return lax.ppermute(x, AXES, inner_route)  1.72 us
  transfers between devices with their start and end apart: 11, of which 8 were waited for; matrix products, arithmetic and copies ran while one was open for 0% of the time, Pallas kernels for 12%

profile of v5, /device:TPU:1, one launch (start us, length us, event | category | flops | bytes accessed | tf_op | source)
XLA Modules:
  0.0 57.1 jit_solution(1829172515070623234)
XLA Ops:
  0.6 1.4 %start.1 = (f32[4,96,128]{2,1,0:T(8,128)S(1)}, f32[4,96,128]{2,1,0:T(8,128)S(1)}, f32[4,96,128]{2,1,0:T(8,128)S(1)}, f32[24,32]{1,0:T(8,128)S(1)}, bf16[288,72]{...) custom-call(s32[1]{0:T(128)} %bitcast.par, ...), custom_call_target="tpu_custom_call" | custom-call | flops 4000000 | bytes 1000000 | tf_op jit(solution)/shard_map/start/pallas_call | solution.py:121
  2.1 1.5 %collective-permute-start = (f32[152,128]{1,0:T(8,128)S(1)}, f32[152,128]{1,0:T(8,128)S(1)}, u32[]{:S(2)}, u32[]{:S(2)}) collective-permute-start(f32[152,128]{1,0:T(8,128)S(1)} %get-tuple-element.81), channel_id=1, source_target_pairs={{0,1},{1,0},{2,3},{3,2},{4,5},{5,4},{6,7},{7,6},{8,9},{9,8},{10,11... | collective-permute-start | bytes 233480 | tf_op jit(solution)/shard_map/ppermute | solution.py:678
  3.6 0.7 %base0.1 = (f32[4,96,128]{2,1,0:T(8,128)S(1)}, f32[5,96,128]{2,1,0:T(8,128)S(1)}, f32[96,128]{1,0:T(8,128)S(1)}) custom-call(f32[1,6]{1,0:T(1,128)S(1)} %get-tuple-element.70.wave, f32[4,96,128]{2,1,0:T(8,128)S(1)} %get-tuple-element.71.now.prev.u0, f32[4,96,128]{2,1,0:T(8,128)S(1)} %get-tuple-element.72.vel, f32[4,96,128]{2,1,0:T(8,128)S(1)} %get-tuple-element.73.src, ...), custom_call_target="tpu_custom_call" | custom-call | flops 4000000 | bytes 1000000 | tf_op jit(solution)/shard_map/base0/pallas_call | solution.py:121
  4.5 0.5 inner0.1
  5.0 1.7 %collective-permute-start.1 = (bf16[432,128]{1,0:T(8,128)(2,1)S(1)}, bf16[432,128]{1,0:T(8,128)(2,1)S(1)}, u32[]{:S(2)}, u32[]{:S(2)}) collective-permute-start(bf16[432,128]{1,0:T(8,128)(2,1)S(1)} %get-tuple-element.86), channel_id=1, source_target_pairs={{0,127},{1,2},{2,1},{3,4},{4,3},{5,6},{6,5},{7,8},{8,7},{9,10},{10... | collective-permute-start | bytes 331784 | tf_op jit(solution)/shard_map/ppermute | solution.py:681
  7.2 1.3 %stations.1 = (f32[3,64,128]{2,1,0:T(8,128)S(1)}, f32[64,128]{1,0:T(8,128)S(1)}) custom-call(s32[1]{0:T(128)} %bitcast.par, s32[1,2]{1,0:T(1,128)S(1)} %copy-done.4, s32[128,128]{1,0:T(8,128)S(1)} %bitcast.8), custom_call_target="tpu_custom_call" | custom-call | flops 4000000 | bytes 1000000 | tf_op jit(solution)/shard_map/stations/pallas_call | solution.py:121
  8.5 0.7 %collective-permute-done.1.recv.outer = bf16[432,128]{1,0:T(8,128)(2,1)S(1)} collective-permute-done((bf16[432,128]{1,0:T(8,128)(2,1)S(1)}, bf16[432,128]{1,0:T(8,128)(2,1)S(1)}, u32[]{:S(2)}, u32[]{:S(2)}) %collective-permute-start.1) | collective-permute-done | bytes 110624 | tf_op jit(solution)/shard_map/ppermute | solution.py:681
  9.3 0.5 outer0.1
  9.8 7.2 %collective-permute-start.2 = (f32[96,128]{1,0:T(8,128)S(1)}, f32[96,128]{1,0:T(8,128)S(1)}, u32[]{:S(2)}, u32[]{:S(2)}) collective-permute-start(f32[96,128]{1,0:T(8,128)S(1)} %get-tuple-element.95), channel_id=1, source_target_pairs={{0,1},{1,0},{2,3},{3,2},{4,5},{5,4},{6,7},{7,6},{8,9},{9,8},{10,11... | collective-permute-start | bytes 147464 | tf_op jit(solution)/shard_map/ppermute | solution.py:678
  17.0 0.5 base.5
  18.4 0.5 base.6
  19.8 0.7 %sample3.1.first = f32[3,128]{1,0:T(4,128)S(1)} custom-call(f32[4,96,128]{2,1,0:T(8,128)S(1)} %get-tuple-element.71.now.prev.u0, f32[96,128]{1,0:T(8,128)S(1)} %get-tuple-element.102.l0, f32[4,96,128]{2,1,0:T(8,128)S(1)} %get-tuple-element.93.now.prev.u1, f32[96,128]{1,0:T(8,128)S(1)} %get-tuple-element.103.l1, ...), custom_call_target="tpu_custom_call" | custom-call | flops 4000000 | bytes 1000000 | tf_op jit(solution)/shard_map/sample3/pallas_call | solution.py:121
  20.6 2.4 %collective-permute-done.4.recv = bf16[192,128]{1,0:T(8,128)(2,1)S(1)} collective-permute-done((bf16[192,128]{1,0:T(8,128)(2,1)S(1)}, bf16[192,128]{1,0:T(8,128)(2,1)S(1)}, u32[]{:S(2)}, u32[]{:S(2)}) %collective-permute-start.4) | collective-permute-done | bytes 49184 | tf_op jit(solution)/shard_map/ppermute | solution.py:681
  23.0 5.9 %collective-permute-start.5 = (f32[96,128]{1,0:T(8,128)S(1)}, f32[96,128]{1,0:T(8,128)S(1)}, u32[]{:S(2)}, u32[]{:S(2)}) collective-permute-start(f32[96,128]{1,0:T(8,128)S(1)} %get-tuple-element.111), channel_id=1, source_target_pairs={{0,1},{1,0},{2,3},{3,2},{4,5},{5,4},{6,7},{7,6},{8,9},{9,8},{10,11... | collective-permute-start | bytes 147464 | tf_op jit(solution)/shard_map/ppermute | solution.py:678
  28.8 0.5 base.7
  30.6 0.5 sample8.1.before
  31.2 1.3 %sample7.1 = f32[576,128]{1,0:T(8,128)} custom-call(s32[1]{0:T(128)} %bitcast.par, f32[8,128]{1,0:T(8,128)S(1)} %sample8.1.before, f32[96,128]{1,0:T(8,128)S(1)} %collective-permute-done.6.recv.inner, f32[4,96,128]{2,1,0:T(8,128)S(1)} %get-tuple-element.128.tent, f32[96,128]{1,0:T(8,128)S(1)} %get-tuple-element.122.g.g_now, ...), custom_call_target="tpu_custom_call" | custom-call | flops 4000000 | bytes 1000000 | tf_op jit(solution)/shard_map/sample7/pallas_call | solution.py:121
  32.5 9.3 %all-to-all-start = ((f32[64,1,1152]{2,1,0:T(1,128)}), f32[64,1,1152]{2,1,0:T(1,128)S(1)}, u32[]{:S(2)}, u32[]{:S(2)}) async-start(f32[64,1,1152]{2,1,0:T(1,128)} %bitcast.4), calls=%async_computation | async-start | bytes 589824 | tf_op jit(solution)/shard_map/all_to_all | solution.py:800
  41.9 1.8 %collective-permute-start.7 = (bf16[192,128]{1,0:T(8,128)(2,1)S(1)}, bf16[192,128]{1,0:T(8,128)(2,1)S(1)}, u32[]{:S(2)}, u32[]{:S(2)}) collective-permute-start(bf16[192,128]{1,0:T(8,128)(2,1)S(1)} %get-tuple-element.129), channel_id=1, source_target_pairs={{0,127},{1,2},{2,1},{3,4},{4,3},{5,6},{6,5},{7,8},{8,7},{9,10},{10... | collective-permute-start | bytes 147464 | tf_op jit(solution)/shard_map/ppermute | solution.py:681
  43.7 2.6 %collective-permute-done.7.recv = bf16[192,128]{1,0:T(8,128)(2,1)S(1)} collective-permute-done((bf16[192,128]{1,0:T(8,128)(2,1)S(1)}, bf16[192,128]{1,0:T(8,128)(2,1)S(1)}, u32[]{:S(2)}, u32[]{:S(2)}) %collective-permute-start.7) | collective-permute-done | bytes 49184 | tf_op jit(solution)/shard_map/ppermute | solution.py:681
  46.3 5.8 %all-to-all-done = f32[64,1,1152]{2,1,0:T(1,128)S(1)} async-done(((f32[64,1,1152]{2,1,0:T(1,128)}), f32[64,1,1152]{2,1,0:T(1,128)S(1)}, u32[]{:S(2)}, u32[]{:S(2)}) %all-to-all-start) | async-done | bytes 294944 | tf_op jit(solution)/shard_map/all_to_all | solution.py:800
  52.1 1.7 %collective-permute-start.9 = (f32[576,128]{1,0:T(8,128)S(1)}, f32[576,128]{1,0:T(8,128)S(1)}, u32[]{:S(2)}, u32[]{:S(2)}) collective-permute-start(f32[576,128]{1,0:T(8,128)S(1)} %bitcast.6), channel_id=1, source_target_pairs={{0,1},{1,0},{2,3},{3,2},{4,5},{5,4},{6,7},{7,6},{8,9},{9,8},{10,11... | collective-permute-start | bytes 884744 | tf_op jit(solution)/shard_map/ppermute | solution.py:678
  54.4 0.7 %collective-permute-done.8.inner = f32[96,128]{1,0:T(8,128)S(1)} collective-permute-done((f32[96,128]{1,0:T(8,128)S(1)}, f32[96,128]{1,0:T(8,128)S(1)}, u32[]{:S(2)}, u32[]{:S(2)}) %collective-permute-start.8) | collective-permute-done | bytes 49184 | tf_op jit(solution)/shard_map/ppermute | solution.py:678
  55.2 1.9 %cross.1 = (f32[4,96,128]{2,1,0:T(8,128)}, bf16[1,2,256,1024]{3,2,1,0:T(8,128)(2,1)}) custom-call(s32[1]{0:T(128)} %bitcast.par, f32[4,96,128]{2,1,0:T(8,128)S(1)} %base.9, f32[96,128]{1,0:T(8,128)S(1)} %collective-permute-done.8.inner, f32[96,128]{1,0:T(8,128)S(1)} %get-tuple-element.134.outer, f32[5,96,128]{2,1,0:T(8,128)S(1)} %get-tuple-element.84.coef, ...), custom_call_target="tpu_custom_call" | custom-call | flops 4000000 | bytes 1000000 | tf_op jit(solution)/shard_map/cross/pallas_call | solution.py:121
  (31 shorter events, 4.5 us)
Async XLA Ops:
  2.1 5.1 %copy-start.2 = (s32[16384]{0:T(1024)S(1)}, s32[16384]{0:T(1024)}, u32[]{:S(2)}) copy-start(s32[16384]{0:T(1024)} %param.22) | copy-start | bytes 196612
  2.1 5.1 %copy-start.4 = (s32[1,2]{1,0:T(1,128)S(1)}, s32[1,2]{1,0:T(1,128)}, u32[]{:S(2)}) copy-start(s32[1,2]{1,0:T(1,128)} %blocks.1) | copy-start | bytes 28
  2.1 2.4 %collective-permute-start = (f32[152,128]{1,0:T(8,128)S(1)}, f32[152,128]{1,0:T(8,128)S(1)}, u32[]{:S(2)}, u32[]{:S(2)}) collective-permute-start(f32[152,128]{1,0:T(8,128)S(1)} %get-tuple-element.81), channel_id=1, source_target_pairs={{0,1},{1,0},{2,3},{3,2},{4,5},{5,4},{6,7},{7,6},{8,9},{9,8},{10,11... | collective-permute-start | bytes 233480 | tf_op jit(solution)/shard_map/ppermute | solution.py:678
  5.0 4.3 %collective-permute-start.1 = (bf16[432,128]{1,0:T(8,128)(2,1)S(1)}, bf16[432,128]{1,0:T(8,128)(2,1)S(1)}, u32[]{:S(2)}, u32[]{:S(2)}) collective-permute-start(bf16[432,128]{1,0:T(8,128)(2,1)S(1)} %get-tuple-element.86), channel_id=1, source_target_pairs={{0,127},{1,2},{2,1},{3,4},{4,3},{5,6},{6,5},{7,8},{8,7},{9,10},{10... | collective-permute-start | bytes 331784 | tf_op jit(solution)/shard_map/ppermute | solution.py:681
  9.8 8.1 %collective-permute-start.2 = (f32[96,128]{1,0:T(8,128)S(1)}, f32[96,128]{1,0:T(8,128)S(1)}, u32[]{:S(2)}, u32[]{:S(2)}) collective-permute-start(f32[96,128]{1,0:T(8,128)S(1)} %get-tuple-element.95), channel_id=1, source_target_pairs={{0,1},{1,0},{2,3},{3,2},{4,5},{5,4},{6,7},{7,6},{8,9},{9,8},{10,11... | collective-permute-start | bytes 147464 | tf_op jit(solution)/shard_map/ppermute | solution.py:678
  17.9 1.3 %collective-permute-start.3 = (f32[96,128]{1,0:T(8,128)S(1)}, f32[96,128]{1,0:T(8,128)S(1)}, u32[]{:S(2)}, u32[]{:S(2)}) collective-permute-start(f32[96,128]{1,0:T(8,128)S(1)} %get-tuple-element.99), channel_id=1, source_target_pairs={{0,1},{1,0},{2,3},{3,2},{4,5},{5,4},{6,7},{7,6},{8,9},{9,8},{10,11... | collective-permute-start | bytes 147464 | tf_op jit(solution)/shard_map/ppermute | solution.py:678
  19.3 3.6 %collective-permute-start.4 = (bf16[192,128]{1,0:T(8,128)(2,1)S(1)}, bf16[192,128]{1,0:T(8,128)(2,1)S(1)}, u32[]{:S(2)}, u32[]{:S(2)}) collective-permute-start(bf16[192,128]{1,0:T(8,128)(2,1)S(1)} %get-tuple-element.101), channel_id=1, source_target_pairs={{0,127},{1,2},{2,1},{3,4},{4,3},{5,6},{6,5},{7,8},{8,7},{9,10},{10... | collective-permute-start | bytes 147464 | tf_op jit(solution)/shard_map/ppermute | solution.py:681
  23.0 6.7 %collective-permute-start.5 = (f32[96,128]{1,0:T(8,128)S(1)}, f32[96,128]{1,0:T(8,128)S(1)}, u32[]{:S(2)}, u32[]{:S(2)}) collective-permute-start(f32[96,128]{1,0:T(8,128)S(1)} %get-tuple-element.111), channel_id=1, source_target_pairs={{0,1},{1,0},{2,3},{3,2},{4,5},{5,4},{6,7},{7,6},{8,9},{9,8},{10,11... | collective-permute-start | bytes 147464 | tf_op jit(solution)/shard_map/ppermute | solution.py:678
  29.8 1.4 %collective-permute-start.6 = (f32[96,128]{1,0:T(8,128)S(1)}, f32[96,128]{1,0:T(8,128)S(1)}, u32[]{:S(2)}, u32[]{:S(2)}) collective-permute-start(f32[96,128]{1,0:T(8,128)S(1)} %get-tuple-element.118), channel_id=1, source_target_pairs={{0,1},{1,0},{2,3},{3,2},{4,5},{5,4},{6,7},{7,6},{8,9},{9,8},{10,11... | collective-permute-start | bytes 147464 | tf_op jit(solution)/shard_map/ppermute | solution.py:678
  32.5 19.6 %all-to-all-start = ((f32[64,1,1152]{2,1,0:T(1,128)}), f32[64,1,1152]{2,1,0:T(1,128)S(1)}, u32[]{:S(2)}, u32[]{:S(2)}) async-start(f32[64,1,1152]{2,1,0:T(1,128)} %bitcast.4), calls=%async_computation | async-start | bytes 589824 | tf_op jit(solution)/shard_map/all_to_all | solution.py:800
  41.8 13.4 %copy-start = (bf16[64,1024]{1,0:T(8,128)(2,1)S(1)}, bf16[64,1024]{1,0:T(8,128)(2,1)}, u32[]{:S(2)}) copy-start(bf16[64,1024]{1,0:T(8,128)(2,1)} %constant.23.clone.spread_a) | copy-start | bytes 393220
  41.8 13.3 %copy-start.1 = (bf16[512,128]{1,0:T(8,128)(2,1)S(1)}, bf16[512,128]{1,0:T(8,128)(2,1)}, u32[]{:S(2)}) copy-start(bf16[512,128]{1,0:T(8,128)(2,1)} %constant.22.clone.table) | copy-start | bytes 393220
  41.9 13.3 %copy-start.3 = (bf16[64,128]{1,0:T(8,128)(2,1)S(1)}, bf16[64,128]{1,0:T(8,128)(2,1)}, u32[]{:S(2)}) copy-start(bf16[64,128]{1,0:T(8,128)(2,1)} %constant.24.clone.spread_b) | copy-start | bytes 49156
  41.9 4.4 %collective-permute-start.7 = (bf16[192,128]{1,0:T(8,128)(2,1)S(1)}, bf16[192,128]{1,0:T(8,128)(2,1)S(1)}, u32[]{:S(2)}, u32[]{:S(2)}) collective-permute-start(bf16[192,128]{1,0:T(8,128)(2,1)S(1)} %get-tuple-element.129), channel_id=1, source_target_pairs={{0,127},{1,2},{2,1},{3,4},{4,3},{5,6},{6,5},{7,8},{8,7},{9,10},{10... | collective-permute-start | bytes 147464 | tf_op jit(solution)/shard_map/ppermute | solution.py:681
  52.1 3.1 %collective-permute-start.9 = (f32[576,128]{1,0:T(8,128)S(1)}, f32[576,128]{1,0:T(8,128)S(1)}, u32[]{:S(2)}, u32[]{:S(2)}) collective-permute-start(f32[576,128]{1,0:T(8,128)S(1)} %bitcast.6), channel_id=1, source_target_pairs={{0,1},{1,0},{2,3},{3,2},{4,5},{5,4},{6,7},{7,6},{8,9},{9,8},{10,11... | collective-permute-start | bytes 884744 | tf_op jit(solution)/shard_map/ppermute | solution.py:678
  53.9 1.3 %collective-permute-start.8 = (f32[96,128]{1,0:T(8,128)S(1)}, f32[96,128]{1,0:T(8,128)S(1)}, u32[]{:S(2)}, u32[]{:S(2)}) collective-permute-start(f32[96,128]{1,0:T(8,128)S(1)} %get-tuple-element.133), channel_id=1, source_target_pairs={{0,1},{1,0},{2,3},{3,2},{4,5},{5,4},{6,7},{7,6},{8,9},{9,8},{10,11... | collective-permute-start | bytes 147464 | tf_op jit(solution)/shard_map/ppermute | solution.py:678

commit v6 on v5

--- a/solution.py
+++ b/solution.py
@@ -208,12 +208,12 @@
 
 
 def start_kernel(
-    par, now_in, vel_in, src_in, speed_in, left_in, right_in, over_in, mat_in, elem_in, weight_in, wave_in,
-    now, vel, src, speed, left, right, over, mat, elem, weight, wave, msg_ref, sems,
+    par, now_in, speed_in, left_in, right_in, over_in, mat_in, elem_in, weight_in, wave_in,
+    now, speed, left, right, over, mat, elem, weight, wave, msg_ref, sems,
 ):
     pairs = (
-        (now_in, now), (speed_in.at[0], speed), (elem_in, elem), (weight_in, weight), (vel_in, vel),
-        (src_in, src), (left_in, left), (right_in, right), (over_in, over), (mat_in, mat), (wave_in, wave),
+        (now_in, now), (speed_in.at[0], speed), (elem_in, elem), (weight_in, weight), (left_in, left),
+        (right_in, right), (over_in, over), (mat_in, mat), (wave_in, wave),
     )
     copies = [pltpu.make_async_copy(a, b, sems.at[i]) for i, (a, b) in enumerate(pairs)]
     for copy in copies:
@@ -231,16 +231,27 @@
 
 
 def base_first_kernel(
-    wave, now, vel, src, speed, left, right, over, mat_z, out, coef_ref, first_ref, pad
+    wave, now, vel_in, src_in, speed, left, right, over, mat_z,
+    out, src, coef_ref, first_ref, vel, pad, sems,
 ):
+    copies = [
+        pltpu.make_async_copy(vel_in, vel, sems.at[0]), pltpu.make_async_copy(src_in, src, sems.at[1])
+    ]
+    for copy in copies:
+        copy.start()
     coefs = expand_speed(speed_parts(speed[...]), left[...], right[...], over[...])
     for i in range(5):
         coef_ref[i] = coefs[i]
     first_ref[...] = to_right(coefs[4], [now[k] for k in range(4)])
-    base_body(0, wave, now, None, vel, src, coef_ref, None, mat_z, out, pad)
-
-
-def base_body(step, wave, now, prev, vel, src, coef, coef0, mat_z, out, pad):
+    base_body(0, wave, now, None, None, coef_ref, None, mat_z, out, pad)
+    for copy in copies:
+        copy.wait()
+    scale = jnp.broadcast_to(wave[:, 0:1] * (STEP_DT * STEP_DT), PLANE)
+    for k in range(4):
+        out[k] = out[k] + STEP_DT * vel[k] + scale * src[k]
+
+
+def base_body(step, wave, now, prev, src, coef, coef0, mat_z, out, pad):
     scale = jnp.broadcast_to(wave[:, step : step + 1] * (STEP_DT * STEP_DT), (8, NZ))
     by_z = along_z(now[...].reshape(4 * NY, NZ), mat_z)
     patterns = y_patterns()
@@ -263,15 +274,15 @@
             mix = float(AB[k, 0]) * u[0]
             for m in range(1, 4):
                 mix = mix + float(AB[k, m]) * u[m]
-            force = scale * src[k, at, :] - (force + sx * mix)
+            force = force + sx * mix
             if prev is None:
-                out[k, at, :] = u[k] + STEP_DT * vel[k, at, :] + force
+                out[k, at, :] = u[k] - force
             else:
-                out[k, at, :] = 2.0 * u[k] - prev[k, at, :] + force
+                out[k, at, :] = 2.0 * u[k] - prev[k, at, :] + (scale * src[k, at, :] - force)
 
 
 def base_kernel(step, wave, now, prev, src, coef, coef0, mat_z, out, pad):
-    base_body(step, wave, now, prev, None, src, coef, coef0, mat_z, out, pad)
+    base_body(step, wave, now, prev, src, coef, coef0, mat_z, out, pad)
 
 
 def half_left(plane, coefs, mat_z, pad):
@@ -406,11 +417,13 @@
     last_ref[...] = last
 
 
-def outer_last_kernel(par, tent, now, g_now, recv, inner, coef, sxl, u_ref, msg_ref, outer_ref):
+def outer_last_kernel(par, tent, now, g_now, recv, near, coef, sxl, u_ref, both_ref, outer_ref):
+    gathered = near.shape[0]
+    both_ref[:gathered] = near[...]
     outer_finish(
         par[0] == 1, tent, coef[4], sxl[...], recv[:NY].astype(FP), recv[NY:].astype(FP), g_now[...],
         now[0], None,
-        (u_ref, msg_ref, outer_ref),
+        (u_ref, both_ref.at[pl.ds(gathered, NY), :], outer_ref),
     )
 
 
@@ -635,14 +648,15 @@
 
 
 def cross_kernel(
-    par, base, inner, outer, coef, near, far, row, lane, table, spread_a, spread_b,
+    par, base, outer, coef, near, far, row, lane, table, spread_a, spread_b,
     end, out, held_end, held, sems,
 ):
     odd = par[0] == 1
-    pull = coef[4] * jnp.where(odd, outer[...], inner[...])
+    inner = far[near.shape[0] :]
+    pull = coef[4] * jnp.where(odd, outer[...], inner)
     for k in range(4):
         value = base[k] - float(AB[k, 4]) * pull
-        held_end[k] = value - jnp.where(odd, inner[...], outer[...]) if k == 0 else value
+        held_end[k] = value - jnp.where(odd, inner, outer[...]) if k == 0 else value
     copies = [pltpu.make_async_copy(held_end, end, sems.at[4])]
     copies[0].start()
     spectra = station_spectra(near, far, row, lane, table)
@@ -696,21 +710,23 @@
     par = lax.axis_index("core").astype(jnp.int32).reshape(1)
 
     inputs = (
-        now, vel, src, speed_sq, left, right, over, mat_z, slot_elem.reshape(1, CAP), slot_weight,
+        now, speed_sq, left, right, over, mat_z, slot_elem.reshape(1, CAP), slot_weight,
         wavelet.reshape(1, NT),
     )
     kept = [jax.ShapeDtypeStruct(x.shape, x.dtype) for x in inputs]
-    kept[3] = jax.ShapeDtypeStruct((EY, EZ), FP)
-    now, vel, src, speed, left, right, over, mat_z, elem, weight, wavelet, msg = call(
+    kept[1] = jax.ShapeDtypeStruct((EY, EZ), FP)
+    now, speed, left, right, over, mat_z, elem, weight, wavelet, msg = call(
         start_kernel,
         [(x.shape, x.dtype) for x in kept] + [((NY + EY + PACK, NZ), FP)],
         (par, *(in_hbm(x) for x in inputs)), "start",
         specs=[SMEM] + [HBM] * len(inputs), scratch=(pltpu.SemaphoreType.DMA((len(inputs),)),),
     )
     inner0 = swap_inner(msg)
-    base, coef, g0 = call(
-        base_first_kernel, [(FOUR, FP), (FIVE, FP), (PLANE, FP)],
-        (wavelet, now, vel, src, speed, left, right, over, mat_z), "base0", scratch=pads,
+    base, src, coef, g0 = call(
+        base_first_kernel, [(FOUR, FP), (FOUR, FP), (FIVE, FP), (PLANE, FP)],
+        (wavelet, now, in_hbm(vel), in_hbm(src), speed, left, right, over, mat_z), "base0",
+        specs=[VMEM, VMEM, HBM, HBM] + [VMEM] * 5,
+        scratch=(pltpu.VMEM(FOUR, FP), *pads, pltpu.SemaphoreType.DMA((2,))),
     )
     tent, msg, cleft = call(
         inner_first_kernel,
@@ -802,16 +818,16 @@
     ).reshape(devices // 2 * ROWS, CAP)
     recv = swap_outer(msg)
     recv, near = lax.optimization_barrier((recv, near))
-    far = swap_inner(near)
+    gathered = devices // 2 * ROWS
     u5, msg, outer = call(
-        outer_last_kernel, [(FOUR, FP), (PLANE, FP), (PLANE, FP)],
-        (par, tent, u4, g4, recv, inner4, coef, sxl), "outer", 1,
-    )
-    inner = swap_inner(msg)
+        outer_last_kernel, [(FOUR, FP), ((gathered + NY, NZ), FP), (PLANE, FP)],
+        (par, tent, u4, g4, recv, near, coef, sxl), "outer", 1,
+    )
+    far = swap_inner(msg)
     base = base_of(5, u5, u4)
     end, cross = call(
         cross_kernel, [(FOUR, FP), ((1, 2, F, SB * SB), jnp.bfloat16)],
-        (par, base, inner, outer, coef, near, far, row, lane, table, reps, tiles), "cross", 1,
+        (par, base, outer, coef, near, far, row, lane, table, reps, tiles), "cross", 1,
         out_specs=[HBM, HBM],
         scratch=(
             pltpu.VMEM(FOUR, FP), pltpu.VMEM((2, F, SB * SB), jnp.bfloat16),

time: 57.3 us -> 57.6 us (level)
    ppermute x7 -> x6, waiting for transfers between devices: 1.72 us -> 1.61 us  [swap_inner(): return lax.ppermute(x, AXES, inner_route)]
    ppermute x7 -> x6, starting transfers between devices: 17.2 us -> 17.2 us  [swap_inner(): return lax.ppermute(x, AXES, inner_route)]
  transfers between devices with their start and end apart: 11 -> 10, of which waited for: 8 -> 7; matrix products, arithmetic and copies ran while one was open for 0% -> 0% of each run, Pallas kernels for 12% -> 13%
where the time goes in v6:
time: 57.6 us; the launch traced here: 57.4 us
  starting transfers between devices  29.8 us (52%)
  waiting for transfers between devices  13.5 us (23%)
  Pallas kernels  13.2 us (23%)
  between operations  0.81 us (1%)
    ppermute x6, starting transfers between devices, swap_inner(): return lax.ppermute(x, AXES, inner_route)  17.2 us
    pallas_call x23, Pallas kernels, call(): pl.pallas_call(kernel, out_shape=[jax.ShapeDtypeStruct(s, d) for s, d in...  13.2 us
    all_to_all x1, starting transfers between devices, body(): lax.all_to_all(mine.reshape(devices // 2, 1, ROWS * CAP), ('pair', 'chip'...  9.3 us
    ppermute x3, waiting for transfers between devices, swap_outer(): return lax.ppermute(x, AXES, outer_route)  6.07 us
    all_to_all x1, waiting for transfers between devices, body(): lax.all_to_all(mine.reshape(devices // 2, 1, ROWS * CAP), ('pair', 'chip'...  5.82 us
    ppermute x3, starting transfers between devices, swap_outer(): return lax.ppermute(x, AXES, outer_route)  3.26 us
    ppermute x6, waiting for transfers between devices, swap_inner(): return lax.ppermute(x, AXES, inner_route)  1.61 us
  transfers between devices with their start and end apart: 10, of which 7 were waited for; matrix products, arithmetic and copies ran while one was open for 0% of the time, Pallas kernels for 13%

profile of v6, /device:TPU:1, one launch (start us, length us, event | category | flops | bytes accessed | tf_op | source)
XLA Modules:
  0.0 57.4 jit_solution(4392638247417661678)
XLA Ops:
  0.6 1.3 %start.1 = (f32[4,96,128]{2,1,0:T(8,128)S(1)}, f32[24,32]{1,0:T(8,128)S(1)}, bf16[288,72]{1,0:T(8,128)(2,1)S(1)}, bf16[96,384]{1,0:T(8,128)(2,1)S(1)}, f32[16,12...) custom-call(s32[1]{0:T(128)} %bitcast.par, ...), custom_call_target="tpu_custom_call" | custom-call | flops 4000000 | bytes 1000000 | tf_op jit(solution)/shard_map/start/pallas_call | solution.py:121
  1.9 1.5 %collective-permute-start = (f32[152,128]{1,0:T(8,128)S(1)}, f32[152,128]{1,0:T(8,128)S(1)}, u32[]{:S(2)}, u32[]{:S(2)}) collective-permute-start(f32[152,128]{1,0:T(8,128)S(1)} %get-tuple-element.78), channel_id=1, source_target_pairs={{0,1},{1,0},{2,3},{3,2},{4,5},{5,4},{6,7},{7,6},{8,9},{9,8},{10,11... | collective-permute-start | bytes 233480 | tf_op jit(solution)/shard_map/ppermute | solution.py:692
  3.4 1.3 %base0.1 = (f32[4,96,128]{2,1,0:T(8,128)S(1)}, f32[4,96,128]{2,1,0:T(8,128)S(1)}, f32[5,96,128]{2,1,0:T(8,128)S(1)}, f32[96,128]{1,0:T(8,128)S(1)}) custom-call(f32[1,6]{1,0:T(1,128)S(1)} %get-tuple-element.69.wave, f32[4,96,128]{2,1,0:T(8,128)S(1)} %get-tuple-element.70.now.prev.u0, f32[4,96,128]{2,1,0:T(8,128)} %vel_in.1, f32[4,96,128]{2,1,0:T(8,128)} %src_in.1, ...), custom_call_target="tpu_custom_call" | custom-call | flops 4000000 | bytes 1000000 | tf_op jit(solution)/shard_map/base0/pallas_call | solution.py:121
  4.7 0.5 inner0.1
  5.2 1.4 %collective-permute-start.1 = (bf16[432,128]{1,0:T(8,128)(2,1)S(1)}, bf16[432,128]{1,0:T(8,128)(2,1)S(1)}, u32[]{:S(2)}, u32[]{:S(2)}) collective-permute-start(bf16[432,128]{1,0:T(8,128)(2,1)S(1)} %get-tuple-element.83), channel_id=1, source_target_pairs={{0,127},{1,2},{2,1},{3,4},{4,3},{5,6},{6,5},{7,8},{8,7},{9,10},{10... | collective-permute-start | bytes 331784 | tf_op jit(solution)/shard_map/ppermute | solution.py:695
  7.1 1.3 %stations.1 = (f32[3,64,128]{2,1,0:T(8,128)S(1)}, f32[64,128]{1,0:T(8,128)S(1)}) custom-call(s32[1]{0:T(128)} %bitcast.par, s32[1,2]{1,0:T(1,128)S(1)} %copy-done.4, s32[128,128]{1,0:T(8,128)S(1)} %bitcast.8), custom_call_target="tpu_custom_call" | custom-call | flops 4000000 | bytes 1000000 | tf_op jit(solution)/shard_map/stations/pallas_call | solution.py:121
  8.4 1.1 %collective-permute-done.1.recv.outer = bf16[432,128]{1,0:T(8,128)(2,1)S(1)} collective-permute-done((bf16[432,128]{1,0:T(8,128)(2,1)S(1)}, bf16[432,128]{1,0:T(8,128)(2,1)S(1)}, u32[]{:S(2)}, u32[]{:S(2)}) %collective-permute-start.1) | collective-permute-done | bytes 110624 | tf_op jit(solution)/shard_map/ppermute | solution.py:695
  9.5 0.5 outer0.1
  10.0 7.2 %collective-permute-start.2 = (f32[96,128]{1,0:T(8,128)S(1)}, f32[96,128]{1,0:T(8,128)S(1)}, u32[]{:S(2)}, u32[]{:S(2)}) collective-permute-start(f32[96,128]{1,0:T(8,128)S(1)} %get-tuple-element.93), channel_id=1, source_target_pairs={{0,1},{1,0},{2,3},{3,2},{4,5},{5,4},{6,7},{7,6},{8,9},{9,8},{10,11... | collective-permute-start | bytes 147464 | tf_op jit(solution)/shard_map/ppermute | solution.py:692
  17.2 0.5 base.5
  18.6 0.5 base.6
  20.0 0.7 %sample3.1.first = f32[3,128]{1,0:T(4,128)S(1)} custom-call(f32[4,96,128]{2,1,0:T(8,128)S(1)} %get-tuple-element.70.now.prev.u0, f32[96,128]{1,0:T(8,128)S(1)} %get-tuple-element.100.l0, f32[4,96,128]{2,1,0:T(8,128)S(1)} %get-tuple-element.90.now.prev.u1, f32[96,128]{1,0:T(8,128)S(1)} %get-tuple-element.101.l1, ...), custom_call_target="tpu_custom_call" | custom-call | flops 4000000 | bytes 1000000 | tf_op jit(solution)/shard_map/sample3/pallas_call | solution.py:121
  20.8 2.4 %collective-permute-done.4.recv = bf16[192,128]{1,0:T(8,128)(2,1)S(1)} collective-permute-done((bf16[192,128]{1,0:T(8,128)(2,1)S(1)}, bf16[192,128]{1,0:T(8,128)(2,1)S(1)}, u32[]{:S(2)}, u32[]{:S(2)}) %collective-permute-start.4) | collective-permute-done | bytes 49184 | tf_op jit(solution)/shard_map/ppermute | solution.py:695
  23.2 5.9 %collective-permute-start.5 = (f32[96,128]{1,0:T(8,128)S(1)}, f32[96,128]{1,0:T(8,128)S(1)}, u32[]{:S(2)}, u32[]{:S(2)}) collective-permute-start(f32[96,128]{1,0:T(8,128)S(1)} %get-tuple-element.109), channel_id=1, source_target_pairs={{0,1},{1,0},{2,3},{3,2},{4,5},{5,4},{6,7},{7,6},{8,9},{9,8},{10,11... | collective-permute-start | bytes 147464 | tf_op jit(solution)/shard_map/ppermute | solution.py:692
  29.0 0.5 base.7
  30.8 0.5 sample8.1.before
  31.4 1.3 %sample7.1 = f32[576,128]{1,0:T(8,128)} custom-call(s32[1]{0:T(128)} %bitcast.par, f32[8,128]{1,0:T(8,128)S(1)} %sample8.1.before, f32[96,128]{1,0:T(8,128)S(1)} %collective-permute-done.6.recv.inner, f32[4,96,128]{2,1,0:T(8,128)S(1)} %get-tuple-element.126.tent, f32[96,128]{1,0:T(8,128)S(1)} %get-tuple-element.120.g.g_now, ...), custom_call_target="tpu_custom_call" | custom-call | flops 4000000 | bytes 1000000 | tf_op jit(solution)/shard_map/sample7/pallas_call | solution.py:121
  32.7 9.3 %all-to-all-start = ((f32[64,1,1152]{2,1,0:T(1,128)}), f32[64,1,1152]{2,1,0:T(1,128)S(1)}, u32[]{:S(2)}, u32[]{:S(2)}) async-start(f32[64,1,1152]{2,1,0:T(1,128)} %bitcast.4), calls=%async_computation | async-start | bytes 589824 | tf_op jit(solution)/shard_map/all_to_all | solution.py:816
  42.0 1.8 %collective-permute-start.7 = (bf16[192,128]{1,0:T(8,128)(2,1)S(1)}, bf16[192,128]{1,0:T(8,128)(2,1)S(1)}, u32[]{:S(2)}, u32[]{:S(2)}) collective-permute-start(bf16[192,128]{1,0:T(8,128)(2,1)S(1)} %get-tuple-element.127), channel_id=1, source_target_pairs={{0,127},{1,2},{2,1},{3,4},{4,3},{5,6},{6,5},{7,8},{8,7},{9,10},{10... | collective-permute-start | bytes 147464 | tf_op jit(solution)/shard_map/ppermute | solution.py:695
  43.9 2.6 %collective-permute-done.7.recv = bf16[192,128]{1,0:T(8,128)(2,1)S(1)} collective-permute-done((bf16[192,128]{1,0:T(8,128)(2,1)S(1)}, bf16[192,128]{1,0:T(8,128)(2,1)S(1)}, u32[]{:S(2)}, u32[]{:S(2)}) %collective-permute-start.7) | collective-permute-done | bytes 49184 | tf_op jit(solution)/shard_map/ppermute | solution.py:695
  46.5 5.8 %all-to-all-done = f32[64,1,1152]{2,1,0:T(1,128)S(1)} async-done(((f32[64,1,1152]{2,1,0:T(1,128)}), f32[64,1,1152]{2,1,0:T(1,128)S(1)}, u32[]{:S(2)}, u32[]{:S(2)}) %all-to-all-start) | async-done | bytes 294944 | tf_op jit(solution)/shard_map/all_to_all | solution.py:816
  52.4 1.8 %collective-permute-start.8 = (f32[672,128]{1,0:T(8,128)S(1)}, f32[672,128]{1,0:T(8,128)S(1)}, u32[]{:S(2)}, u32[]{:S(2)}) collective-permute-start(f32[672,128]{1,0:T(8,128)S(1)} %get-tuple-element.133), channel_id=1, source_target_pairs={{0,1},{1,0},{2,3},{3,2},{4,5},{5,4},{6,7},{7,6},{8,9},{9,8},{10,11... | collective-permute-start | bytes 1032200 | tf_op jit(solution)/shard_map/ppermute | solution.py:692
  54.7 0.8 %collective-permute-done.8.far = f32[672,128]{1,0:T(8,128)S(1)} collective-permute-done((f32[672,128]{1,0:T(8,128)S(1)}, f32[672,128]{1,0:T(8,128)S(1)}, u32[]{:S(2)}, u32[]{:S(2)}) %collective-permute-start.8) | collective-permute-done | bytes 344096 | tf_op jit(solution)/shard_map/ppermute | solution.py:692
  55.5 1.9 %cross.1 = (f32[4,96,128]{2,1,0:T(8,128)}, bf16[1,2,256,1024]{3,2,1,0:T(8,128)(2,1)}) custom-call(s32[1]{0:T(128)} %bitcast.par, f32[4,96,128]{2,1,0:T(8,128)S(1)} %base.9, f32[96,128]{1,0:T(8,128)S(1)} %get-tuple-element.132.outer, f32[5,96,128]{2,1,0:T(8,128)S(1)} %get-tuple-element.81.coef, f32[576,128]{1,0:T(8,128)S(1)} %bitcast.7, ...), custom_call_target="tpu_custom_call" | custom-call | flops 4000000 | bytes 1000000 | tf_op jit(solution)/shard_map/cross/pallas_call | solution.py:121
  (29 shorter events, 4.2 us)
Async XLA Ops:
  1.9 5.2 %copy-start.2 = (s32[16384]{0:T(1024)S(1)}, s32[16384]{0:T(1024)}, u32[]{:S(2)}) copy-start(s32[16384]{0:T(1024)} %param.22) | copy-start | bytes 196612
  1.9 5.2 %copy-start.4 = (s32[1,2]{1,0:T(1,128)S(1)}, s32[1,2]{1,0:T(1,128)}, u32[]{:S(2)}) copy-start(s32[1,2]{1,0:T(1,128)} %blocks.1) | copy-start | bytes 28
  1.9 2.8 %collective-permute-start = (f32[152,128]{1,0:T(8,128)S(1)}, f32[152,128]{1,0:T(8,128)S(1)}, u32[]{:S(2)}, u32[]{:S(2)}) collective-permute-start(f32[152,128]{1,0:T(8,128)S(1)} %get-tuple-element.78), channel_id=1, source_target_pairs={{0,1},{1,0},{2,3},{3,2},{4,5},{5,4},{6,7},{7,6},{8,9},{9,8},{10,11... | collective-permute-start | bytes 233480 | tf_op jit(solution)/shard_map/ppermute | solution.py:692
  5.2 4.3 %collective-permute-start.1 = (bf16[432,128]{1,0:T(8,128)(2,1)S(1)}, bf16[432,128]{1,0:T(8,128)(2,1)S(1)}, u32[]{:S(2)}, u32[]{:S(2)}) collective-permute-start(bf16[432,128]{1,0:T(8,128)(2,1)S(1)} %get-tuple-element.83), channel_id=1, source_target_pairs={{0,127},{1,2},{2,1},{3,4},{4,3},{5,6},{6,5},{7,8},{8,7},{9,10},{10... | collective-permute-start | bytes 331784 | tf_op jit(solution)/shard_map/ppermute | solution.py:695
  10.0 8.1 %collective-permute-start.2 = (f32[96,128]{1,0:T(8,128)S(1)}, f32[96,128]{1,0:T(8,128)S(1)}, u32[]{:S(2)}, u32[]{:S(2)}) collective-permute-start(f32[96,128]{1,0:T(8,128)S(1)} %get-tuple-element.93), channel_id=1, source_target_pairs={{0,1},{1,0},{2,3},{3,2},{4,5},{5,4},{6,7},{7,6},{8,9},{9,8},{10,11... | collective-permute-start | bytes 147464 | tf_op jit(solution)/shard_map/ppermute | solution.py:692
  18.2 1.3 %collective-permute-start.3 = (f32[96,128]{1,0:T(8,128)S(1)}, f32[96,128]{1,0:T(8,128)S(1)}, u32[]{:S(2)}, u32[]{:S(2)}) collective-permute-start(f32[96,128]{1,0:T(8,128)S(1)} %get-tuple-element.97), channel_id=1, source_target_pairs={{0,1},{1,0},{2,3},{3,2},{4,5},{5,4},{6,7},{7,6},{8,9},{9,8},{10,11... | collective-permute-start | bytes 147464 | tf_op jit(solution)/shard_map/ppermute | solution.py:692
  19.5 3.6 %collective-permute-start.4 = (bf16[192,128]{1,0:T(8,128)(2,1)S(1)}, bf16[192,128]{1,0:T(8,128)(2,1)S(1)}, u32[]{:S(2)}, u32[]{:S(2)}) collective-permute-start(bf16[192,128]{1,0:T(8,128)(2,1)S(1)} %get-tuple-element.99), channel_id=1, source_target_pairs={{0,127},{1,2},{2,1},{3,4},{4,3},{5,6},{6,5},{7,8},{8,7},{9,10},{10... | collective-permute-start | bytes 147464 | tf_op jit(solution)/shard_map/ppermute | solution.py:695
  23.2 6.7 %collective-permute-start.5 = (f32[96,128]{1,0:T(8,128)S(1)}, f32[96,128]{1,0:T(8,128)S(1)}, u32[]{:S(2)}, u32[]{:S(2)}) collective-permute-start(f32[96,128]{1,0:T(8,128)S(1)} %get-tuple-element.109), channel_id=1, source_target_pairs={{0,1},{1,0},{2,3},{3,2},{4,5},{5,4},{6,7},{7,6},{8,9},{9,8},{10,11... | collective-permute-start | bytes 147464 | tf_op jit(solution)/shard_map/ppermute | solution.py:692
  30.0 1.4 %collective-permute-start.6 = (f32[96,128]{1,0:T(8,128)S(1)}, f32[96,128]{1,0:T(8,128)S(1)}, u32[]{:S(2)}, u32[]{:S(2)}) collective-permute-start(f32[96,128]{1,0:T(8,128)S(1)} %get-tuple-element.116), channel_id=1, source_target_pairs={{0,1},{1,0},{2,3},{3,2},{4,5},{5,4},{6,7},{7,6},{8,9},{9,8},{10,11... | collective-permute-start | bytes 147464 | tf_op jit(solution)/shard_map/ppermute | solution.py:692
  32.7 19.6 %all-to-all-start = ((f32[64,1,1152]{2,1,0:T(1,128)}), f32[64,1,1152]{2,1,0:T(1,128)S(1)}, u32[]{:S(2)}, u32[]{:S(2)}) async-start(f32[64,1,1152]{2,1,0:T(1,128)} %bitcast.4), calls=%async_computation | async-start | bytes 589824 | tf_op jit(solution)/shard_map/all_to_all | solution.py:816
  42.0 4.5 %collective-permute-start.7 = (bf16[192,128]{1,0:T(8,128)(2,1)S(1)}, bf16[192,128]{1,0:T(8,128)(2,1)S(1)}, u32[]{:S(2)}, u32[]{:S(2)}) collective-permute-start(bf16[192,128]{1,0:T(8,128)(2,1)S(1)} %get-tuple-element.127), channel_id=1, source_target_pairs={{0,127},{1,2},{2,1},{3,4},{4,3},{5,6},{6,5},{7,8},{8,7},{9,10},{10... | collective-permute-start | bytes 147464 | tf_op jit(solution)/shard_map/ppermute | solution.py:695
  52.3 3.1 %copy-start = (bf16[64,1024]{1,0:T(8,128)(2,1)S(1)}, bf16[64,1024]{1,0:T(8,128)(2,1)}, u32[]{:S(2)}) copy-start(bf16[64,1024]{1,0:T(8,128)(2,1)} %constant.23.clone.spread_a) | copy-start | bytes 393220
  52.3 3.1 %copy-start.1 = (bf16[512,128]{1,0:T(8,128)(2,1)S(1)}, bf16[512,128]{1,0:T(8,128)(2,1)}, u32[]{:S(2)}) copy-start(bf16[512,128]{1,0:T(8,128)(2,1)} %constant.22.clone.table) | copy-start | bytes 393220
  52.3 3.1 %copy-start.3 = (bf16[64,128]{1,0:T(8,128)(2,1)S(1)}, bf16[64,128]{1,0:T(8,128)(2,1)}, u32[]{:S(2)}) copy-start(bf16[64,128]{1,0:T(8,128)(2,1)} %constant.24.clone.spread_b) | copy-start | bytes 49156
  52.4 3.1 %collective-permute-start.8 = (f32[672,128]{1,0:T(8,128)S(1)}, f32[672,128]{1,0:T(8,128)S(1)}, u32[]{:S(2)}, u32[]{:S(2)}) collective-permute-start(f32[672,128]{1,0:T(8,128)S(1)} %get-tuple-element.133), channel_id=1, source_target_pairs={{0,1},{1,0},{2,3},{3,2},{4,5},{5,4},{6,7},{7,6},{8,9},{9,8},{10,11... | collective-permute-start | bytes 1032200 | tf_op jit(solution)/shard_map/ppermute | solution.py:692

commit v7 on v6

--- a/solution.py
+++ b/solution.py
@@ -417,13 +417,11 @@
     last_ref[...] = last
 
 
-def outer_last_kernel(par, tent, now, g_now, recv, near, coef, sxl, u_ref, both_ref, outer_ref):
-    gathered = near.shape[0]
-    both_ref[:gathered] = near[...]
+def outer_last_kernel(par, tent, now, g_now, recv, inner, coef, sxl, u_ref, msg_ref, outer_ref):
     outer_finish(
         par[0] == 1, tent, coef[4], sxl[...], recv[:NY].astype(FP), recv[NY:].astype(FP), g_now[...],
         now[0], None,
-        (u_ref, both_ref.at[pl.ds(gathered, NY), :], outer_ref),
+        (u_ref, msg_ref, outer_ref),
     )
 
 
@@ -648,15 +646,14 @@
 
 
 def cross_kernel(
-    par, base, outer, coef, near, far, row, lane, table, spread_a, spread_b,
+    par, base, inner, outer, coef, near, far, row, lane, table, spread_a, spread_b,
     end, out, held_end, held, sems,
 ):
     odd = par[0] == 1
-    inner = far[near.shape[0] :]
-    pull = coef[4] * jnp.where(odd, outer[...], inner)
+    pull = coef[4] * jnp.where(odd, outer[...], inner[...])
     for k in range(4):
         value = base[k] - float(AB[k, 4]) * pull
-        held_end[k] = value - jnp.where(odd, inner, outer[...]) if k == 0 else value
+        held_end[k] = value - jnp.where(odd, inner[...], outer[...]) if k == 0 else value
     copies = [pltpu.make_async_copy(held_end, end, sems.at[4])]
     copies[0].start()
     spectra = station_spectra(near, far, row, lane, table)
@@ -818,16 +815,16 @@
     ).reshape(devices // 2 * ROWS, CAP)
     recv = swap_outer(msg)
     recv, near = lax.optimization_barrier((recv, near))
-    gathered = devices // 2 * ROWS
+    far = swap_inner(near)
     u5, msg, outer = call(
-        outer_last_kernel, [(FOUR, FP), ((gathered + NY, NZ), FP), (PLANE, FP)],
-        (par, tent, u4, g4, recv, near, coef, sxl), "outer", 1,
-    )
-    far = swap_inner(msg)
+        outer_last_kernel, [(FOUR, FP), (PLANE, FP), (PLANE, FP)],
+        (par, tent, u4, g4, recv, inner4, coef, sxl), "outer", 1,
+    )
+    inner = swap_inner(msg)
     base = base_of(5, u5, u4)
     end, cross = call(
         cross_kernel, [(FOUR, FP), ((1, 2, F, SB * SB), jnp.bfloat16)],
-        (par, base, outer, coef, near, far, row, lane, table, reps, tiles), "cross", 1,
+        (par, base, inner, outer, coef, near, far, row, lane, table, reps, tiles), "cross", 1,
         out_specs=[HBM, HBM],
         scratch=(
             pltpu.VMEM(FOUR, FP), pltpu.VMEM((2, F, SB * SB), jnp.bfloat16),

time: 57.6 us -> 57.5 us (level)
    ppermute x6 -> x7, waiting for transfers between devices: 1.61 us -> 1.55 us  [swap_inner(): return lax.ppermute(x, AXES, inner_route)]
    ppermute x6 -> x7, starting transfers between devices: 17.2 us -> 17.2 us  [swap_inner(): return lax.ppermute(x, AXES, inner_route)]
  transfers between devices with their start and end apart: 10 -> 11, of which waited for: 7 -> 7; matrix products, arithmetic and copies ran while one was open for 0% -> 0% of each run, Pallas kernels for 13% -> 13%
where the time goes in v7:
time: 57.5 us; the launch traced here: 57.3 us
  starting transfers between devices  29.8 us (52%)
  waiting for transfers between devices  13.4 us (23%)
  Pallas kernels  13.2 us (23%)
  between operations  0.85 us (1%)
    ppermute x7, starting transfers between devices, swap_inner(): return lax.ppermute(x, AXES, inner_route)  17.2 us
    pallas_call x23, Pallas kernels, call(): pl.pallas_call(kernel, out_shape=[jax.ShapeDtypeStruct(s, d) for s, d in...  13.2 us
    all_to_all x1, starting transfers between devices, body(): lax.all_to_all(mine.reshape(devices // 2, 1, ROWS * CAP), ('pair', 'chip'...  9.31 us
    ppermute x3, waiting for transfers between devices, swap_outer(): return lax.ppermute(x, AXES, outer_route)  6.04 us
    all_to_all x1, waiting for transfers between devices, body(): lax.all_to_all(mine.reshape(devices // 2, 1, ROWS * CAP), ('pair', 'chip'...  5.82 us
    ppermute x3, starting transfers between devices, swap_outer(): return lax.ppermute(x, AXES, outer_route)  3.25 us
    ppermute x7, waiting for transfers between devices, swap_inner(): return lax.ppermute(x, AXES, inner_route)  1.55 us
  transfers between devices with their start and end apart: 11, of which 7 were waited for; matrix products, arithmetic and copies ran while one was open for 0% of the time, Pallas kernels for 13%

profile of v7, /device:TPU:1, one launch (start us, length us, event | category | flops | bytes accessed | tf_op | source)
XLA Modules:
  0.0 57.3 jit_solution(9537696853639643915)
XLA Ops:
  0.6 1.3 %start.1 = (f32[4,96,128]{2,1,0:T(8,128)S(1)}, f32[24,32]{1,0:T(8,128)S(1)}, bf16[288,72]{1,0:T(8,128)(2,1)S(1)}, bf16[96,384]{1,0:T(8,128)(2,1)S(1)}, f32[16,12...) custom-call(s32[1]{0:T(128)} %bitcast.par, ...), custom_call_target="tpu_custom_call" | custom-call | flops 4000000 | bytes 1000000 | tf_op jit(solution)/shard_map/start/pallas_call | solution.py:121
  1.9 1.5 %collective-permute-start = (f32[152,128]{1,0:T(8,128)S(1)}, f32[152,128]{1,0:T(8,128)S(1)}, u32[]{:S(2)}, u32[]{:S(2)}) collective-permute-start(f32[152,128]{1,0:T(8,128)S(1)} %get-tuple-element.78), channel_id=1, source_target_pairs={{0,1},{1,0},{2,3},{3,2},{4,5},{5,4},{6,7},{7,6},{8,9},{9,8},{10,11... | collective-permute-start | bytes 233480 | tf_op jit(solution)/shard_map/ppermute | solution.py:689
  3.4 1.3 %base0.1 = (f32[4,96,128]{2,1,0:T(8,128)S(1)}, f32[4,96,128]{2,1,0:T(8,128)S(1)}, f32[5,96,128]{2,1,0:T(8,128)S(1)}, f32[96,128]{1,0:T(8,128)S(1)}) custom-call(f32[1,6]{1,0:T(1,128)S(1)} %get-tuple-element.69.wave, f32[4,96,128]{2,1,0:T(8,128)S(1)} %get-tuple-element.70.now.prev.u0, f32[4,96,128]{2,1,0:T(8,128)} %vel_in.1, f32[4,96,128]{2,1,0:T(8,128)} %src_in.1, ...), custom_call_target="tpu_custom_call" | custom-call | flops 4000000 | bytes 1000000 | tf_op jit(solution)/shard_map/base0/pallas_call | solution.py:121
  4.7 0.5 inner0.1
  5.2 1.4 %collective-permute-start.1 = (bf16[432,128]{1,0:T(8,128)(2,1)S(1)}, bf16[432,128]{1,0:T(8,128)(2,1)S(1)}, u32[]{:S(2)}, u32[]{:S(2)}) collective-permute-start(bf16[432,128]{1,0:T(8,128)(2,1)S(1)} %get-tuple-element.83), channel_id=1, source_target_pairs={{0,127},{1,2},{2,1},{3,4},{4,3},{5,6},{6,5},{7,8},{8,7},{9,10},{10... | collective-permute-start | bytes 331784 | tf_op jit(solution)/shard_map/ppermute | solution.py:692
  7.1 1.3 %stations.1 = (f32[3,64,128]{2,1,0:T(8,128)S(1)}, f32[64,128]{1,0:T(8,128)S(1)}) custom-call(s32[1]{0:T(128)} %bitcast.par, s32[1,2]{1,0:T(1,128)S(1)} %copy-done.4, s32[128,128]{1,0:T(8,128)S(1)} %bitcast.8), custom_call_target="tpu_custom_call" | custom-call | flops 4000000 | bytes 1000000 | tf_op jit(solution)/shard_map/stations/pallas_call | solution.py:121
  8.4 1.1 %collective-permute-done.1.recv.outer = bf16[432,128]{1,0:T(8,128)(2,1)S(1)} collective-permute-done((bf16[432,128]{1,0:T(8,128)(2,1)S(1)}, bf16[432,128]{1,0:T(8,128)(2,1)S(1)}, u32[]{:S(2)}, u32[]{:S(2)}) %collective-permute-start.1) | collective-permute-done | bytes 110624 | tf_op jit(solution)/shard_map/ppermute | solution.py:692
  9.5 0.5 outer0.1
  10.0 7.2 %collective-permute-start.2 = (f32[96,128]{1,0:T(8,128)S(1)}, f32[96,128]{1,0:T(8,128)S(1)}, u32[]{:S(2)}, u32[]{:S(2)}) collective-permute-start(f32[96,128]{1,0:T(8,128)S(1)} %get-tuple-element.93), channel_id=1, source_target_pairs={{0,1},{1,0},{2,3},{3,2},{4,5},{5,4},{6,7},{7,6},{8,9},{9,8},{10,11... | collective-permute-start | bytes 147464 | tf_op jit(solution)/shard_map/ppermute | solution.py:689
  17.2 0.5 base.5
  18.6 0.5 base.6
  20.0 0.7 %sample3.1.first = f32[3,128]{1,0:T(4,128)S(1)} custom-call(f32[4,96,128]{2,1,0:T(8,128)S(1)} %get-tuple-element.70.now.prev.u0, f32[96,128]{1,0:T(8,128)S(1)} %get-tuple-element.100.l0, f32[4,96,128]{2,1,0:T(8,128)S(1)} %get-tuple-element.90.now.prev.u1, f32[96,128]{1,0:T(8,128)S(1)} %get-tuple-element.101.l1, ...), custom_call_target="tpu_custom_call" | custom-call | flops 4000000 | bytes 1000000 | tf_op jit(solution)/shard_map/sample3/pallas_call | solution.py:121
  20.8 2.4 %collective-permute-done.4.recv = bf16[192,128]{1,0:T(8,128)(2,1)S(1)} collective-permute-done((bf16[192,128]{1,0:T(8,128)(2,1)S(1)}, bf16[192,128]{1,0:T(8,128)(2,1)S(1)}, u32[]{:S(2)}, u32[]{:S(2)}) %collective-permute-start.4) | collective-permute-done | bytes 49184 | tf_op jit(solution)/shard_map/ppermute | solution.py:692
  23.2 5.9 %collective-permute-start.5 = (f32[96,128]{1,0:T(8,128)S(1)}, f32[96,128]{1,0:T(8,128)S(1)}, u32[]{:S(2)}, u32[]{:S(2)}) collective-permute-start(f32[96,128]{1,0:T(8,128)S(1)} %get-tuple-element.109), channel_id=1, source_target_pairs={{0,1},{1,0},{2,3},{3,2},{4,5},{5,4},{6,7},{7,6},{8,9},{9,8},{10,11... | collective-permute-start | bytes 147464 | tf_op jit(solution)/shard_map/ppermute | solution.py:689
  29.0 0.5 base.7
  30.8 0.5 sample8.1.before
  31.4 1.3 %sample7.1 = f32[576,128]{1,0:T(8,128)} custom-call(s32[1]{0:T(128)} %bitcast.par, f32[8,128]{1,0:T(8,128)S(1)} %sample8.1.before, f32[96,128]{1,0:T(8,128)S(1)} %collective-permute-done.6.recv.inner, f32[4,96,128]{2,1,0:T(8,128)S(1)} %get-tuple-element.126.tent, f32[96,128]{1,0:T(8,128)S(1)} %get-tuple-element.120.g.g_now, ...), custom_call_target="tpu_custom_call" | custom-call | flops 4000000 | bytes 1000000 | tf_op jit(solution)/shard_map/sample7/pallas_call | solution.py:121
  32.7 9.3 %all-to-all-start = ((f32[64,1,1152]{2,1,0:T(1,128)}), f32[64,1,1152]{2,1,0:T(1,128)S(1)}, u32[]{:S(2)}, u32[]{:S(2)}) async-start(f32[64,1,1152]{2,1,0:T(1,128)} %bitcast.4), calls=%async_computation | async-start | bytes 589824 | tf_op jit(solution)/shard_map/all_to_all | solution.py:813
  42.1 1.8 %collective-permute-start.7 = (bf16[192,128]{1,0:T(8,128)(2,1)S(1)}, bf16[192,128]{1,0:T(8,128)(2,1)S(1)}, u32[]{:S(2)}, u32[]{:S(2)}) collective-permute-start(bf16[192,128]{1,0:T(8,128)(2,1)S(1)} %get-tuple-element.127), channel_id=1, source_target_pairs={{0,127},{1,2},{2,1},{3,4},{4,3},{5,6},{6,5},{7,8},{8,7},{9,10},{10... | collective-permute-start | bytes 147464 | tf_op jit(solution)/shard_map/ppermute | solution.py:692
  43.9 2.6 %collective-permute-done.7.recv = bf16[192,128]{1,0:T(8,128)(2,1)S(1)} collective-permute-done((bf16[192,128]{1,0:T(8,128)(2,1)S(1)}, bf16[192,128]{1,0:T(8,128)(2,1)S(1)}, u32[]{:S(2)}, u32[]{:S(2)}) %collective-permute-start.7) | collective-permute-done | bytes 49184 | tf_op jit(solution)/shard_map/ppermute | solution.py:692
  46.5 5.8 %all-to-all-done = f32[64,1,1152]{2,1,0:T(1,128)S(1)} async-done(((f32[64,1,1152]{2,1,0:T(1,128)}), f32[64,1,1152]{2,1,0:T(1,128)S(1)}, u32[]{:S(2)}, u32[]{:S(2)}) %all-to-all-start) | async-done | bytes 294944 | tf_op jit(solution)/shard_map/all_to_all | solution.py:813
  52.3 1.7 %collective-permute-start.9 = (f32[576,128]{1,0:T(8,128)S(1)}, f32[576,128]{1,0:T(8,128)S(1)}, u32[]{:S(2)}, u32[]{:S(2)}) collective-permute-start(f32[576,128]{1,0:T(8,128)S(1)} %bitcast.6), channel_id=1, source_target_pairs={{0,1},{1,0},{2,3},{3,2},{4,5},{5,4},{6,7},{7,6},{8,9},{9,8},{10,11... | collective-permute-start | bytes 884744 | tf_op jit(solution)/shard_map/ppermute | solution.py:689
  54.7 0.7 %collective-permute-done.8.inner = f32[96,128]{1,0:T(8,128)S(1)} collective-permute-done((f32[96,128]{1,0:T(8,128)S(1)}, f32[96,128]{1,0:T(8,128)S(1)}, u32[]{:S(2)}, u32[]{:S(2)}) %collective-permute-start.8) | collective-permute-done | bytes 49184 | tf_op jit(solution)/shard_map/ppermute | solution.py:689
  55.4 1.9 %cross.1 = (f32[4,96,128]{2,1,0:T(8,128)}, bf16[1,2,256,1024]{3,2,1,0:T(8,128)(2,1)}) custom-call(s32[1]{0:T(128)} %bitcast.par, f32[4,96,128]{2,1,0:T(8,128)S(1)} %base.9, f32[96,128]{1,0:T(8,128)S(1)} %collective-permute-done.8.inner, f32[96,128]{1,0:T(8,128)S(1)} %get-tuple-element.132.outer, f32[5,96,128]{2,1,0:T(8,128)S(1)} %get-tuple-element.81.coef, ...), custom_call_target="tpu_custom_call" | custom-call | flops 4000000 | bytes 1000000 | tf_op jit(solution)/shard_map/cross/pallas_call | solution.py:121
  (31 shorter events, 4.3 us)
Async XLA Ops:
  1.9 5.2 %copy-start.2 = (s32[16384]{0:T(1024)S(1)}, s32[16384]{0:T(1024)}, u32[]{:S(2)}) copy-start(s32[16384]{0:T(1024)} %param.22) | copy-start | bytes 196612
  1.9 5.2 %copy-start.4 = (s32[1,2]{1,0:T(1,128)S(1)}, s32[1,2]{1,0:T(1,128)}, u32[]{:S(2)}) copy-start(s32[1,2]{1,0:T(1,128)} %blocks.1) | copy-start | bytes 28
  1.9 2.8 %collective-permute-start = (f32[152,128]{1,0:T(8,128)S(1)}, f32[152,128]{1,0:T(8,128)S(1)}, u32[]{:S(2)}, u32[]{:S(2)}) collective-permute-start(f32[152,128]{1,0:T(8,128)S(1)} %get-tuple-element.78), channel_id=1, source_target_pairs={{0,1},{1,0},{2,3},{3,2},{4,5},{5,4},{6,7},{7,6},{8,9},{9,8},{10,11... | collective-permute-start | bytes 233480 | tf_op jit(solution)/shard_map/ppermute | solution.py:689
  5.2 4.3 %collective-permute-start.1 = (bf16[432,128]{1,0:T(8,128)(2,1)S(1)}, bf16[432,128]{1,0:T(8,128)(2,1)S(1)}, u32[]{:S(2)}, u32[]{:S(2)}) collective-permute-start(bf16[432,128]{1,0:T(8,128)(2,1)S(1)} %get-tuple-element.83), channel_id=1, source_target_pairs={{0,127},{1,2},{2,1},{3,4},{4,3},{5,6},{6,5},{7,8},{8,7},{9,10},{10... | collective-permute-start | bytes 331784 | tf_op jit(solution)/shard_map/ppermute | solution.py:692
  10.0 8.1 %collective-permute-start.2 = (f32[96,128]{1,0:T(8,128)S(1)}, f32[96,128]{1,0:T(8,128)S(1)}, u32[]{:S(2)}, u32[]{:S(2)}) collective-permute-start(f32[96,128]{1,0:T(8,128)S(1)} %get-tuple-element.93), channel_id=1, source_target_pairs={{0,1},{1,0},{2,3},{3,2},{4,5},{5,4},{6,7},{7,6},{8,9},{9,8},{10,11... | collective-permute-start | bytes 147464 | tf_op jit(solution)/shard_map/ppermute | solution.py:689
  18.2 1.3 %collective-permute-start.3 = (f32[96,128]{1,0:T(8,128)S(1)}, f32[96,128]{1,0:T(8,128)S(1)}, u32[]{:S(2)}, u32[]{:S(2)}) collective-permute-start(f32[96,128]{1,0:T(8,128)S(1)} %get-tuple-element.97), channel_id=1, source_target_pairs={{0,1},{1,0},{2,3},{3,2},{4,5},{5,4},{6,7},{7,6},{8,9},{9,8},{10,11... | collective-permute-start | bytes 147464 | tf_op jit(solution)/shard_map/ppermute | solution.py:689
  19.5 3.6 %collective-permute-start.4 = (bf16[192,128]{1,0:T(8,128)(2,1)S(1)}, bf16[192,128]{1,0:T(8,128)(2,1)S(1)}, u32[]{:S(2)}, u32[]{:S(2)}) collective-permute-start(bf16[192,128]{1,0:T(8,128)(2,1)S(1)} %get-tuple-element.99), channel_id=1, source_target_pairs={{0,127},{1,2},{2,1},{3,4},{4,3},{5,6},{6,5},{7,8},{8,7},{9,10},{10... | collective-permute-start | bytes 147464 | tf_op jit(solution)/shard_map/ppermute | solution.py:692
  23.2 6.7 %collective-permute-start.5 = (f32[96,128]{1,0:T(8,128)S(1)}, f32[96,128]{1,0:T(8,128)S(1)}, u32[]{:S(2)}, u32[]{:S(2)}) collective-permute-start(f32[96,128]{1,0:T(8,128)S(1)} %get-tuple-element.109), channel_id=1, source_target_pairs={{0,1},{1,0},{2,3},{3,2},{4,5},{5,4},{6,7},{7,6},{8,9},{9,8},{10,11... | collective-permute-start | bytes 147464 | tf_op jit(solution)/shard_map/ppermute | solution.py:689
  30.0 1.4 %collective-permute-start.6 = (f32[96,128]{1,0:T(8,128)S(1)}, f32[96,128]{1,0:T(8,128)S(1)}, u32[]{:S(2)}, u32[]{:S(2)}) collective-permute-start(f32[96,128]{1,0:T(8,128)S(1)} %get-tuple-element.116), channel_id=1, source_target_pairs={{0,1},{1,0},{2,3},{3,2},{4,5},{5,4},{6,7},{7,6},{8,9},{9,8},{10,11... | collective-permute-start | bytes 147464 | tf_op jit(solution)/shard_map/ppermute | solution.py:689
  32.7 19.6 %all-to-all-start = ((f32[64,1,1152]{2,1,0:T(1,128)}), f32[64,1,1152]{2,1,0:T(1,128)S(1)}, u32[]{:S(2)}, u32[]{:S(2)}) async-start(f32[64,1,1152]{2,1,0:T(1,128)} %bitcast.4), calls=%async_computation | async-start | bytes 589824 | tf_op jit(solution)/shard_map/all_to_all | solution.py:813
  42.0 13.4 %copy-start = (bf16[64,1024]{1,0:T(8,128)(2,1)S(1)}, bf16[64,1024]{1,0:T(8,128)(2,1)}, u32[]{:S(2)}) copy-start(bf16[64,1024]{1,0:T(8,128)(2,1)} %constant.23.clone.spread_a) | copy-start | bytes 393220
  42.1 13.3 %copy-start.1 = (bf16[512,128]{1,0:T(8,128)(2,1)S(1)}, bf16[512,128]{1,0:T(8,128)(2,1)}, u32[]{:S(2)}) copy-start(bf16[512,128]{1,0:T(8,128)(2,1)} %constant.22.clone.table) | copy-start | bytes 393220
  42.1 13.3 %copy-start.3 = (bf16[64,128]{1,0:T(8,128)(2,1)S(1)}, bf16[64,128]{1,0:T(8,128)(2,1)}, u32[]{:S(2)}) copy-start(bf16[64,128]{1,0:T(8,128)(2,1)} %constant.24.clone.spread_b) | copy-start | bytes 49156
  42.1 4.4 %collective-permute-start.7 = (bf16[192,128]{1,0:T(8,128)(2,1)S(1)}, bf16[192,128]{1,0:T(8,128)(2,1)S(1)}, u32[]{:S(2)}, u32[]{:S(2)}) collective-permute-start(bf16[192,128]{1,0:T(8,128)(2,1)S(1)} %get-tuple-element.127), channel_id=1, source_target_pairs={{0,127},{1,2},{2,1},{3,4},{4,3},{5,6},{6,5},{7,8},{8,7},{9,10},{10... | collective-permute-start | bytes 147464 | tf_op jit(solution)/shard_map/ppermute | solution.py:692
  52.3 3.1 %collective-permute-start.9 = (f32[576,128]{1,0:T(8,128)S(1)}, f32[576,128]{1,0:T(8,128)S(1)}, u32[]{:S(2)}, u32[]{:S(2)}) collective-permute-start(f32[576,128]{1,0:T(8,128)S(1)} %bitcast.6), channel_id=1, source_target_pairs={{0,1},{1,0},{2,3},{3,2},{4,5},{5,4},{6,7},{7,6},{8,9},{9,8},{10,11... | collective-permute-start | bytes 884744 | tf_op jit(solution)/shard_map/ppermute | solution.py:689
  54.1 1.3 %collective-permute-start.8 = (f32[96,128]{1,0:T(8,128)S(1)}, f32[96,128]{1,0:T(8,128)S(1)}, u32[]{:S(2)}, u32[]{:S(2)}) collective-permute-start(f32[96,128]{1,0:T(8,128)S(1)} %get-tuple-element.131), channel_id=1, source_target_pairs={{0,1},{1,0},{2,3},{3,2},{4,5},{5,4},{6,7},{7,6},{8,9},{9,8},{10,11... | collective-permute-start | bytes 147464 | tf_op jit(solution)/shard_map/ppermute | solution.py:689
